TPU v7x, 128 devices: a whole 4x4x4 slice. The times are simulated.
128 devices in a mesh: grp: 8 (over z, core), dev: 16 (over y, x).
Axes of the slice: x: 4, y: 4, z: 4, core: 2. Of those that a mesh axis runs over, the one named last changes fastest.
Arguments:
- a_blocks: bfloat16 [4096, 7, 192, 192], P(('grp', 'dev')), may hold values from -0.4375 to 0.4375
- prolong_t: bfloat16 [4096, 32, 192], P(('grp', 'dev')), may hold values from -1.796875 to 1.796875
- elem_slot: int32 [4096], P(('grp', 'dev')), may hold values from 0 to 5, as said below
- touch_agg: int32 [128, 6], replicated, may hold values from 0 to 527, as said below
- nbr: int32 [4096, 6], P(('grp', 'dev')), may hold values from -1 to 4095, as said below
- nbr_agg: int32 [4096, 6], P(('grp', 'dev')), may hold values from -1 to 527, as said below
- coarse_row: int32 [528], replicated, may hold values from 0 to 1407, as said below
Outputs:
- coarse: float32 [1408, 7, 1024], P('dev')
Inputs may be any that keep to these rules, and one draw needn't show every extreme that they name: Element e lies on device e // 32 (devices numbered grp-major). elem_slot[e] is the position of e's aggregate in touch_agg[e // 32]. `touch_agg`: each row lists 6 distinct aggregates, exactly those of the device's elements; all devices that touch one aggregate share their grp index. `nbr`: global element index across each face, or -1 on the domain's boundary; adjacency is symmetric; a neighbour lies on the same device, or on the device whose grp index differs by one (same dev index), or whose dev index differs by one (same grp index); exactly 8 elements of a device have a neighbour on each existing device next along grp, and exactly 8 on each existing device next along dev. `nbr_agg`: the aggregate of the element nbr[e, f], -1 exactly where nbr[e, f] is -1. Distinct values; aggregate a's row belongs to dev index coarse_row[a] // 88. Of the aggregates touched by one device at most 1 belong to one dev index, and of those touched by the devices of one grp index at most 11; one dev index reaches both bounds and holds 88 rows.
All inputs are finite; a program needn't handle non-finite values.
Results may differ from a plain program's by a relative error of at most 0.005.
Values may be sent and summed in bfloat16 or wider, within the bound.
No kernel may reach another device: no remote copies, remote signals or barrier semaphores. Data moves between devices by JAX's collectives and lax.ppermute only.
A program may use at most 128 MiB of HBM per device.

v0:
```python
import jax
import jax.numpy as jnp
from jax import lax
from jax.sharding import PartitionSpec as P

EY = 4
TOUCH = 6


def extended(array, sides, width):
    edges = {}
    for axis, dim in sides:
        size, length = (lax.axis_size(axis), array.shape[dim])
        up = [(i, (i + 1) % size) for i in range(size - 1)]
        last = lax.slice_in_dim(array, length - width, length, axis=dim)
        first = lax.slice_in_dim(array, 0, width, axis=dim)
        edges[dim] = (
            lax.ppermute(last, axis, up),
            lax.ppermute(first, axis, [(b, a) for a, b in up]),
        )
    done = []
    for _, dim in sides:
        low, high = edges[dim]
        around = [(width, width) if d in done else (0, 0) for d in range(array.ndim)]
        array = jnp.concatenate([jnp.pad(low, around), array, jnp.pad(high, around)], axis=dim)
        done.append(dim)
    return array


def sent_to_all(array, axis):
    size = lax.axis_size(axis)
    return lax.all_to_all(
        jnp.broadcast_to(array[None], (size, *array.shape)), axis, 0, 0, tiled=True
    )


def laid_out(parts, dim):
    parts = jnp.moveaxis(parts, 0, dim)
    dims = parts.shape
    return parts.reshape(*dims[:dim], dims[dim] * dims[dim + 1], *dims[dim + 2 :])


def collect(array, axis, dim):
    parts = sent_to_all(array, axis)
    return laid_out(parts, dim)


def lookup_small(table, index):
    matches = index[..., None] == jnp.arange(table.shape[0], dtype=jnp.int32)
    return jnp.sum(jnp.where(matches, table, 0), axis=-1)


def owner_ranks(owners, width):
    tagged = (owners[..., :, None] == jnp.arange(width, dtype=jnp.int32)).astype(jnp.int32)
    earlier = jnp.cumsum(tagged, axis=-2) - tagged
    return jnp.sum(earlier * tagged, axis=-1)


def on_device(a_blocks, prolong_t, elem_slot, touch_agg, nbr, nbr_agg, coarse_row):
    n_grp = lax.axis_size("grp")
    n_dev = lax.axis_size("dev")
    grp_index = lax.axis_index("grp")
    dev_index = lax.axis_index("dev")
    device = grp_index * n_dev + dev_index
    e_dev, width_c, width_b = prolong_t.shape
    half_y = EY // 2
    span_y = half_y + 1
    box_rows = n_dev * half_y + 1
    send_cap = (TOUCH + n_dev - 1) // n_dev
    group_rows = send_cap * ((box_rows + half_y) // span_y)
    rows_own = n_grp * group_rows
    row_width = width_c * width_c
    touched = lax.dynamic_index_in_dim(touch_agg, device, 0, keepdims=False)
    own_agg = lookup_small(touched, elem_slot)
    left_blocks = jnp.einsum(
        "ecb,ekbd->ekcd", prolong_t, a_blocks, preferred_element_type=jnp.float32
    ).astype(jnp.bfloat16)
    valid = nbr >= 0
    safe_nbr = jnp.where(valid, nbr, device * e_dev)
    source = safe_nbr // e_dev
    local = safe_nbr % e_dev
    source_grp = source // n_dev
    source_dev = source % n_dev
    padded = extended(prolong_t[None, None], (("grp", 0), ("dev", 1)), 1)
    blocks_pool = padded.reshape(9 * e_dev, width_c, width_b)
    where_from = ((source_grp - grp_index + 1) * 3 + (source_dev - dev_index + 1)) * e_dev + local
    neighbours = jnp.take(blocks_pool, where_from, axis=0)
    right_blocks = jnp.concatenate([prolong_t[:, None], neighbours], axis=1)
    products = jnp.einsum(
        "ekcd,ekxd->ekcx", left_blocks, right_blocks, preferred_element_type=jnp.float32
    ).reshape(e_dev, 7, row_width)
    same = valid & (nbr_agg == own_agg[:, None])
    apart = valid & jnp.logical_not(same)
    faces = products[:, 1:]
    diagonal = products[:, 0] + jnp.sum(jnp.where(same[:, :, None], faces, 0.0), axis=1)
    contrib = jnp.concatenate([diagonal[:, None], jnp.where(apart[:, :, None], faces, 0.0)], axis=1)
    member = (elem_slot[None, :] == jnp.arange(TOUCH, dtype=jnp.int32)[:, None]).astype(jnp.float32)
    partial_rows = jnp.dot(
        member,
        contrib.reshape(e_dev, 7 * row_width),
        precision=lax.Precision.HIGHEST,
        preferred_element_type=jnp.float32,
    ).reshape(TOUCH, 7, row_width)
    target_rows = lookup_small(coarse_row, touched)
    group_touch = lax.dynamic_slice_in_dim(touch_agg, grp_index * n_dev, n_dev, 0)
    group_targets = lookup_small(coarse_row, group_touch)
    owners = target_rows // rows_own
    slots = owners * send_cap + owner_ranks(owners, n_dev)
    outgoing = jax.ops.segment_sum(partial_rows, slots, num_segments=n_dev * send_cap)
    incoming = lax.all_to_all(
        outgoing.astype(jnp.bfloat16), "dev", split_axis=0, concat_axis=0, tiled=True
    ).astype(outgoing.dtype)
    sender_owners = group_targets // rows_own
    sender_ranks = owner_ranks(sender_owners, n_dev)
    matched = (sender_owners == dev_index)[:, :, None] & (
        sender_ranks[:, :, None] == jnp.arange(send_cap, dtype=jnp.int32)[None, None, :]
    )
    places = jnp.sum(jnp.where(matched, (group_targets % rows_own)[:, :, None], 0), axis=1)
    places = places + rows_own * (1 - jnp.any(matched, axis=1).astype(jnp.int32))
    table = jax.ops.segment_sum(incoming, places.reshape(-1), num_segments=rows_own + 1)[:rows_own]
    all_targets = lookup_small(coarse_row, touch_agg).reshape(n_grp, n_dev * TOUCH)
    owned = all_targets // rows_own == dev_index
    present = jnp.any(
        owned[:, :, None]
        & ((all_targets % rows_own)[:, :, None] == jnp.arange(rows_own, dtype=jnp.int32)),
        axis=1,
    )
    ranking = jnp.cumsum(present.astype(jnp.int32), axis=1) - 1
    own_present = lax.dynamic_index_in_dim(present, grp_index, 0, keepdims=False)
    own_ranking = lax.dynamic_index_in_dim(ranking, grp_index, 0, keepdims=False)
    chosen = own_present[None, :] & (
        own_ranking[None, :] == jnp.arange(group_rows, dtype=jnp.int32)[:, None]
    )
    source_rows = jnp.sum(
        jnp.where(chosen, jnp.arange(rows_own, dtype=jnp.int32)[None, :], 0), axis=1
    )
    filled = jnp.any(chosen, axis=1)
    packed = jnp.where(filled[:, None, None], jnp.take(table, source_rows, axis=0), 0.0)
    home_group = jnp.sum(jnp.where(present, jnp.arange(n_grp, dtype=jnp.int32)[:, None], 0), axis=0)
    anywhere = jnp.any(present, axis=0)
    compact = home_group * group_rows + jnp.sum(jnp.where(present, ranking, 0), axis=0)
    piece = collect(packed.astype(jnp.bfloat16), "grp", 0).astype(packed.dtype)
    count = piece.shape[0]
    inside = anywhere & (compact >= 0) & (compact < count)
    arrived_rows = jnp.take(piece, jnp.clip(compact, 0, count - 1), axis=0)
    return jnp.zeros_like(table) + jnp.where(inside[:, None, None], arrived_rows, 0.0)


def solution(mesh):
    in_specs = (
        P(("grp", "dev"), None, None, None),
        P(("grp", "dev"), None, None),
        P(("grp", "dev")),
        P(),
        P(("grp", "dev"), None),
        P(("grp", "dev"), None),
        P(),
    )
    out_specs = P("dev", None, None)
    return jax.shard_map(
        on_device, mesh=mesh, in_specs=in_specs, out_specs=out_specs, check_vma=False
    )
```

profile of v0, /device:TPU:1, one launch (start us, length us, event | category | flops | bytes accessed | tf_op | source)
XLA Modules:
  0.0 104.8 jit_solution(2321856532202243040)
XLA Ops:
  0.0 4.0 %collective-permute-start = (bf16[1,1,32,32,192]{4,3,2,1,0:T(8,128)(2,1)}, bf16[1,1,32,32,192]{4,3,2,1,0:T(8,128)(2,1)S(1)}, u32[]{:S(2)}, u32[]{:S(2)}) collective-permute-start(bf16[1,1,32,32,192]{4,3,2,1,0:T(8,128)(2,1)} %bitcast.67), channel_id=1, source_target_pairs={{0,1},{1,2},{2,3},{3,4},{4,5},{5,6},{6,7},{7,8},{8,9},{9,10},{10,1... | collective-permute-start | bytes 1179656 | tf_op jit(solution)/shard_map/ppermute | solution.py:18
  4.0 4.4 %collective-permute-start.1 = (bf16[1,1,32,32,192]{4,3,2,1,0:T(8,128)(2,1)}, bf16[1,1,32,32,192]{4,3,2,1,0:T(8,128)(2,1)S(1)}, u32[]{:S(2)}, u32[]{:S(2)}) collective-permute-start(bf16[1,1,32,32,192]{4,3,2,1,0:T(8,128)(2,1)} %bitcast.68), channel_id=1, source_target_pairs={{0,16},{16,32},{32,48},{48,64},{64,80},{80,96},{96,112},{1,17},{17... | collective-permute-start | bytes 1179656 | tf_op jit(solution)/shard_map/ppermute | solution.py:18
  8.4 1.9 %collective-permute-start.2 = (bf16[1,1,32,32,192]{4,3,2,1,0:T(8,128)(2,1)}, bf16[1,1,32,32,192]{4,3,2,1,0:T(8,128)(2,1)S(1)}, u32[]{:S(2)}, u32[]{:S(2)}) collective-permute-start(bf16[1,1,32,32,192]{4,3,2,1,0:T(8,128)(2,1)} %bitcast.69), channel_id=1, source_target_pairs={{16,0},{32,16},{48,32},{64,48},{80,64},{96,80},{112,96},{17,1},{33... | collective-permute-start | bytes 1179656 | tf_op jit(solution)/shard_map/ppermute | solution.py:19
  10.3 1.3 %collective-permute-start.3 = (bf16[1,1,32,32,192]{4,3,2,1,0:T(8,128)(2,1)}, bf16[1,1,32,32,192]{4,3,2,1,0:T(8,128)(2,1)S(1)}, u32[]{:S(2)}, u32[]{:S(2)}) collective-permute-start(bf16[1,1,32,32,192]{4,3,2,1,0:T(8,128)(2,1)} %bitcast.70), channel_id=1, source_target_pairs={{1,0},{2,1},{3,2},{4,3},{5,4},{6,5},{7,6},{8,7},{9,8},{10,9},{11,1... | collective-permute-start | bytes 1179656 | tf_op jit(solution)/shard_map/ppermute | solution.py:19
  11.6 1.0 select_reduce_fusion
  12.6 0.1 copy.23
  12.7 0.1 rem.111
  12.8 0.1 copy.24
  12.9 0.1 div.69
  13.0 0.1 copy.22
  13.2 0.1 ne.149
  13.3 0.3 fusion.14
  13.6 0.2 reduce_window_sum.33
  13.9 0.1 select_reduce_fusion.4
  14.0 0.1 fusion.18
  14.1 0.9 dynamic-slice_reduce_fusion
  15.0 0.9 select_reduce_fusion.3
  15.9 0.7 select_reduce_fusion.5
  16.6 0.7 not_and_fusion
  17.3 0.1 copy.26
  17.4 0.1 reshape.239
  17.5 0.0 copy-start.4
  17.5 0.0 copy-start.3
  17.6 0.0 copy-start.1
  17.6 13.5 %convolution_convert_fusion = bf16[32,7,192,32]{2,3,1,0:T(8,128)(2,1)} fusion(bf16[32,7,192,192]{3,2,1,0:T(8,128)(2,1)} %param.7, bf16[32,32,192]{2,1,0:T(8,128)(2,1)} %param.8), kind=kOutput, calls=%fused_computation.17 | convolution fusion | flops 529858560 | bytes 19660800 | tf_op jit(solution)/shard_map/ecb,ekbd->ekcd/dot_general | solution.py:75
  31.1 0.1 fusion.32
  31.2 0.0 copy-done.4
  31.2 0.1 constant_dynamic-slice_fusion
  31.3 0.0 copy-done.3
  31.3 0.3 select_reduce_fusion.2
  31.6 0.3 fusion.47
  31.9 0.1 copy.25
  32.0 0.2 select_reduce_fusion.6
  32.2 0.0 collective-permute-done
  32.3 0.0 collective-permute-done.1
  32.3 0.0 collective-permute-done.2
  32.3 0.0 collective-permute-done.3
  32.3 2.9 %fusion.2 = bf16[3,3,32,32,192]{4,3,2,1,0:T(8,128)(2,1)} fusion(bf16[1,1,32,32,192]{4,3,2,1,0:T(8,128)(2,1)S(1)} %collective-permute-done.3, bf16[1,1,32,32,192]{4,3,2,1,0:T(8,128)(2,1)S(1)} %collective-permute-done, bf16[1,1,32,32,192]{4,3,2,1,0:T(8,128)(2,1)S(1)} %collective-permute-done.2, bf16[1,1,32,32,192]{4,3,2,1,0:T(8,128)(2,1)S(1)} %bitcast.71, ...), kind=kLoop, calls=%fused_computation.9 | loop fusion | flops 24772608 | bytes 5505024 | tf_op jit(solution)/shard_map/concatenate | solution.py:25
  35.2 3.2 %gather_fusion = bf16[192,32,192]{2,1,0:T(8,128)(2,1)S(1)} fusion(bf16[288,32,192]{2,1,0:T(8,128)(2,1)} %bitcast.65, s32[1024]{0:T(1024)S(1)} %pad_clamp_fusion.2), kind=kCustom, calls=%fused_computation | custom fusion | bytes 4719360 | tf_op jit(solution)/shard_map/jit(_take)/gather | solution.py:87
  38.5 0.0 copy-start.2
  38.5 0.5 broadcast_select_fusion
  39.0 1.5 %copy-done = bf16[32,7,192,32]{2,3,1,0:T(8,128)(2,1)S(1)} copy-done((bf16[32,7,192,32]{2,3,1,0:T(8,128)(2,1)S(1)}, bf16[32,7,192,32]{2,3,1,0:T(8,128)(2,1)}, u32[]{:S(2)}) %copy-start) | copy-done | bytes 2752536
  40.5 0.1 copy-done.2
  40.6 2.5 %fusion.4 = f32[32,7,32,32]{3,2,0,1:T(8,128)} fusion(bf16[32,7,192,32]{2,3,1,0:T(8,128)(2,1)S(1)} %copy-done, bf16[32,6,32,192]{3,2,1,0:T(8,128)(2,1)S(1)} %broadcast_select_fusion, bf16[32,1,32,192]{3,2,1,0:T(8,128)(2,1)S(1)} %bitcast.72), kind=kOutput, calls=%fused_computation.12 | convolution fusion | flops 89456640 | bytes 6422528 | tf_op jit(solution)/shard_map/ekcd,ekxd->ekcx/dot_general | solution.py:89
  43.1 3.3 %reshape.234 = f32[32,7,1024]{2,0,1:T(8,128)S(1)} reshape(f32[32,7,32,32]{3,2,0,1:T(8,128)} %fusion.4) | data formatting | bytes 1835008 | tf_op jit(solution)/shard_map/reshape | solution.py:91
  46.4 0.2 select_reduce_fusion.1
  46.7 0.4 fusion.8
  47.1 0.1 copy.30
  47.2 0.8 scatter_fusion
  48.1 0.7 convert_element_type.53
  48.8 7.6 %all-to-all-start = ((bf16[16,7,1024]{2,1,0:T(8,128)(2,1)}), bf16[16,7,1024]{2,1,0:T(8,128)(2,1)S(1)}, u32[]{:S(2)}, u32[]{:S(2)}) async-start(bf16[16,7,1024]{2,1,0:T(8,128)(2,1)} %convert_element_type.53), calls=%async_computation | async-start | bytes 524288 | tf_op jit(solution)/shard_map/all_to_all | solution.py:110
  56.4 7.5 %all-to-all-done = bf16[16,7,1024]{2,1,0:T(8,128)(2,1)S(1)} async-done(((bf16[16,7,1024]{2,1,0:T(8,128)(2,1)}), bf16[16,7,1024]{2,1,0:T(8,128)(2,1)S(1)}, u32[]{:S(2)}, u32[]{:S(2)}) %all-to-all-start) | async-done | bytes 229408 | tf_op jit(solution)/shard_map/all_to_all | solution.py:110
  64.0 0.3 broadcast_in_dim.196
  64.4 1.3 %scatter_fusion.1 = f32[89,7,1024]{2,1,0:T(8,128)S(1)} fusion(f32[89,7,1024]{2,1,0:T(8,128)S(1)} %broadcast_in_dim.196, s32[16]{0:T(128)S(1)} %multiply_add_fusion, f32[16,7,1024]{2,1,0:T(8,128)S(1)} %convert_element_type.54), kind=kCustom, calls=%fused_computation.4 | custom fusion | flops 114688 | bytes 1376320 | tf_op jit(solution)/shard_map/scatter-add | solution.py:120
  65.7 1.3 %slice.20 = bf16[88,7,1024]{2,1,0:T(8,128)(2,1)} slice(f32[89,7,1024]{2,1,0:T(8,128)S(1)} %scatter_fusion.1), slice={[0:88], [0:7], [0:1024]} | slice | bytes 2523136 | tf_op jit(solution)/shard_map/slice | solution.py:120
  67.1 1.9 %gather_fusion.1 = bf16[11,7,1024]{2,1,0:T(8,128)(2,1)S(1)} fusion(bf16[88,7,1024]{2,1,0:T(8,128)(2,1)} %slice.20, s32[1024]{0:T(1024)S(1)} %pad_clamp_fusion.1), kind=kCustom, calls=%fused_computation.1 | custom fusion | bytes 315436 | tf_op jit(solution)/shard_map/jit(_take)/gather | solution.py:138
  69.0 0.1 select_convert_fusion
  69.1 1.3 %broadcast_in_dim.214 = bf16[8,11,7,1024]{3,2,1,0:T(8,128)(2,1)} broadcast(bf16[11,7,1024]{2,1,0:T(8,128)(2,1)S(1)} %select_convert_fusion), dimensions={1,2,3} | broadcast | bytes 1419264 | tf_op jit(solution)/shard_map/broadcast_in_dim | solution.py:33
  70.4 7.2 %all-to-all-start.1 = ((bf16[8,11,7,1024]{3,2,1,0:T(8,128)(2,1)}), bf16[8,11,7,1024]{3,2,1,0:T(8,128)(2,1)S(1)}, u32[]{:S(2)}, u32[]{:S(2)}) async-start(bf16[8,11,7,1024]{3,2,1,0:T(8,128)(2,1)} %broadcast_in_dim.214), calls=%async_computation.1 | async-start | bytes 2883584 | tf_op jit(solution)/shard_map/all_to_all | solution.py:32
  77.6 19.3 %all-to-all-done.1 = bf16[8,11,7,1024]{3,2,1,0:T(8,128)(2,1)S(1)} async-done(((bf16[8,11,7,1024]{3,2,1,0:T(8,128)(2,1)}), bf16[8,11,7,1024]{3,2,1,0:T(8,128)(2,1)S(1)}, u32[]{:S(2)}, u32[]{:S(2)}) %all-to-all-start.1) | async-done | bytes 1261600 | tf_op jit(solution)/shard_map/all_to_all | solution.py:32
  96.9 2.0 %bitcast_convert_fusion = f32[88,7,1024]{2,1,0:T(8,128)} fusion(bf16[8,11,7,1024]{3,2,1,0:T(8,128)(2,1)S(1)} %all-to-all-done.1), kind=kLoop, calls=%fused_computation.20 | loop fusion | flops 630784 | bytes 3784704 | tf_op jit(solution)/shard_map/convert_element_type | solution.py:142
  98.9 2.5 %gather_fusion.2 = f32[88,7,1024]{2,1,0:T(8,128)S(1)} fusion(f32[88,7,1024]{2,1,0:T(8,128)} %bitcast_convert_fusion, s32[1024]{0:T(1024)S(1)} %pad_clamp_fusion), kind=kCustom, calls=%fused_computation.2 | custom fusion | bytes 5046624 | tf_op jit(solution)/shard_map/jit(_take)/gather | solution.py:145
  101.5 0.4 select_select_fusion
  101.9 2.9 %copy.31 = f32[88,7,1024]{2,0,1:T(8,128)} copy(f32[88,7,1024]{2,1,0:T(8,128)S(1)} %select_select_fusion) | data formatting | bytes 5046272 | tf_op jit(solution)/shard_map/jit(_where)/select_n | solution.py:146
  (29 shorter events, 0.4 us)
Async XLA Ops:
  0.0 32.2 %collective-permute-start = (bf16[1,1,32,32,192]{4,3,2,1,0:T(8,128)(2,1)}, bf16[1,1,32,32,192]{4,3,2,1,0:T(8,128)(2,1)S(1)}, u32[]{:S(2)}, u32[]{:S(2)}) collective-permute-start(bf16[1,1,32,32,192]{4,3,2,1,0:T(8,128)(2,1)} %bitcast.67), channel_id=1, source_target_pairs={{0,1},{1,2},{2,3},{3,4},{4,5},{5,6},{6,7},{7,8},{8,9},{9,10},{10,1... | collective-permute-start | bytes 1179656 | tf_op jit(solution)/shard_map/ppermute | solution.py:18
  4.0 28.3 %collective-permute-start.1 = (bf16[1,1,32,32,192]{4,3,2,1,0:T(8,128)(2,1)}, bf16[1,1,32,32,192]{4,3,2,1,0:T(8,128)(2,1)S(1)}, u32[]{:S(2)}, u32[]{:S(2)}) collective-permute-start(bf16[1,1,32,32,192]{4,3,2,1,0:T(8,128)(2,1)} %bitcast.68), channel_id=1, source_target_pairs={{0,16},{16,32},{32,48},{48,64},{64,80},{80,96},{96,112},{1,17},{17... | collective-permute-start | bytes 1179656 | tf_op jit(solution)/shard_map/ppermute | solution.py:18
  8.4 23.9 %collective-permute-start.2 = (bf16[1,1,32,32,192]{4,3,2,1,0:T(8,128)(2,1)}, bf16[1,1,32,32,192]{4,3,2,1,0:T(8,128)(2,1)S(1)}, u32[]{:S(2)}, u32[]{:S(2)}) collective-permute-start(bf16[1,1,32,32,192]{4,3,2,1,0:T(8,128)(2,1)} %bitcast.69), channel_id=1, source_target_pairs={{16,0},{32,16},{48,32},{64,48},{80,64},{96,80},{112,96},{17,1},{33... | collective-permute-start | bytes 1179656 | tf_op jit(solution)/shard_map/ppermute | solution.py:19
  10.3 22.0 %collective-permute-start.3 = (bf16[1,1,32,32,192]{4,3,2,1,0:T(8,128)(2,1)}, bf16[1,1,32,32,192]{4,3,2,1,0:T(8,128)(2,1)S(1)}, u32[]{:S(2)}, u32[]{:S(2)}) collective-permute-start(bf16[1,1,32,32,192]{4,3,2,1,0:T(8,128)(2,1)} %bitcast.70), channel_id=1, source_target_pairs={{1,0},{2,1},{3,2},{4,3},{5,4},{6,5},{7,6},{8,7},{9,8},{10,9},{11,1... | collective-permute-start | bytes 1179656 | tf_op jit(solution)/shard_map/ppermute | solution.py:19
  17.5 13.7 %copy-start.4 = (s32[128,6]{0,1:T(8,128)S(1)}, s32[128,6]{0,1:T(8,128)}, u32[]{:S(2)}) copy-start(s32[128,6]{0,1:T(8,128)} %param.10) | copy-start | bytes 9220
  17.5 13.7 %copy-start.3 = (s32[528]{0:T(1024)S(1)}, s32[528]{0:T(1024)}, u32[]{:S(2)}) copy-start(s32[528]{0:T(1024)} %param.13) | copy-start | bytes 6340
  17.6 14.7 %copy-start.1 = (bf16[32,32,192]{2,1,0:T(8,128)(2,1)S(1)}, bf16[32,32,192]{2,1,0:T(8,128)(2,1)}, u32[]{:S(2)}) copy-start(bf16[32,32,192]{2,1,0:T(8,128)(2,1)} %param.8) | copy-start | bytes 1179652
  38.5 2.0 %copy-start = (bf16[32,7,192,32]{2,3,1,0:T(8,128)(2,1)S(1)}, bf16[32,7,192,32]{2,3,1,0:T(8,128)(2,1)}, u32[]{:S(2)}) copy-start(bf16[32,7,192,32]{2,3,1,0:T(8,128)(2,1)} %convolution_convert_fusion) | copy-start | bytes 8257540
  38.5 2.1 %copy-start.2 = (bf16[32,32,192]{2,1,0:T(8,128)(2,1)S(1)}, bf16[32,32,192]{2,1,0:T(8,128)(2,1)}, u32[]{:S(2)}) copy-start(bf16[32,32,192]{2,1,0:T(8,128)(2,1)} %param.8) | copy-start | bytes 1179652
  43.1 3.6 %copy-start.5 = (s32[32]{0:T(128)S(1)}, s32[32]{0:T(128)}, u32[]{:S(2)}) copy-start(s32[32]{0:T(128)} %param.9) | copy-start | bytes 388
  48.8 15.2 %all-to-all-start = ((bf16[16,7,1024]{2,1,0:T(8,128)(2,1)}), bf16[16,7,1024]{2,1,0:T(8,128)(2,1)S(1)}, u32[]{:S(2)}, u32[]{:S(2)}) async-start(bf16[16,7,1024]{2,1,0:T(8,128)(2,1)} %convert_element_type.53), calls=%async_computation | async-start | bytes 524288 | tf_op jit(solution)/shard_map/all_to_all | solution.py:110
  70.4 26.5 %all-to-all-start.1 = ((bf16[8,11,7,1024]{3,2,1,0:T(8,128)(2,1)}), bf16[8,11,7,1024]{3,2,1,0:T(8,128)(2,1)S(1)}, u32[]{:S(2)}, u32[]{:S(2)}) async-start(bf16[8,11,7,1024]{3,2,1,0:T(8,128)(2,1)} %broadcast_in_dim.214), calls=%async_computation.1 | async-start | bytes 2883584 | tf_op jit(solution)/shard_map/all_to_all | solution.py:32
where the time goes:
time: 105 us
  waiting for transfers between devices  26.8 us (26%)
  starting transfers between devices  26.4 us (25%)
  local copies, waits for them, and re-layouts  20.6 us (20%)
  matrix products  16.4 us (16%)
  other arithmetic  14.2 us (14%)
    all_to_all x1, waiting for transfers between devices, sent_to_all(): lax.all_to_all(jnp.broadcast_to(array[None], (size, *array.shape)), axis,...  19.3 us
    dot_general x1, matrix products, on_device(): jnp.einsum('ecb,ekbd->ekcd', prolong_t, a_blocks, preferred_element_type=...  13.5 us
    ppermute x2, starting transfers between devices, extended(): lax.ppermute(last, axis, up)  8.36 us
    all_to_all x1, starting transfers between devices, on_device(): lax.all_to_all(outgoing.astype(jnp.bfloat16), 'dev', split_axis=0, concat...  7.6 us
    all_to_all x1, waiting for transfers between devices, on_device(): lax.all_to_all(outgoing.astype(jnp.bfloat16), 'dev', split_axis=0, concat...  7.53 us
    all_to_all x1, starting transfers between devices, sent_to_all(): lax.all_to_all(jnp.broadcast_to(array[None], (size, *array.shape)), axis,...  7.23 us
    reshape x1, local copies, waits for them, and re-layouts, on_device(): products = jnp.einsum('ekcd,ekxd->ekcx', left_blocks, right_blocks, prefe...  3.34 us
    gather x1, local copies, waits for them, and re-layouts, on_device(): neighbours = jnp.take(blocks_pool, where_from, axis=0)  3.22 us
  transfers between devices with their start and end apart: 6, of which 2 were waited for; matrix products, arithmetic and copies ran while one was open for 20% of the time, Pallas kernels for 0%

commit v1 on v0

v1 whole, which is shorter than its diff:
```python
import jax
import jax.numpy as jnp
from jax import lax
from jax.experimental import pallas as pl
from jax.experimental.pallas import tpu as pltpu
from jax.sharding import PartitionSpec as P

TOUCH = 6
FACES = 6
BLOCKS = 7
LANES = 128
HALO = 8
F32 = jnp.float32
BF16 = jnp.bfloat16
SMEM = pltpu.MemorySpace.SMEM
VMEM = pltpu.MemorySpace.VMEM


def position(n_dev):
    return lax.axis_index("grp") * n_dev + lax.axis_index("dev")


def pack_kernel(n_dev, nbr_ref, p_ref, *refs):
    outs, bufs = refs[:4], refs[4:]
    e_dev = p_ref.shape[0]
    shift = e_dev.bit_length() - 1
    device = position(n_dev)
    homes = (device - n_dev, device + n_dev, device - 1, device + 1)

    def step(e, counts):
        hits = [jnp.bool_(False)] * 4
        for f in range(FACES):
            home = lax.shift_right_arithmetic(nbr_ref[e, f], shift)
            hits = [hit | (home == h) for hit, h in zip(hits, homes)]
        block = p_ref[e]
        new = []
        for d in range(4):
            bufs[d][jnp.minimum(counts[d], HALO)] = block
            new.append(counts[d] + hits[d].astype(jnp.int32))
        return tuple(new)

    lax.fori_loop(0, e_dev, step, (jnp.int32(0),) * 4, unroll=4)
    for d in range(4):
        outs[d][...] = bufs[d][0:HALO]


def main_kernel(n_dev, rows_own, slot_ref, nbr_ref, nagg_ref, crow_ref, touch_hbm, a_hbm, p_ref, h0, h1, h2, h3,
                out_ref, abuf, pool, acc, touch, seen, place, a_sems, t_sem):
    e_dev, width_c, _ = p_ref.shape
    shift = e_dev.bit_length() - 1
    device = position(n_dev)
    base8 = pl.multiple_of((device // 8) * 8, 8)
    row8 = device % 8
    t_copy = pltpu.make_async_copy(touch_hbm.at[pl.ds(base8, 8)], touch, t_sem)
    t_copy.start()

    def fetch(e):
        return pltpu.make_async_copy(a_hbm.at[e], abuf.at[e], a_sems.at[e])

    for e in range(e_dev):
        fetch(e).start()
    acc[...] = jnp.zeros_like(acc)
    out_ref[...] = jnp.zeros_like(out_ref)
    pool[0:e_dev] = p_ref[...]
    for d, h in enumerate((h0, h1, h2, h3)):
        pool[e_dev + HALO * d : e_dev + HALO * (d + 1)] = h[...]
    t_copy.wait()

    def clear(i, c):
        seen[i] = 0
        return c

    lax.fori_loop(0, 5 * e_dev, clear, 0, unroll=8)
    homes = (device - n_dev, device + n_dev, device - 1, device + 1)

    def side_of(n):
        home = lax.shift_right_arithmetic(n, shift)
        side = jnp.int32(4)
        for d, h in enumerate(homes):
            side = jnp.where(home == h, d, side)
        return side

    def mark(e, c):
        for f in range(FACES):
            n = nbr_ref[e, f]
            seen[side_of(n) * e_dev + (n & (e_dev - 1))] = 1
        return c

    lax.fori_loop(0, e_dev, mark, 0, unroll=2)

    def order(i, counts):
        new = []
        for d in range(4):
            at = d * e_dev + i
            hit = seen[at]
            place[at] = e_dev + HALO * d + jnp.minimum(counts[d], HALO - 1)
            new.append(counts[d] + hit)
        place[4 * e_dev + i] = i
        return tuple(new)

    lax.fori_loop(0, e_dev, order, (jnp.int32(0),) * 4, unroll=2)

    def element(e, c):
        fetch(e).wait()
        left = p_ref[e]
        slot = slot_ref[e]
        own = touch[row8, slot]
        total = None
        for k in range(BLOCKS):
            lk = jnp.dot(left, abuf[e, k], preferred_element_type=F32).astype(BF16)
            if k == 0:
                right = left
            else:
                n = nbr_ref[e, k - 1]
                right = pool[place[side_of(n) * e_dev + (n & (e_dev - 1))]]
            prod = lax.dot_general(lk, right, (((1,), (1,)), ((), ())), preferred_element_type=F32)
            if k == 0:
                total = prod
                continue
            valid = n >= 0
            same = valid & (nagg_ref[e, k - 1] == own)
            apart = valid & jnp.logical_not(nagg_ref[e, k - 1] == own)
            total = total + jnp.where(same, prod, 0.0)
            at = pl.multiple_of((slot * 8 + k) * width_c, width_c)
            acc[pl.ds(at, width_c), 0:width_c] += jnp.where(apart, prod, 0.0)
        at = pl.multiple_of(slot * 8 * width_c, width_c)
        acc[pl.ds(at, width_c), 0:width_c] += total
        return c

    lax.fori_loop(0, e_dev, element, 0)

    lane = lax.broadcasted_iota(jnp.int32, (8, LANES), 1)
    sub = lax.broadcasted_iota(jnp.int32, (8, LANES), 0)
    per = LANES // width_c
    for t in range(TOUCH):
        row = crow_ref[touch[row8, t]]
        owner = row // rows_own
        code = (row - owner * rows_own + 1).astype(F32)
        for j in range(width_c // per):
            value = None
            for i in range(per):
                piece = acc[pl.ds(t * 8 * width_c + j * per + i, 8, stride=width_c), :]
                if i == 0:
                    value = piece
                else:
                    piece = pltpu.roll(piece, i * width_c, 1)
                    value = jnp.where(lane >= i * width_c, piece, value)
            value = jnp.where(sub == 7, code, value)
            out_ref[owner, :, j * LANES : (j + 1) * LANES] = value.astype(BF16)


def combine_kernel(rows_own, in_ref, out_ref, sums, rank, codes):
    n_dev, _, width = in_ref.shape
    group_rows = out_ref.shape[0]

    def clear(i, c):
        rank[i] = -1
        return c

    lax.fori_loop(0, rows_own + 1, clear, 0, unroll=8)
    for r in range(group_rows + 1):
        codes[r] = 0
    sums[...] = jnp.zeros_like(sums)
    used = jnp.int32(0)
    for d in range(n_dev):
        code = in_ref[d, :, 0:LANES].astype(F32)[7, 0].astype(jnp.int32)
        old = rank[code]
        fresh = (code > 0) & (old < 0)
        at = jnp.where(code > 0, jnp.where(old < 0, jnp.minimum(used, group_rows - 1), old), group_rows)
        rank[code] = jnp.where(code > 0, at, -1)
        codes[at] = code
        used = used + fresh.astype(jnp.int32)
        sums[at] += in_ref[d].astype(F32)
    sub = lax.broadcasted_iota(jnp.int32, (8, width), 0)
    for r in range(group_rows):
        out_ref[r] = jnp.where(sub == 7, codes[r].astype(F32), sums[r]).astype(BF16)


def scatter_kernel(*refs):
    ins, out_ref, sink = refs[:-2], refs[-2], refs[-1]
    rows = out_ref.shape[0]
    out_ref[...] = jnp.zeros_like(out_ref)

    def put(block):
        value = block.astype(F32)
        code = value[7, 0].astype(jnp.int32)

        @pl.when(code > 0)
        def _():
            out_ref[jnp.clip(code - 1, 0, rows - 1)] = value[0:7]

    for ref in ins:
        if len(ref.shape) == 3:
            for r in range(ref.shape[0]):
                put(ref[r])
        else:
            for q in range(ref.shape[0]):
                for r in range(ref.shape[1]):
                    put(ref[q, r])


def on_device(a_blocks, prolong_t, elem_slot, touch_agg, nbr, nbr_agg, coarse_row):
    n_grp = lax.axis_size("grp")
    n_dev = lax.axis_size("dev")
    e_dev, width_c, width_b = prolong_t.shape
    half = 2
    group_rows = ((n_dev * half + 1) + half) // (half + 1)
    rows_own = n_grp * group_rows
    width = width_c * width_c
    smem = pl.BlockSpec(memory_space=SMEM)
    vmem = pl.BlockSpec(memory_space=VMEM)
    hbm = pl.BlockSpec(memory_space=pl.ANY)
    params = pltpu.CompilerParams(vmem_limit_bytes=56 << 20)

    def pack(*args):
        return pack_kernel(n_dev, *args)

    halo_shape = jax.ShapeDtypeStruct((HALO, width_c, width_b), BF16)
    packed = pl.pallas_call(
        pack, out_shape=(halo_shape,) * 4, in_specs=[smem, vmem], out_specs=(vmem,) * 4,
        scratch_shapes=[pltpu.VMEM((HALO + 1, width_c, width_b), BF16)] * 4, compiler_params=params, name="pack",
    )(nbr, prolong_t)
    up = lambda size: [(i, i + 1) for i in range(size - 1)]
    down = lambda size: [(i + 1, i) for i in range(size - 1)]
    from_low = lax.ppermute(packed[1], "grp", up(n_grp))
    from_high = lax.ppermute(packed[0], "grp", down(n_grp))
    from_left = lax.ppermute(packed[3], "dev", up(n_dev))
    from_right = lax.ppermute(packed[2], "dev", down(n_dev))

    def main(*args):
        return main_kernel(n_dev, rows_own, *args)

    outgoing = pl.pallas_call(
        main, out_shape=jax.ShapeDtypeStruct((n_dev, 8, width), BF16),
        in_specs=[smem] * 4 + [hbm] * 2 + [vmem] * 5, out_specs=vmem,
        scratch_shapes=[
            pltpu.VMEM((e_dev, BLOCKS, width_b, width_b), BF16),
            pltpu.VMEM((e_dev + 4 * HALO, width_c, width_b), BF16),
            pltpu.VMEM((TOUCH * 8 * width_c, LANES), F32),
            pltpu.SMEM((8, TOUCH), jnp.int32),
            pltpu.SMEM((5 * e_dev,), jnp.int32),
            pltpu.SMEM((5 * e_dev,), jnp.int32),
            pltpu.SemaphoreType.DMA((e_dev,)),
            pltpu.SemaphoreType.DMA(()),
        ],
        compiler_params=params, name="products",
    )(elem_slot, nbr, nbr_agg, coarse_row, touch_agg, a_blocks, prolong_t, from_low, from_high, from_left, from_right)
    incoming = lax.all_to_all(outgoing, "dev", split_axis=0, concat_axis=0, tiled=True)

    def combine(*args):
        return combine_kernel(rows_own, *args)

    mine = pl.pallas_call(
        combine, out_shape=jax.ShapeDtypeStruct((group_rows, 8, width), BF16), in_specs=[vmem], out_specs=vmem,
        scratch_shapes=[pltpu.VMEM((group_rows + 1, 8, width), F32), pltpu.SMEM((rows_own + 1,), jnp.int32),
                        pltpu.SMEM((group_rows + 1,), jnp.int32)],
        compiler_params=params, name="combine",
    )(incoming)
    swap = [(i, i ^ 1) for i in range(n_grp)]
    across = [lax.ppermute(mine, "grp", [(i, (i + 2 * k) % n_grp) for i in range(n_grp)]) for k in range(1, n_grp // 2)]
    twin = lax.ppermute(mine, "grp", swap)
    others = lax.ppermute(jnp.stack(across), "grp", swap)
    pieces = (mine, twin, *across, others)
    return pl.pallas_call(
        scatter_kernel, out_shape=jax.ShapeDtypeStruct((rows_own, BLOCKS, width), F32), in_specs=[vmem] * len(pieces),
        out_specs=vmem, scratch_shapes=[pltpu.SMEM((1,), jnp.int32)], compiler_params=params, name="scatter",
    )(*pieces)


def solution(mesh):
    in_specs = (
        P(("grp", "dev"), None, None, None),
        P(("grp", "dev"), None, None),
        P(("grp", "dev")),
        P(),
        P(("grp", "dev"), None),
        P(("grp", "dev"), None),
        P(),
    )
    return jax.shard_map(
        on_device, mesh=mesh, in_specs=in_specs, out_specs=P("dev", None, None), check_vma=False
    )
```

time: 105 us -> 104 us (level)
  Pallas kernels: 0 us -> 44.9 us
  waiting for transfers between devices: 26.8 us -> 9.37 us
  blocking collectives: 0 us -> 17.4 us
  matrix products: 16.4 us -> 0 us
  other arithmetic: 14.2 us -> 0.06 us
  local copies, waits for them, and re-layouts: 20.6 us -> 11 us
  starting transfers between devices: 26.4 us -> 20.6 us
    pallas_call x0 -> x4, Pallas kernels: none -> 44.9 us  [the longest x1 33 us: on_device(): pl.pallas_call(main, out_shape=jax.ShapeDtypeStruct((n_dev, 8, width), BF...]
    all_to_all x2 -> x0, waiting for transfers between devices: 26.8 us -> none  [the longest x1 19.3 us: sent_to_all(): lax.all_to_all(jnp.broadcast_to(array[None], (size, *array.shape)), axis,...]
    all_to_all x0 -> x1, blocking collectives: none -> 17.4 us  [on_device(): lax.all_to_all(outgoing, 'dev', split_axis=0, concat_axis=0, tiled=True)]
    dot_general x3 -> x0, matrix products: 16.4 us -> none  [the longest x1 13.5 us: on_device(): jnp.einsum('ecb,ekbd->ekcd', prolong_t, a_blocks, preferred_element_type=...]
    all_to_all x2 -> x0, starting transfers between devices: 14.8 us -> none  [the longest x1 7.6 us: on_device(): lax.all_to_all(outgoing.astype(jnp.bfloat16), 'dev', split_axis=0, concat...]
    ppermute x4 -> x9, waiting for transfers between devices: 0.01 us -> 9.37 us  [the longest x3 5.64 us: on_device(): lax.ppermute(mine, 'grp', [(i, (i + 2 * k) % n_grp) for i in range(n_grp)])]
    ppermute x4 -> x9, starting transfers between devices: 11.6 us -> 20.6 us  [the longest x1 6.1 us: on_device(): others = lax.ppermute(jnp.stack(across), 'grp', swap)]
    gather x3 -> x0, local copies, waits for them, and re-layouts: 7.68 us -> none  [the longest x1 3.22 us: on_device(): neighbours = jnp.take(blocks_pool, where_from, axis=0)]
  transfers between devices with their start and end apart: 6 -> 9, of which waited for: 2 -> 5; matrix products, arithmetic and copies ran while one was open for 20% -> 3% of each run, Pallas kernels for 0% -> 0%
where the time goes in v1:
time: 104 us; the launch traced here: 103 us
  Pallas kernels  44.9 us (43%)
  starting transfers between devices  20.6 us (20%)
  blocking collectives  17.4 us (17%)
  local copies, waits for them, and re-layouts  11 us (11%)
  waiting for transfers between devices  9.37 us (9%)
    pallas_call x1, Pallas kernels, on_device(): pl.pallas_call(main, out_shape=jax.ShapeDtypeStruct((n_dev, 8, width), BF...  33 us
    all_to_all x1, blocking collectives, on_device(): lax.all_to_all(outgoing, 'dev', split_axis=0, concat_axis=0, tiled=True)  17.4 us
    pallas_call x1, Pallas kernels, on_device(): pl.pallas_call(scatter_kernel, out_shape=jax.ShapeDtypeStruct((rows_own,...  7.21 us
    unnamed x21, local copies, waits for them, and re-layouts  6.28 us
    ppermute x1, starting transfers between devices, on_device(): others = lax.ppermute(jnp.stack(across), 'grp', swap)  6.1 us
    ppermute x3, waiting for transfers between devices, on_device(): lax.ppermute(mine, 'grp', [(i, (i + 2 * k) % n_grp) for i in range(n_grp)])  5.64 us
    ppermute x1, starting transfers between devices, on_device(): from_low = lax.ppermute(packed[1], 'grp', up(n_grp))  4.92 us
    pallas_call x1, local copies, waits for them, and re-layouts, on_device(): pl.pallas_call(scatter_kernel, out_shape=jax.ShapeDtypeStruct((rows_own,...  4.74 us
  transfers between devices with their start and end apart: 9, of which 5 were waited for; matrix products, arithmetic and copies ran while one was open for 3% of the time, Pallas kernels for 0%

profile of v1, /device:TPU:1, one launch (start us, length us, event | category | flops | bytes accessed | tf_op | source)
XLA Modules:
  0.0 103.4 jit_solution(13244549940974497947)
XLA Ops:
  0.0 1.4 %copy.9.args_0_.args_1_ = s32[32,6]{1,0:T(8,128)} copy(s32[32,6]{0,1:T(8,128)} %param.11) | data formatting | bytes 1536 | tf_op args[4]
  1.4 2.8 %pack.1 = (bf16[8,32,192]{2,1,0:T(8,128)(2,1)}, bf16[8,32,192]{2,1,0:T(8,128)(2,1)}, bf16[8,32,192]{2,1,0:T(8,128)(2,1)}, bf16[8,32,192]{2,1,0:T(8,128)(2,1)}) custom-call(s32[32,6]{1,0:T(8,128)} %copy.9.args_0_.args_1_, bf16[32,32,192]{2,1,0:T(8,128)(2,1)} %args_6_.4), custom_call_target="tpu_custom_call" | custom-call | tf_op jit(solution)/shard_map/pack/pallas_call | solution.py:219
  4.2 4.9 %collective-permute-start = (bf16[8,32,192]{2,1,0:T(8,128)(2,1)}, bf16[8,32,192]{2,1,0:T(8,128)(2,1)S(1)}, u32[]{:S(2)}, u32[]{:S(2)}) collective-permute-start(bf16[8,32,192]{2,1,0:T(8,128)(2,1)} %get-tuple-element.9), channel_id=1, source_target_pairs={{0,16},{16,32},{32,48},{48,64},{64,80},{80,96},{96,112},{1,17},{17... | collective-permute-start | bytes 294920 | tf_op jit(solution)/shard_map/ppermute | solution.py:225
  9.1 1.9 %collective-permute-start.1 = (bf16[8,32,192]{2,1,0:T(8,128)(2,1)}, bf16[8,32,192]{2,1,0:T(8,128)(2,1)S(1)}, u32[]{:S(2)}, u32[]{:S(2)}) collective-permute-start(bf16[8,32,192]{2,1,0:T(8,128)(2,1)} %get-tuple-element.10), channel_id=1, source_target_pairs={{16,0},{32,16},{48,32},{64,48},{80,64},{96,80},{112,96},{17,1},{33... | collective-permute-start | bytes 294920 | tf_op jit(solution)/shard_map/ppermute | solution.py:226
  11.0 3.1 %collective-permute-start.2 = (bf16[8,32,192]{2,1,0:T(8,128)(2,1)}, bf16[8,32,192]{2,1,0:T(8,128)(2,1)S(1)}, u32[]{:S(2)}, u32[]{:S(2)}) collective-permute-start(bf16[8,32,192]{2,1,0:T(8,128)(2,1)} %get-tuple-element.11), channel_id=1, source_target_pairs={{0,1},{1,2},{2,3},{3,4},{4,5},{5,6},{6,7},{7,8},{8,9},{9,10},{10,1... | collective-permute-start | bytes 294920 | tf_op jit(solution)/shard_map/ppermute | solution.py:227
  14.2 1.3 %collective-permute-start.3 = (bf16[8,32,192]{2,1,0:T(8,128)(2,1)}, bf16[8,32,192]{2,1,0:T(8,128)(2,1)S(1)}, u32[]{:S(2)}, u32[]{:S(2)}) collective-permute-start(bf16[8,32,192]{2,1,0:T(8,128)(2,1)} %get-tuple-element.12), channel_id=1, source_target_pairs={{1,0},{2,1},{3,2},{4,3},{5,4},{6,5},{7,6},{8,7},{9,8},{10,9},{11,1... | collective-permute-start | bytes 294920 | tf_op jit(solution)/shard_map/ppermute | solution.py:228
  15.5 1.4 %copy.10.args_2_ = s32[32,6]{1,0:T(8,128)} copy(s32[32,6]{0,1:T(8,128)} %param.12) | data formatting | bytes 1536 | tf_op args[5]
  16.8 1.4 %copy.11.args_4_ = s32[128,6]{1,0:T(8,128)} copy(s32[128,6]{0,1:T(8,128)} %param.10) | data formatting | bytes 6144 | tf_op args[3]
  18.2 0.0 collective-permute-done.args_7_
  18.2 0.0 copy-start.5
  18.2 0.0 collective-permute-done.1.args_8_
  18.3 0.0 copy-start.6
  18.3 0.0 collective-permute-done.2.args_9_
  18.3 0.0 copy-start.7
  18.3 1.8 %collective-permute-done.3.args_10_ = bf16[8,32,192]{2,1,0:T(8,128)(2,1)S(1)} collective-permute-done((bf16[8,32,192]{2,1,0:T(8,128)(2,1)}, bf16[8,32,192]{2,1,0:T(8,128)(2,1)S(1)}, u32[]{:S(2)}, u32[]{:S(2)}) %collective-permute-start.3) | collective-permute-done | bytes 98336 | tf_op jit(solution)/shard_map/ppermute | solution.py:228
  20.1 0.0 copy-done.5
  20.1 0.0 copy-done.6
  20.1 0.0 copy-done.7
  20.1 0.0 copy-start.8
  20.1 0.6 copy-done.8
  20.7 33.0 %products.1 = bf16[16,8,1024]{2,1,0:T(8,128)(2,1)} custom-call(s32[32]{0:T(128)} %args_0_.5, s32[32,6]{1,0:T(8,128)} %copy.9.args_0_.args_1_, s32[32,6]{1,0:T(8,128)} %copy.10.args_2_, s32[528]{0:T(1024)} %args_3_.4, s32[128,6]{1,0:T(8,128)} %copy.11.args_4_, bf16[32,7,192,192]{3,2,1,0:T(8,128)(2,1)} %args_5_.4, bf16[32,32,192]{2,1,0:T(8,128)(2,1)} %args_6_.4, ...), custom_call_target="tpu_custom_call" | custom-call | tf_op jit(solution)/shard_map/products/pallas_call | solution.py:233
  53.7 17.4 %all_to_all.5.args_0_ = bf16[16,8,1024]{2,1,0:T(8,128)(2,1)} all-to-all(bf16[16,8,1024]{2,1,0:T(8,128)(2,1)} %products.1), channel_id=1, replica_groups=mesh['grp'=8,'dev'=16] {'dev'}, dimensions={0} | all-to-all | bytes 524288 | tf_op jit(solution)/shard_map/all_to_all | solution.py:248
  71.1 1.8 %combine.1.refs_0_ = bf16[11,8,1024]{2,1,0:T(8,128)(2,1)} custom-call(bf16[16,8,1024]{2,1,0:T(8,128)(2,1)} %all_to_all.5.args_0_), custom_call_target="tpu_custom_call" | custom-call | tf_op jit(solution)/shard_map/combine/pallas_call | solution.py:253
  73.0 0.8 collective-permute-start.7
  73.8 2.0 %collective-permute-start.6 = (bf16[11,8,1024]{2,1,0:T(8,128)(2,1)}, bf16[11,8,1024]{2,1,0:T(8,128)(2,1)S(1)}, u32[]{:S(2)}, u32[]{:S(2)}) collective-permute-start(bf16[11,8,1024]{2,1,0:T(8,128)(2,1)} %combine.1.refs_0_), channel_id=1, source_target_pairs={{0,64},{16,80},{32,96},{48,112},{64,0},{80,16},{96,32},{112,48},{1... | collective-permute-start | bytes 540680 | tf_op jit(solution)/shard_map/ppermute | solution.py:260
  75.8 0.4 collective-permute-start.5
  76.1 1.4 %collective-permute-done.7.refs_4_ = bf16[11,8,1024]{2,1,0:T(8,128)(2,1)S(1)} collective-permute-done((bf16[11,8,1024]{2,1,0:T(8,128)(2,1)}, bf16[11,8,1024]{2,1,0:T(8,128)(2,1)S(1)}, u32[]{:S(2)}, u32[]{:S(2)}) %collective-permute-start.7) | collective-permute-done | bytes 180256 | tf_op jit(solution)/shard_map/ppermute | solution.py:260
  77.5 0.0 copy-start
  77.5 2.4 %collective-permute-done.6.refs_3_ = bf16[11,8,1024]{2,1,0:T(8,128)(2,1)S(1)} collective-permute-done((bf16[11,8,1024]{2,1,0:T(8,128)(2,1)}, bf16[11,8,1024]{2,1,0:T(8,128)(2,1)S(1)}, u32[]{:S(2)}, u32[]{:S(2)}) %collective-permute-start.6) | collective-permute-done | bytes 180256 | tf_op jit(solution)/shard_map/ppermute | solution.py:260
  79.9 0.0 copy-start.1
  79.9 1.9 %collective-permute-done.5.refs_2_ = bf16[11,8,1024]{2,1,0:T(8,128)(2,1)S(1)} collective-permute-done((bf16[11,8,1024]{2,1,0:T(8,128)(2,1)}, bf16[11,8,1024]{2,1,0:T(8,128)(2,1)S(1)}, u32[]{:S(2)}, u32[]{:S(2)}) %collective-permute-start.5) | collective-permute-done | bytes 180256 | tf_op jit(solution)/shard_map/ppermute | solution.py:260
  81.8 0.0 copy-start.2
  81.8 0.1 pad_maximum_fusion
  81.9 6.1 %collective-permute-start.8 = (bf16[3,11,8,1024]{3,2,1,0:T(8,128)(2,1)S(1)}, bf16[3,11,8,1024]{3,2,1,0:T(8,128)(2,1)S(1)}, u32[]{:S(2)}, u32[]{:S(2)}) collective-permute-start(bf16[3,11,8,1024]{3,2,1,0:T(8,128)(2,1)S(1)} %pad_maximum_fusion), channel_id=1, source_target_pairs={{0,16},{16,0},{32,48},{48,32},{64,80},{80,64},{96,112},{112,96},{1... | collective-permute-start | bytes 1622024 | tf_op jit(solution)/shard_map/ppermute | solution.py:262
  88.0 0.1 collective-permute-start.4
  88.0 1.9 %collective-permute-done.4.refs_1_ = bf16[11,8,1024]{2,1,0:T(8,128)(2,1)S(1)} collective-permute-done((bf16[11,8,1024]{2,1,0:T(8,128)(2,1)}, bf16[11,8,1024]{2,1,0:T(8,128)(2,1)S(1)}, u32[]{:S(2)}, u32[]{:S(2)}) %collective-permute-start.4) | collective-permute-done | bytes 180256 | tf_op jit(solution)/shard_map/ppermute | solution.py:261
  90.0 0.0 copy-start.4
  90.0 0.0 collective-permute-done.8.refs_5_
  90.0 0.0 copy-done
  90.0 0.0 copy-done.1
  90.0 0.0 copy-done.2
  90.0 0.7 copy-done.4
  90.7 0.0 copy-start.3
  90.7 0.8 copy-done.3
  91.5 7.2 %scatter.1 = f32[88,7,1024]{2,1,0:T(8,128)} custom-call(bf16[11,8,1024]{2,1,0:T(8,128)(2,1)} %combine.1.refs_0_, bf16[11,8,1024]{2,1,0:T(8,128)(2,1)} %copy-done.4, bf16[11,8,1024]{2,1,0:T(8,128)(2,1)} %copy-done.2, bf16[11,8,1024]{2,1,0:T(8,128)(2,1)} %copy-done.1, bf16[11,8,1024]{2,1,0:T(8,128)(2,1)} %copy-done, bf16[3,11,8,1024]{3,2,1,0:T(8,128)(2,1)} %copy-done.3), custom_call_target="tpu_custom_call" | custom-call | tf_op jit(solution)/shard_map/scatter/pallas_call | solution.py:264
  98.7 4.7 %copy.12 = f32[88,7,1024]{2,0,1:T(8,128)} copy(f32[88,7,1024]{2,1,0:T(8,128)} %scatter.1) | data formatting | bytes 5046272 | tf_op jit(solution)/shard_map/scatter/pallas_call | solution.py:264
Async XLA Ops:
  4.2 14.1 %collective-permute-start = (bf16[8,32,192]{2,1,0:T(8,128)(2,1)}, bf16[8,32,192]{2,1,0:T(8,128)(2,1)S(1)}, u32[]{:S(2)}, u32[]{:S(2)}) collective-permute-start(bf16[8,32,192]{2,1,0:T(8,128)(2,1)} %get-tuple-element.9), channel_id=1, source_target_pairs={{0,16},{16,32},{32,48},{48,64},{64,80},{80,96},{96,112},{1,17},{17... | collective-permute-start | bytes 294920 | tf_op jit(solution)/shard_map/ppermute | solution.py:225
  9.1 9.2 %collective-permute-start.1 = (bf16[8,32,192]{2,1,0:T(8,128)(2,1)}, bf16[8,32,192]{2,1,0:T(8,128)(2,1)S(1)}, u32[]{:S(2)}, u32[]{:S(2)}) collective-permute-start(bf16[8,32,192]{2,1,0:T(8,128)(2,1)} %get-tuple-element.10), channel_id=1, source_target_pairs={{16,0},{32,16},{48,32},{64,48},{80,64},{96,80},{112,96},{17,1},{33... | collective-permute-start | bytes 294920 | tf_op jit(solution)/shard_map/ppermute | solution.py:226
  11.0 7.2 %collective-permute-start.2 = (bf16[8,32,192]{2,1,0:T(8,128)(2,1)}, bf16[8,32,192]{2,1,0:T(8,128)(2,1)S(1)}, u32[]{:S(2)}, u32[]{:S(2)}) collective-permute-start(bf16[8,32,192]{2,1,0:T(8,128)(2,1)} %get-tuple-element.11), channel_id=1, source_target_pairs={{0,1},{1,2},{2,3},{3,4},{4,5},{5,6},{6,7},{7,8},{8,9},{9,10},{10,1... | collective-permute-start | bytes 294920 | tf_op jit(solution)/shard_map/ppermute | solution.py:227
  14.2 5.9 %collective-permute-start.3 = (bf16[8,32,192]{2,1,0:T(8,128)(2,1)}, bf16[8,32,192]{2,1,0:T(8,128)(2,1)S(1)}, u32[]{:S(2)}, u32[]{:S(2)}) collective-permute-start(bf16[8,32,192]{2,1,0:T(8,128)(2,1)} %get-tuple-element.12), channel_id=1, source_target_pairs={{1,0},{2,1},{3,2},{4,3},{5,4},{6,5},{7,6},{8,7},{9,8},{10,9},{11,1... | collective-permute-start | bytes 294920 | tf_op jit(solution)/shard_map/ppermute | solution.py:228
  18.2 1.8 %copy-start.5 = (bf16[8,32,192]{2,1,0:T(8,128)(2,1)}, bf16[8,32,192]{2,1,0:T(8,128)(2,1)S(1)}, u32[]{:S(2)}) copy-start(bf16[8,32,192]{2,1,0:T(8,128)(2,1)S(1)} %collective-permute-done.args_7_) | copy-start | bytes 294916
  18.3 1.8 %copy-start.6 = (bf16[8,32,192]{2,1,0:T(8,128)(2,1)}, bf16[8,32,192]{2,1,0:T(8,128)(2,1)S(1)}, u32[]{:S(2)}) copy-start(bf16[8,32,192]{2,1,0:T(8,128)(2,1)S(1)} %collective-permute-done.1.args_8_) | copy-start | bytes 294916
  18.3 1.8 %copy-start.7 = (bf16[8,32,192]{2,1,0:T(8,128)(2,1)}, bf16[8,32,192]{2,1,0:T(8,128)(2,1)S(1)}, u32[]{:S(2)}) copy-start(bf16[8,32,192]{2,1,0:T(8,128)(2,1)S(1)} %collective-permute-done.2.args_9_) | copy-start | bytes 294916
  20.1 0.6 copy-start.8
  73.0 4.6 %collective-permute-start.7 = (bf16[11,8,1024]{2,1,0:T(8,128)(2,1)}, bf16[11,8,1024]{2,1,0:T(8,128)(2,1)S(1)}, u32[]{:S(2)}, u32[]{:S(2)}) collective-permute-start(bf16[11,8,1024]{2,1,0:T(8,128)(2,1)} %combine.1.refs_0_), channel_id=1, source_target_pairs={{0,96},{16,112},{32,0},{48,16},{64,32},{80,48},{96,64},{112,80},{1... | collective-permute-start | bytes 540680 | tf_op jit(solution)/shard_map/ppermute | solution.py:260
  73.8 6.1 %collective-permute-start.6 = (bf16[11,8,1024]{2,1,0:T(8,128)(2,1)}, bf16[11,8,1024]{2,1,0:T(8,128)(2,1)S(1)}, u32[]{:S(2)}, u32[]{:S(2)}) collective-permute-start(bf16[11,8,1024]{2,1,0:T(8,128)(2,1)} %combine.1.refs_0_), channel_id=1, source_target_pairs={{0,64},{16,80},{32,96},{48,112},{64,0},{80,16},{96,32},{112,48},{1... | collective-permute-start | bytes 540680 | tf_op jit(solution)/shard_map/ppermute | solution.py:260
  75.8 6.0 %collective-permute-start.5 = (bf16[11,8,1024]{2,1,0:T(8,128)(2,1)}, bf16[11,8,1024]{2,1,0:T(8,128)(2,1)S(1)}, u32[]{:S(2)}, u32[]{:S(2)}) collective-permute-start(bf16[11,8,1024]{2,1,0:T(8,128)(2,1)} %combine.1.refs_0_), channel_id=1, source_target_pairs={{0,32},{16,48},{32,64},{48,80},{64,96},{80,112},{96,0},{112,16},{1... | collective-permute-start | bytes 540680 | tf_op jit(solution)/shard_map/ppermute | solution.py:260
  77.5 12.5 %copy-start = (bf16[11,8,1024]{2,1,0:T(8,128)(2,1)}, bf16[11,8,1024]{2,1,0:T(8,128)(2,1)S(1)}, u32[]{:S(2)}) copy-start(bf16[11,8,1024]{2,1,0:T(8,128)(2,1)S(1)} %collective-permute-done.7.refs_4_) | copy-start | bytes 540676
  79.9 10.1 %copy-start.1 = (bf16[11,8,1024]{2,1,0:T(8,128)(2,1)}, bf16[11,8,1024]{2,1,0:T(8,128)(2,1)S(1)}, u32[]{:S(2)}) copy-start(bf16[11,8,1024]{2,1,0:T(8,128)(2,1)S(1)} %collective-permute-done.6.refs_3_) | copy-start | bytes 540676
  81.8 8.2 %copy-start.2 = (bf16[11,8,1024]{2,1,0:T(8,128)(2,1)}, bf16[11,8,1024]{2,1,0:T(8,128)(2,1)S(1)}, u32[]{:S(2)}) copy-start(bf16[11,8,1024]{2,1,0:T(8,128)(2,1)S(1)} %collective-permute-done.5.refs_2_) | copy-start | bytes 540676
  81.9 8.1 %collective-permute-start.8 = (bf16[3,11,8,1024]{3,2,1,0:T(8,128)(2,1)S(1)}, bf16[3,11,8,1024]{3,2,1,0:T(8,128)(2,1)S(1)}, u32[]{:S(2)}, u32[]{:S(2)}) collective-permute-start(bf16[3,11,8,1024]{3,2,1,0:T(8,128)(2,1)S(1)} %pad_maximum_fusion), channel_id=1, source_target_pairs={{0,16},{16,0},{32,48},{48,32},{64,80},{80,64},{96,112},{112,96},{1... | collective-permute-start | bytes 1622024 | tf_op jit(solution)/shard_map/ppermute | solution.py:262
  88.0 2.0 %collective-permute-start.4 = (bf16[11,8,1024]{2,1,0:T(8,128)(2,1)}, bf16[11,8,1024]{2,1,0:T(8,128)(2,1)S(1)}, u32[]{:S(2)}, u32[]{:S(2)}) collective-permute-start(bf16[11,8,1024]{2,1,0:T(8,128)(2,1)} %combine.1.refs_0_), channel_id=1, source_target_pairs={{0,16},{16,0},{32,48},{48,32},{64,80},{80,64},{96,112},{112,96},{1... | collective-permute-start | bytes 540680 | tf_op jit(solution)/shard_map/ppermute | solution.py:261
  90.0 0.7 copy-start.4
  90.7 0.8 copy-start.3

commit v2 on v1

v2 whole, which is shorter than its diff:
```python
import jax
import jax.numpy as jnp
from jax import lax
from jax.experimental import pallas as pl
from jax.experimental.pallas import tpu as pltpu
from jax.sharding import PartitionSpec as P

TOUCH = 6
FACES = 6
BLOCKS = 7
LANES = 128
HALO = 8
F32 = jnp.float32
BF16 = jnp.bfloat16
SMEM = pltpu.MemorySpace.SMEM
VMEM = pltpu.MemorySpace.VMEM


def position(n_dev):
    return lax.axis_index("grp") * n_dev + lax.axis_index("dev")


def pack_kernel(n_dev, nbr_ref, p_ref, *refs):
    outs, bufs = refs[:4], refs[4:]
    e_dev = p_ref.shape[0]
    shift = e_dev.bit_length() - 1
    device = position(n_dev)
    homes = (device - n_dev, device + n_dev, device - 1, device + 1)

    def step(e, counts):
        hits = [jnp.bool_(False)] * 4
        for f in range(FACES):
            home = lax.shift_right_arithmetic(nbr_ref[f, e], shift)
            hits = [hit | (home == h) for hit, h in zip(hits, homes)]
        block = p_ref[e]
        new = []
        for d in range(4):
            bufs[d][jnp.minimum(counts[d], HALO)] = block
            new.append(counts[d] + hits[d].astype(jnp.int32))
        return tuple(new)

    lax.fori_loop(0, e_dev, step, (jnp.int32(0),) * 4, unroll=4)
    for d in range(4):
        outs[d][...] = bufs[d][0:HALO]


def main_kernel(n_dev, rows_own, slot_ref, nbr_ref, nagg_ref, crow_ref, touch_ref, a_hbm, p_ref, h0, h1, h2, h3,
                out_ref, abuf, pool, acc, lefts0, lefts1, seen, place, a_sems, h_sems):
    e_dev, width_c, _ = p_ref.shape
    shift = e_dev.bit_length() - 1
    device = position(n_dev)

    def fetch(e):
        return pltpu.make_async_copy(a_hbm.at[e], abuf.at[e], a_sems.at[e])

    for e in range(e_dev):
        fetch(e).start()
    halos = [
        pltpu.make_async_copy(h, pool.at[pl.ds(e_dev + HALO * d, HALO)], h_sems.at[d])
        for d, h in enumerate((h0, h1, h2, h3))
    ]
    for copy in halos:
        copy.start()
    acc[...] = jnp.zeros_like(acc)
    out_ref[...] = jnp.zeros_like(out_ref)
    pool[0:e_dev] = p_ref[...]

    def clear(i, c):
        seen[i] = 0
        return c

    lax.fori_loop(0, 5 * e_dev, clear, 0, unroll=8)
    homes = (device - n_dev, device + n_dev, device - 1, device + 1)

    def side_of(n):
        home = lax.shift_right_arithmetic(n, shift)
        side = jnp.int32(4)
        for d, h in enumerate(homes):
            side = jnp.where(home == h, d, side)
        return side

    def mark(e, c):
        for f in range(FACES):
            n = nbr_ref[f, e]
            seen[side_of(n) * e_dev + (n & (e_dev - 1))] = 1
        return c

    lax.fori_loop(0, e_dev, mark, 0, unroll=2)

    def order(i, counts):
        new = []
        for d in range(4):
            at = d * e_dev + i
            hit = seen[at]
            place[at] = e_dev + HALO * d + jnp.minimum(counts[d], HALO - 1)
            new.append(counts[d] + hit)
        place[4 * e_dev + i] = i
        return tuple(new)

    lax.fori_loop(0, e_dev, order, (jnp.int32(0),) * 4, unroll=2)
    for copy in halos:
        copy.wait()

    def make_lefts(e, lefts):
        left = p_ref[e]
        for k in range(BLOCKS):
            lefts[k] = jnp.dot(left, abuf[e, k], preferred_element_type=F32).astype(BF16)

    def add_products(e, lefts):
        slot = slot_ref[e]
        own = touch_ref[slot, device]
        total = None
        for k in range(BLOCKS):
            if k == 0:
                right = p_ref[e]
            else:
                n = nbr_ref[k - 1, e]
                right = pool[place[side_of(n) * e_dev + (n & (e_dev - 1))]]
            prod = lax.dot_general(lefts[k], right, (((1,), (1,)), ((), ())), preferred_element_type=F32)
            if k == 0:
                total = prod
                continue
            valid = n >= 0
            same = valid & (nagg_ref[k - 1, e] == own)
            apart = valid & (nagg_ref[k - 1, e] != own)
            total = total + jnp.where(same, prod, 0.0)
            at = pl.multiple_of((slot * 8 + k) * width_c, width_c)
            acc[pl.ds(at, width_c), 0:width_c] += jnp.where(apart, prod, 0.0)
        at = pl.multiple_of(slot * 8 * width_c, width_c)
        acc[pl.ds(at, width_c), 0:width_c] += total

    fetch(0).wait()
    make_lefts(0, lefts0)

    def two(i, c):
        e = 2 * i + 1
        fetch(e).wait()
        fetch(e + 1).wait()
        add_products(e - 1, lefts0)
        make_lefts(e, lefts1)
        add_products(e, lefts1)
        make_lefts(e + 1, lefts0)
        return c

    lax.fori_loop(0, e_dev // 2 - 1, two, 0)
    fetch(e_dev - 1).wait()
    make_lefts(e_dev - 1, lefts1)
    add_products(e_dev - 2, lefts0)
    add_products(e_dev - 1, lefts1)

    lane = lax.broadcasted_iota(jnp.int32, (8, LANES), 1)
    sub = lax.broadcasted_iota(jnp.int32, (8, LANES), 0)
    per = LANES // width_c
    for t in range(TOUCH):
        row = crow_ref[touch_ref[t, device]]
        owner = row // rows_own
        code = (row - owner * rows_own + 1).astype(F32)
        for j in range(width_c // per):
            value = None
            for i in range(per):
                piece = acc[pl.ds(t * 8 * width_c + j * per + i, 8, stride=width_c), :]
                if i == 0:
                    value = piece
                else:
                    piece = pltpu.roll(piece, i * width_c, 1)
                    value = jnp.where(lane >= i * width_c, piece, value)
            value = jnp.where(sub == 7, code, value)
            out_ref[owner, :, j * LANES : (j + 1) * LANES] = value.astype(BF16)


def combine_kernel(rows_own, group_rows, in_ref, out_ref, rank, codes):
    slots, width = in_ref.shape
    n_dev = slots // 8
    piece = out_ref.shape[0]

    def clear(i, c):
        rank[i] = -1
        return c

    lax.fori_loop(0, rows_own + 1, clear, 0, unroll=8)
    for r in range(group_rows + 1):
        codes[r] = 0
    used = jnp.int32(0)
    lane = lax.broadcasted_iota(jnp.int32, (1, slots), 1)
    key = jnp.full((1, slots), -1, jnp.int32)
    for d in range(n_dev):
        code = in_ref[8 * d : 8 * d + 8, 0:LANES].astype(F32)[7, 0].astype(jnp.int32)
        old = rank[code]
        fresh = (code > 0) & (old < 0)
        at = jnp.where(code > 0, jnp.where(old < 0, jnp.minimum(used, group_rows - 1), old), group_rows)
        rank[code] = jnp.where(code > 0, at, -1)
        codes[at] = code
        used = used + fresh.astype(jnp.int32)
        mine = (lane >= 8 * d) & (lane < 8 * d + 7)
        key = jnp.where(mine, jnp.where(code > 0, (lane - 8 * d) * group_rows + at, -1), key)
    row = lax.broadcasted_iota(jnp.int32, (piece, slots), 0)
    chosen = jnp.where(row == key, 1.0, 0.0).astype(BF16)
    out = jnp.dot(chosen, in_ref[...], preferred_element_type=F32)
    at = lax.broadcasted_iota(jnp.int32, (1, width), 1) % piece
    of_row = at % group_rows
    tags = jnp.zeros((1, width), F32)
    for r in range(group_rows):
        tags = jnp.where((of_row == r) & (at < BLOCKS * group_rows), codes[r].astype(F32), tags)
    rows = lax.broadcasted_iota(jnp.int32, (piece, width), 0)
    out_ref[...] = jnp.where(rows >= BLOCKS * group_rows, tags, out).astype(BF16)


def scatter_kernel(rows_own, group_rows, *refs):
    ins, out_hbm, held, chosen, out_buf, in_sems, out_sems = refs[:-6], *refs[-6:]
    total, width = out_buf.shape
    piece = ins[0].shape[-2]
    sources = [ref if len(ref.shape) == 2 else ref.at[q] for ref in ins for q in range(1 if len(ref.shape) == 2 else ref.shape[0])]
    copies = [
        pltpu.make_async_copy(ref, held.at[pl.ds(q * piece, piece)], in_sems.at[q]) for q, ref in enumerate(sources)
    ]
    for copy in copies:
        copy.start()
    depth = held.shape[0]
    lane = lax.broadcasted_iota(jnp.int32, (1, depth), 1)
    in_piece = lane % piece
    block = in_piece // group_rows
    for copy in copies:
        copy.wait()
    tags = jnp.zeros((1, depth), F32)
    for q in range(len(sources)):
        tag = held[(q + 1) * piece - 8 : (q + 1) * piece, 0:depth].astype(F32)[7:8]
        tags = jnp.where((lane >= q * piece) & (lane < (q + 1) * piece), tag, tags)
    tags = tags.astype(jnp.int32)
    key = jnp.where((tags > 0) & (block < BLOCKS), block * rows_own + tags - 1, -1)
    for s in range(BLOCKS):
        row = lax.broadcasted_iota(jnp.int32, (rows_own, depth), 0) + s * rows_own
        chosen[s * rows_own : (s + 1) * rows_own] = jnp.where(row == key, 1.0, 0.0).astype(BF16)
    n_out = out_sems.shape[0]
    step = width // n_out
    outs = []
    for n in range(n_out):
        cols = pl.ds(n * step, step)
        out_buf[:, n * step : (n + 1) * step] = jnp.dot(
            chosen[...], held[:, n * step : (n + 1) * step], preferred_element_type=F32
        )
        copy = pltpu.make_async_copy(out_buf.at[:, cols], out_hbm.at[:, cols], out_sems.at[n])
        copy.start()
        outs.append(copy)
    for copy in outs:
        copy.wait()


def on_device(a_blocks, prolong_t, elem_slot, touch_agg, nbr, nbr_agg, coarse_row):
    n_grp = lax.axis_size("grp")
    n_dev = lax.axis_size("dev")
    e_dev, width_c, width_b = prolong_t.shape
    half = 2
    group_rows = ((n_dev * half + 1) + half) // (half + 1)
    rows_own = n_grp * group_rows
    width = width_c * width_c
    smem = pl.BlockSpec(memory_space=SMEM)
    vmem = pl.BlockSpec(memory_space=VMEM)
    hbm = pl.BlockSpec(memory_space=pl.ANY)
    params = pltpu.CompilerParams(vmem_limit_bytes=56 << 20)

    def pack(*args):
        return pack_kernel(n_dev, *args)

    halo_shape = jax.ShapeDtypeStruct((HALO, width_c, width_b), BF16)
    packed = pl.pallas_call(
        pack, out_shape=(halo_shape,) * 4, in_specs=[smem, vmem], out_specs=(vmem,) * 4,
        scratch_shapes=[pltpu.VMEM((HALO + 1, width_c, width_b), BF16)] * 4, compiler_params=params, name="pack",
    )(nbr.T, prolong_t)
    up = lambda size: [(i, i + 1) for i in range(size - 1)]
    down = lambda size: [(i + 1, i) for i in range(size - 1)]
    from_low = lax.ppermute(packed[1], "grp", up(n_grp))
    from_high = lax.ppermute(packed[0], "grp", down(n_grp))
    from_left = lax.ppermute(packed[3], "dev", up(n_dev))
    from_right = lax.ppermute(packed[2], "dev", down(n_dev))

    def main(*args):
        return main_kernel(n_dev, rows_own, *args)

    outgoing = pl.pallas_call(
        main, out_shape=jax.ShapeDtypeStruct((n_dev, 8, width), BF16),
        in_specs=[smem] * 5 + [hbm, vmem] + [hbm] * 4, out_specs=vmem,
        scratch_shapes=[
            pltpu.VMEM((e_dev, BLOCKS, width_b, width_b), BF16),
            pltpu.VMEM((e_dev + 4 * HALO, width_c, width_b), BF16),
            pltpu.VMEM((TOUCH * 8 * width_c, LANES), F32),
            pltpu.VMEM((BLOCKS, width_c, width_b), BF16),
            pltpu.VMEM((BLOCKS, width_c, width_b), BF16),
            pltpu.SMEM((5 * e_dev,), jnp.int32),
            pltpu.SMEM((5 * e_dev,), jnp.int32),
            pltpu.SemaphoreType.DMA((e_dev,)),
            pltpu.SemaphoreType.DMA((4,)),
        ],
        compiler_params=params, name="products",
    )(elem_slot, nbr.T, nbr_agg.T, coarse_row, touch_agg.T, a_blocks, prolong_t, from_low, from_high, from_left, from_right)
    incoming = lax.all_to_all(outgoing, "dev", split_axis=0, concat_axis=0, tiled=True)
    piece = 8 * ((BLOCKS * group_rows) // 8 + 1)

    def combine(*args):
        return combine_kernel(rows_own, group_rows, *args)

    mine = pl.pallas_call(
        combine, out_shape=jax.ShapeDtypeStruct((piece, width), BF16), in_specs=[vmem], out_specs=vmem,
        scratch_shapes=[pltpu.SMEM((rows_own + 1,), jnp.int32), pltpu.SMEM((group_rows + 1,), jnp.int32)],
        compiler_params=params, name="combine",
    )(incoming.reshape(n_dev * 8, width))
    swap = [(i, i ^ 1) for i in range(n_grp)]
    across = [lax.ppermute(mine, "grp", [(i, (i + 2 * k) % n_grp) for i in range(n_grp)]) for k in range(1, n_grp // 2)]
    twin = lax.ppermute(mine, "grp", swap)
    others = lax.ppermute(jnp.stack(across), "grp", swap)
    pieces = (mine, twin, *across, others)

    def scatter(*args):
        return scatter_kernel(rows_own, group_rows, *args)

    out = pl.pallas_call(
        scatter, out_shape=jax.ShapeDtypeStruct((BLOCKS * rows_own, width), F32), in_specs=[hbm] * len(pieces),
        out_specs=hbm,
        scratch_shapes=[
            pltpu.VMEM((n_grp * piece, width), BF16),
            pltpu.VMEM((BLOCKS * rows_own, n_grp * piece), BF16),
            pltpu.VMEM((BLOCKS * rows_own, width), F32),
            pltpu.SemaphoreType.DMA((n_grp,)),
            pltpu.SemaphoreType.DMA((4,)),
        ],
        compiler_params=params, name="scatter",
    )(*pieces)
    return jnp.swapaxes(out.reshape(BLOCKS, rows_own, width), 0, 1)


def solution(mesh):
    in_specs = (
        P(("grp", "dev"), None, None, None),
        P(("grp", "dev"), None, None),
        P(("grp", "dev")),
        P(),
        P(("grp", "dev"), None),
        P(("grp", "dev"), None),
        P(),
    )
    return jax.shard_map(
        on_device, mesh=mesh, in_specs=in_specs, out_specs=P("dev", None, None), check_vma=False
    )
```

time: 104 us -> 78.7 us (0.76)
  Pallas kernels: 44.9 us -> 26.4 us
  local copies, waits for them, and re-layouts: 11 us -> 2.12 us
  waiting for transfers between devices: 9.37 us -> 11.7 us
    pallas_call x1, Pallas kernels: 33 us -> 17.8 us  [on_device(): pl.pallas_call(main, out_shape=jax.ShapeDtypeStruct((n_dev, 8, width), BF...]
    pallas_call x1 -> x0, local copies, waits for them, and re-layouts: 4.74 us -> none  [on_device(): pl.pallas_call(scatter_kernel, out_shape=jax.ShapeDtypeStruct((rows_own,...]
    unnamed x21 -> x18, local copies, waits for them, and re-layouts: 6.28 us -> 2.12 us
    pallas_call x2, Pallas kernels: 9.06 us -> 5.71 us  [the longest x1 3.77 us: on_device(): pl.pallas_call(scatter, out_shape=jax.ShapeDtypeStruct((BLOCKS * rows_own...]
    ppermute x1, waiting for transfers between devices: 1.79 us -> 3.68 us  [on_device(): from_right = lax.ppermute(packed[2], 'dev', down(n_dev))]
  transfers between devices with their start and end apart: 9 -> 9, of which waited for: 5 -> 7; matrix products, arithmetic and copies ran while one was open for 3% -> 0% of each run, Pallas kernels for 0% -> 0%
where the time goes in v2:
time: 78.7 us; the launch traced here: 78.4 us
  Pallas kernels  26.4 us (34%)
  starting transfers between devices  20.6 us (26%)
  blocking collectives  17.4 us (22%)
  waiting for transfers between devices  11.7 us (15%)
  local copies, waits for them, and re-layouts  2.12 us (3%)
    pallas_call x1, Pallas kernels, on_device(): pl.pallas_call(main, out_shape=jax.ShapeDtypeStruct((n_dev, 8, width), BF...  17.8 us
    all_to_all x1, blocking collectives, on_device(): lax.all_to_all(outgoing, 'dev', split_axis=0, concat_axis=0, tiled=True)  17.4 us
    ppermute x1, starting transfers between devices, on_device(): others = lax.ppermute(jnp.stack(across), 'grp', swap)  6.1 us
    ppermute x3, waiting for transfers between devices, on_device(): lax.ppermute(mine, 'grp', [(i, (i + 2 * k) % n_grp) for i in range(n_grp)])  5.29 us
    ppermute x1, starting transfers between devices, on_device(): from_low = lax.ppermute(packed[1], 'grp', up(n_grp))  4.92 us
    pallas_call x1, Pallas kernels, on_device(): pl.pallas_call(scatter, out_shape=jax.ShapeDtypeStruct((BLOCKS * rows_own...  3.77 us
    ppermute x1, waiting for transfers between devices, on_device(): from_right = lax.ppermute(packed[2], 'dev', down(n_dev))  3.68 us
    ppermute x3, starting transfers between devices, on_device(): lax.ppermute(mine, 'grp', [(i, (i + 2 * k) % n_grp) for i in range(n_grp)])  3.18 us
  transfers between devices with their start and end apart: 9, of which 7 were waited for; matrix products, arithmetic and copies ran while one was open for 0% of the time, Pallas kernels for 0%

profile of v2, /device:TPU:1, one launch (start us, length us, event | category | flops | bytes accessed | tf_op | source)
XLA Modules:
  0.0 78.4 jit_solution(2576862720872376400)
XLA Ops:
  0.0 2.9 %pack.1 = (bf16[8,32,192]{2,1,0:T(8,128)(2,1)}, bf16[8,32,192]{2,1,0:T(8,128)(2,1)}, bf16[8,32,192]{2,1,0:T(8,128)(2,1)}, bf16[8,32,192]{2,1,0:T(8,128)(2,1)}) custom-call(s32[6,32]{1,0:T(8,128)} %bitcast.14, bf16[32,32,192]{2,1,0:T(8,128)(2,1)} %args_6_.4), custom_call_target="tpu_custom_call" | custom-call | tf_op jit(solution)/shard_map/pack/pallas_call | solution.py:265
  2.9 4.9 %collective-permute-start = (bf16[8,32,192]{2,1,0:T(8,128)(2,1)}, bf16[8,32,192]{2,1,0:T(8,128)(2,1)S(1)}, u32[]{:S(2)}, u32[]{:S(2)}) collective-permute-start(bf16[8,32,192]{2,1,0:T(8,128)(2,1)} %get-tuple-element.9), channel_id=1, source_target_pairs={{0,16},{16,32},{32,48},{48,64},{64,80},{80,96},{96,112},{1,17},{17... | collective-permute-start | bytes 294920 | tf_op jit(solution)/shard_map/ppermute | solution.py:271
  7.8 1.9 %collective-permute-start.1 = (bf16[8,32,192]{2,1,0:T(8,128)(2,1)}, bf16[8,32,192]{2,1,0:T(8,128)(2,1)S(1)}, u32[]{:S(2)}, u32[]{:S(2)}) collective-permute-start(bf16[8,32,192]{2,1,0:T(8,128)(2,1)} %get-tuple-element.10), channel_id=1, source_target_pairs={{16,0},{32,16},{48,32},{64,48},{80,64},{96,80},{112,96},{17,1},{33... | collective-permute-start | bytes 294920 | tf_op jit(solution)/shard_map/ppermute | solution.py:272
  9.7 3.1 %collective-permute-start.2 = (bf16[8,32,192]{2,1,0:T(8,128)(2,1)}, bf16[8,32,192]{2,1,0:T(8,128)(2,1)S(1)}, u32[]{:S(2)}, u32[]{:S(2)}) collective-permute-start(bf16[8,32,192]{2,1,0:T(8,128)(2,1)} %get-tuple-element.11), channel_id=1, source_target_pairs={{0,1},{1,2},{2,3},{3,4},{4,5},{5,6},{6,7},{7,8},{8,9},{9,10},{10,1... | collective-permute-start | bytes 294920 | tf_op jit(solution)/shard_map/ppermute | solution.py:273
  12.9 1.3 %collective-permute-start.3 = (bf16[8,32,192]{2,1,0:T(8,128)(2,1)}, bf16[8,32,192]{2,1,0:T(8,128)(2,1)S(1)}, u32[]{:S(2)}, u32[]{:S(2)}) collective-permute-start(bf16[8,32,192]{2,1,0:T(8,128)(2,1)} %get-tuple-element.12), channel_id=1, source_target_pairs={{1,0},{2,1},{3,2},{4,3},{5,4},{6,5},{7,6},{8,7},{9,8},{10,9},{11,1... | collective-permute-start | bytes 294920 | tf_op jit(solution)/shard_map/ppermute | solution.py:274
  14.2 0.0 collective-permute-done.args_7_
  14.2 0.0 copy-start.5
  14.2 0.1 collective-permute-done.1.args_8_
  14.3 0.0 copy-start.6
  14.3 0.8 %collective-permute-done.2.args_9_ = bf16[8,32,192]{2,1,0:T(8,128)(2,1)S(1)} collective-permute-done((bf16[8,32,192]{2,1,0:T(8,128)(2,1)}, bf16[8,32,192]{2,1,0:T(8,128)(2,1)S(1)}, u32[]{:S(2)}, u32[]{:S(2)}) %collective-permute-start.2) | collective-permute-done | bytes 98336 | tf_op jit(solution)/shard_map/ppermute | solution.py:273
  15.1 0.0 copy-start.7
  15.1 3.7 %collective-permute-done.3.args_10_ = bf16[8,32,192]{2,1,0:T(8,128)(2,1)S(1)} collective-permute-done((bf16[8,32,192]{2,1,0:T(8,128)(2,1)}, bf16[8,32,192]{2,1,0:T(8,128)(2,1)S(1)}, u32[]{:S(2)}, u32[]{:S(2)}) %collective-permute-start.3) | collective-permute-done | bytes 98336 | tf_op jit(solution)/shard_map/ppermute | solution.py:274
  18.8 0.0 copy-start.8
  18.8 0.0 copy-done.5
  18.8 0.0 copy-done.6
  18.8 0.0 copy-done.7
  18.8 0.7 copy-done.8
  19.5 17.8 %products.1 = bf16[16,8,1024]{2,1,0:T(8,128)(2,1)} custom-call(s32[32]{0:T(128)} %args_0_.4, s32[6,32]{1,0:T(8,128)} %bitcast.15, s32[6,32]{1,0:T(8,128)} %bitcast.16, s32[528]{0:T(1024)} %args_3_.4, s32[6,128]{1,0:T(8,128)} %bitcast.17, bf16[32,7,192,192]{3,2,1,0:T(8,128)(2,1)} %args_5_.4, bf16[32,32,192]{2,1,0:T(8,128)(2,1)} %args_6_.4, ...), custom_call_target="tpu_custom_call" | custom-call | tf_op jit(solution)/shard_map/products/pallas_call | solution.py:279
  37.3 17.4 %all_to_all.5 = bf16[16,8,1024]{2,1,0:T(8,128)(2,1)} all-to-all(bf16[16,8,1024]{2,1,0:T(8,128)(2,1)} %products.1), channel_id=1, replica_groups=mesh['grp'=8,'dev'=16] {'dev'}, dimensions={0} | all-to-all | bytes 524288 | tf_op jit(solution)/shard_map/all_to_all | solution.py:295
  54.6 1.9 %combine.1.args_0_ = bf16[80,1024]{1,0:T(8,128)(2,1)} custom-call(bf16[128,1024]{1,0:T(8,128)(2,1)} %bitcast.10), custom_call_target="tpu_custom_call" | custom-call | tf_op jit(solution)/shard_map/combine/pallas_call | solution.py:301
  56.6 0.8 %collective-permute-start.7 = (bf16[80,1024]{1,0:T(8,128)(2,1)}, bf16[80,1024]{1,0:T(8,128)(2,1)S(1)}, u32[]{:S(2)}, u32[]{:S(2)}) collective-permute-start(bf16[80,1024]{1,0:T(8,128)(2,1)} %combine.1.args_0_), channel_id=1, source_target_pairs={{0,96},{16,112},{32,0},{48,16},{64,32},{80,48},{96,64},{112,80},{1... | collective-permute-start | bytes 491528 | tf_op jit(solution)/shard_map/ppermute | solution.py:307
  57.4 2.0 %collective-permute-start.6 = (bf16[80,1024]{1,0:T(8,128)(2,1)}, bf16[80,1024]{1,0:T(8,128)(2,1)S(1)}, u32[]{:S(2)}, u32[]{:S(2)}) collective-permute-start(bf16[80,1024]{1,0:T(8,128)(2,1)} %combine.1.args_0_), channel_id=1, source_target_pairs={{0,64},{16,80},{32,96},{48,112},{64,0},{80,16},{96,32},{112,48},{1... | collective-permute-start | bytes 491528 | tf_op jit(solution)/shard_map/ppermute | solution.py:307
  59.4 0.4 collective-permute-start.5
  59.8 1.2 %collective-permute-done.7.args_4_ = bf16[80,1024]{1,0:T(8,128)(2,1)S(1)} collective-permute-done((bf16[80,1024]{1,0:T(8,128)(2,1)}, bf16[80,1024]{1,0:T(8,128)(2,1)S(1)}, u32[]{:S(2)}, u32[]{:S(2)}) %collective-permute-start.7) | collective-permute-done | bytes 163872 | tf_op jit(solution)/shard_map/ppermute | solution.py:307
  61.0 0.0 copy-start
  61.0 2.3 %collective-permute-done.6.args_3_ = bf16[80,1024]{1,0:T(8,128)(2,1)S(1)} collective-permute-done((bf16[80,1024]{1,0:T(8,128)(2,1)}, bf16[80,1024]{1,0:T(8,128)(2,1)S(1)}, u32[]{:S(2)}, u32[]{:S(2)}) %collective-permute-start.6) | collective-permute-done | bytes 163872 | tf_op jit(solution)/shard_map/ppermute | solution.py:307
  63.3 0.0 copy-start.1
  63.3 1.8 %collective-permute-done.5.args_2_ = bf16[80,1024]{1,0:T(8,128)(2,1)S(1)} collective-permute-done((bf16[80,1024]{1,0:T(8,128)(2,1)}, bf16[80,1024]{1,0:T(8,128)(2,1)S(1)}, u32[]{:S(2)}, u32[]{:S(2)}) %collective-permute-start.5) | collective-permute-done | bytes 163872 | tf_op jit(solution)/shard_map/ppermute | solution.py:307
  65.1 0.0 copy-start.2
  65.1 0.1 pad_maximum_fusion
  65.1 6.1 %collective-permute-start.8 = (bf16[3,80,1024]{2,1,0:T(8,128)(2,1)S(1)}, bf16[3,80,1024]{2,1,0:T(8,128)(2,1)S(1)}, u32[]{:S(2)}, u32[]{:S(2)}) collective-permute-start(bf16[3,80,1024]{2,1,0:T(8,128)(2,1)S(1)} %pad_maximum_fusion), channel_id=1, source_target_pairs={{0,16},{16,0},{32,48},{48,32},{64,80},{80,64},{96,112},{112,96},{1... | collective-permute-start | bytes 1474568 | tf_op jit(solution)/shard_map/ppermute | solution.py:309
  71.2 0.1 collective-permute-start.4
  71.3 1.8 %collective-permute-done.4.args_1_ = bf16[80,1024]{1,0:T(8,128)(2,1)S(1)} collective-permute-done((bf16[80,1024]{1,0:T(8,128)(2,1)}, bf16[80,1024]{1,0:T(8,128)(2,1)S(1)}, u32[]{:S(2)}, u32[]{:S(2)}) %collective-permute-start.4) | collective-permute-done | bytes 163872 | tf_op jit(solution)/shard_map/ppermute | solution.py:308
  73.2 0.0 copy-start.4
  73.2 0.0 collective-permute-done.8.args_5_
  73.2 0.0 copy-done
  73.2 0.0 copy-done.1
  73.2 0.0 copy-done.2
  73.2 0.6 copy-done.4
  73.8 0.0 copy-start.3
  73.8 0.8 %copy-done.3 = bf16[3,80,1024]{2,1,0:T(8,128)(2,1)} copy-done((bf16[3,80,1024]{2,1,0:T(8,128)(2,1)}, bf16[3,80,1024]{2,1,0:T(8,128)(2,1)S(1)}, u32[]{:S(2)}) %copy-start.3) | copy-done | bytes 491544
  74.6 3.8 %scatter.1 = f32[616,1024]{1,0:T(8,128)} custom-call(bf16[80,1024]{1,0:T(8,128)(2,1)} %combine.1.args_0_, bf16[80,1024]{1,0:T(8,128)(2,1)} %copy-done.4, bf16[80,1024]{1,0:T(8,128)(2,1)} %copy-done.2, bf16[80,1024]{1,0:T(8,128)(2,1)} %copy-done.1, bf16[80,1024]{1,0:T(8,128)(2,1)} %copy-done, bf16[3,80,1024]{2,1,0:T(8,128)(2,1)} %copy-done.3), custom_call_target="tpu_custom_call" | custom-call | tf_op jit(solution)/shard_map/scatter/pallas_call | solution.py:315
Async XLA Ops:
  2.9 11.3 %collective-permute-start = (bf16[8,32,192]{2,1,0:T(8,128)(2,1)}, bf16[8,32,192]{2,1,0:T(8,128)(2,1)S(1)}, u32[]{:S(2)}, u32[]{:S(2)}) collective-permute-start(bf16[8,32,192]{2,1,0:T(8,128)(2,1)} %get-tuple-element.9), channel_id=1, source_target_pairs={{0,16},{16,32},{32,48},{48,64},{64,80},{80,96},{96,112},{1,17},{17... | collective-permute-start | bytes 294920 | tf_op jit(solution)/shard_map/ppermute | solution.py:271
  7.8 6.5 %collective-permute-start.1 = (bf16[8,32,192]{2,1,0:T(8,128)(2,1)}, bf16[8,32,192]{2,1,0:T(8,128)(2,1)S(1)}, u32[]{:S(2)}, u32[]{:S(2)}) collective-permute-start(bf16[8,32,192]{2,1,0:T(8,128)(2,1)} %get-tuple-element.10), channel_id=1, source_target_pairs={{16,0},{32,16},{48,32},{64,48},{80,64},{96,80},{112,96},{17,1},{33... | collective-permute-start | bytes 294920 | tf_op jit(solution)/shard_map/ppermute | solution.py:272
  9.7 5.4 %collective-permute-start.2 = (bf16[8,32,192]{2,1,0:T(8,128)(2,1)}, bf16[8,32,192]{2,1,0:T(8,128)(2,1)S(1)}, u32[]{:S(2)}, u32[]{:S(2)}) collective-permute-start(bf16[8,32,192]{2,1,0:T(8,128)(2,1)} %get-tuple-element.11), channel_id=1, source_target_pairs={{0,1},{1,2},{2,3},{3,4},{4,5},{5,6},{6,7},{7,8},{8,9},{9,10},{10,1... | collective-permute-start | bytes 294920 | tf_op jit(solution)/shard_map/ppermute | solution.py:273
  12.9 5.9 %collective-permute-start.3 = (bf16[8,32,192]{2,1,0:T(8,128)(2,1)}, bf16[8,32,192]{2,1,0:T(8,128)(2,1)S(1)}, u32[]{:S(2)}, u32[]{:S(2)}) collective-permute-start(bf16[8,32,192]{2,1,0:T(8,128)(2,1)} %get-tuple-element.12), channel_id=1, source_target_pairs={{1,0},{2,1},{3,2},{4,3},{5,4},{6,5},{7,6},{8,7},{9,8},{10,9},{11,1... | collective-permute-start | bytes 294920 | tf_op jit(solution)/shard_map/ppermute | solution.py:274
  14.2 4.6 %copy-start.5 = (bf16[8,32,192]{2,1,0:T(8,128)(2,1)}, bf16[8,32,192]{2,1,0:T(8,128)(2,1)S(1)}, u32[]{:S(2)}) copy-start(bf16[8,32,192]{2,1,0:T(8,128)(2,1)S(1)} %collective-permute-done.args_7_) | copy-start | bytes 294916
  14.3 4.5 %copy-start.6 = (bf16[8,32,192]{2,1,0:T(8,128)(2,1)}, bf16[8,32,192]{2,1,0:T(8,128)(2,1)S(1)}, u32[]{:S(2)}) copy-start(bf16[8,32,192]{2,1,0:T(8,128)(2,1)S(1)} %collective-permute-done.1.args_8_) | copy-start | bytes 294916
  15.1 3.7 %copy-start.7 = (bf16[8,32,192]{2,1,0:T(8,128)(2,1)}, bf16[8,32,192]{2,1,0:T(8,128)(2,1)S(1)}, u32[]{:S(2)}) copy-start(bf16[8,32,192]{2,1,0:T(8,128)(2,1)S(1)} %collective-permute-done.2.args_9_) | copy-start | bytes 294916
  18.8 0.7 copy-start.8
  56.6 4.4 %collective-permute-start.7 = (bf16[80,1024]{1,0:T(8,128)(2,1)}, bf16[80,1024]{1,0:T(8,128)(2,1)S(1)}, u32[]{:S(2)}, u32[]{:S(2)}) collective-permute-start(bf16[80,1024]{1,0:T(8,128)(2,1)} %combine.1.args_0_), channel_id=1, source_target_pairs={{0,96},{16,112},{32,0},{48,16},{64,32},{80,48},{96,64},{112,80},{1... | collective-permute-start | bytes 491528 | tf_op jit(solution)/shard_map/ppermute | solution.py:307
  57.4 5.9 %collective-permute-start.6 = (bf16[80,1024]{1,0:T(8,128)(2,1)}, bf16[80,1024]{1,0:T(8,128)(2,1)S(1)}, u32[]{:S(2)}, u32[]{:S(2)}) collective-permute-start(bf16[80,1024]{1,0:T(8,128)(2,1)} %combine.1.args_0_), channel_id=1, source_target_pairs={{0,64},{16,80},{32,96},{48,112},{64,0},{80,16},{96,32},{112,48},{1... | collective-permute-start | bytes 491528 | tf_op jit(solution)/shard_map/ppermute | solution.py:307
  59.4 5.7 %collective-permute-start.5 = (bf16[80,1024]{1,0:T(8,128)(2,1)}, bf16[80,1024]{1,0:T(8,128)(2,1)S(1)}, u32[]{:S(2)}, u32[]{:S(2)}) collective-permute-start(bf16[80,1024]{1,0:T(8,128)(2,1)} %combine.1.args_0_), channel_id=1, source_target_pairs={{0,32},{16,48},{32,64},{48,80},{64,96},{80,112},{96,0},{112,16},{1... | collective-permute-start | bytes 491528 | tf_op jit(solution)/shard_map/ppermute | solution.py:307
  61.0 12.2 %copy-start = (bf16[80,1024]{1,0:T(8,128)(2,1)}, bf16[80,1024]{1,0:T(8,128)(2,1)S(1)}, u32[]{:S(2)}) copy-start(bf16[80,1024]{1,0:T(8,128)(2,1)S(1)} %collective-permute-done.7.args_4_) | copy-start | bytes 491524
  63.3 9.9 %copy-start.1 = (bf16[80,1024]{1,0:T(8,128)(2,1)}, bf16[80,1024]{1,0:T(8,128)(2,1)S(1)}, u32[]{:S(2)}) copy-start(bf16[80,1024]{1,0:T(8,128)(2,1)S(1)} %collective-permute-done.6.args_3_) | copy-start | bytes 491524
  65.1 8.1 %copy-start.2 = (bf16[80,1024]{1,0:T(8,128)(2,1)}, bf16[80,1024]{1,0:T(8,128)(2,1)S(1)}, u32[]{:S(2)}) copy-start(bf16[80,1024]{1,0:T(8,128)(2,1)S(1)} %collective-permute-done.5.args_2_) | copy-start | bytes 491524
  65.1 8.0 %collective-permute-start.8 = (bf16[3,80,1024]{2,1,0:T(8,128)(2,1)S(1)}, bf16[3,80,1024]{2,1,0:T(8,128)(2,1)S(1)}, u32[]{:S(2)}, u32[]{:S(2)}) collective-permute-start(bf16[3,80,1024]{2,1,0:T(8,128)(2,1)S(1)} %pad_maximum_fusion), channel_id=1, source_target_pairs={{0,16},{16,0},{32,48},{48,32},{64,80},{80,64},{96,112},{112,96},{1... | collective-permute-start | bytes 1474568 | tf_op jit(solution)/shard_map/ppermute | solution.py:309
  71.2 1.9 %collective-permute-start.4 = (bf16[80,1024]{1,0:T(8,128)(2,1)}, bf16[80,1024]{1,0:T(8,128)(2,1)S(1)}, u32[]{:S(2)}, u32[]{:S(2)}) collective-permute-start(bf16[80,1024]{1,0:T(8,128)(2,1)} %combine.1.args_0_), channel_id=1, source_target_pairs={{0,16},{16,0},{32,48},{48,32},{64,80},{80,64},{96,112},{112,96},{1... | collective-permute-start | bytes 491528 | tf_op jit(solution)/shard_map/ppermute | solution.py:308
  73.2 0.7 copy-start.4
  73.8 0.8 %copy-start.3 = (bf16[3,80,1024]{2,1,0:T(8,128)(2,1)}, bf16[3,80,1024]{2,1,0:T(8,128)(2,1)S(1)}, u32[]{:S(2)}) copy-start(bf16[3,80,1024]{2,1,0:T(8,128)(2,1)S(1)} %collective-permute-done.8.args_5_) | copy-start | bytes 1474564

commit v3 on v2

--- a/solution.py
+++ b/solution.py
@@ -10,6 +10,9 @@
 BLOCKS = 7
 LANES = 128
 HALO = 8
+WINDOW = 8
+SAME = 256
+APART = 512
 F32 = jnp.float32
 BF16 = jnp.bfloat16
 SMEM = pltpu.MemorySpace.SMEM
@@ -20,8 +23,7 @@
     return lax.axis_index("grp") * n_dev + lax.axis_index("dev")
 
 
-def pack_kernel(n_dev, nbr_ref, p_ref, *refs):
-    outs, bufs = refs[:4], refs[4:]
+def pack_kernel(n_dev, nbr_ref, p_ref, *outs):
     e_dev = p_ref.shape[0]
     shift = e_dev.bit_length() - 1
     device = position(n_dev)
@@ -35,97 +37,96 @@
         block = p_ref[e]
         new = []
         for d in range(4):
-            bufs[d][jnp.minimum(counts[d], HALO)] = block
+            outs[d][jnp.minimum(counts[d], HALO)] = block
             new.append(counts[d] + hits[d].astype(jnp.int32))
         return tuple(new)
 
     lax.fori_loop(0, e_dev, step, (jnp.int32(0),) * 4, unroll=4)
-    for d in range(4):
-        outs[d][...] = bufs[d][0:HALO]
-
-
-def main_kernel(n_dev, rows_own, slot_ref, nbr_ref, nagg_ref, crow_ref, touch_ref, a_hbm, p_ref, h0, h1, h2, h3,
-                out_ref, abuf, pool, acc, lefts0, lefts1, seen, place, a_sems, h_sems):
-    e_dev, width_c, _ = p_ref.shape
+
+
+def route_kernel(n_dev, rows_own, slot_ref, nbr_ref, nagg_ref, touch_ref, crow_ref, out_ref):
+    e_dev = slot_ref.shape[1]
     shift = e_dev.bit_length() - 1
     device = position(n_dev)
+    nbr = nbr_ref[...]
+    home = lax.shift_right_arithmetic(nbr, shift)
+    local = nbr & (e_dev - 1)
+    side = jnp.full(nbr.shape, 4, jnp.int32)
+    for d, h in enumerate((device - n_dev, device + n_dev, device - 1, device + 1)):
+        side = jnp.where(home == h, d, side)
+    slot = slot_ref[...]
+    own = jnp.zeros_like(slot)
+    for t in range(TOUCH):
+        own = jnp.where(slot == t, touch_ref[t, device], own)
+    mode = jnp.where(nbr < 0, 0, jnp.where(nagg_ref[...] == own, SAME, APART))
+    row = lax.broadcasted_iota(jnp.int32, (e_dev, e_dev), 0)
+    seen = []
+    for d in range(4):
+        hit = jnp.zeros((e_dev, e_dev), F32)
+        for f in range(FACES):
+            hit = jnp.where((side[f : f + 1] == d) & (local[f : f + 1] == row), 1.0, hit)
+        seen.append(jnp.max(hit, axis=1, keepdims=True))
+    for f in range(FACES):
+        there = jnp.zeros((e_dev, e_dev), F32)
+        for d in range(4):
+            there = jnp.where(side[f : f + 1] == d, seen[d], there)
+        before = jnp.sum(jnp.where(row < local[f : f + 1], there, 0.0), axis=0, keepdims=True).astype(jnp.int32)
+        halo = e_dev + HALO * side[f : f + 1] + jnp.minimum(before, HALO - 1)
+        out_ref[f : f + 1, 0:e_dev] = jnp.where(side[f : f + 1] < 4, halo, local[f : f + 1]) + mode[f : f + 1]
+    out_ref[FACES : FACES + 1, 0:e_dev] = slot
+    lane = lax.broadcasted_iota(jnp.int32, (1, LANES), 1)
+    rows = jnp.zeros((1, LANES), jnp.int32)
+    for t in range(TOUCH):
+        row = crow_ref[touch_ref[t, device]]
+        owner = row // rows_own
+        rows = jnp.where(lane == t, owner, jnp.where(lane == 8 + t, row - owner * rows_own + 1, rows))
+    out_ref[FACES + 1 : FACES + 2] = rows
+
+
+def main_kernel(route_ref, a_hbm, p_hbm, h0, h1, h2, h3,
+                out_ref, abuf, pool, acc, lefts0, lefts1, a_sems, h_sems):
+    e_dev, width_c, _ = p_hbm.shape
 
     def fetch(e):
         return pltpu.make_async_copy(a_hbm.at[e], abuf.at[e], a_sems.at[e])
 
-    for e in range(e_dev):
-        fetch(e).start()
+    own_copy = pltpu.make_async_copy(p_hbm, pool.at[pl.ds(0, e_dev)], h_sems.at[4])
+    own_copy.start()
     halos = [
-        pltpu.make_async_copy(h, pool.at[pl.ds(e_dev + HALO * d, HALO)], h_sems.at[d])
+        pltpu.make_async_copy(h.at[pl.ds(0, HALO)], pool.at[pl.ds(e_dev + HALO * d, HALO)], h_sems.at[d])
         for d, h in enumerate((h0, h1, h2, h3))
     ]
     for copy in halos:
         copy.start()
+    for e in range(WINDOW):
+        fetch(e).start()
     acc[...] = jnp.zeros_like(acc)
     out_ref[...] = jnp.zeros_like(out_ref)
-    pool[0:e_dev] = p_ref[...]
-
-    def clear(i, c):
-        seen[i] = 0
-        return c
-
-    lax.fori_loop(0, 5 * e_dev, clear, 0, unroll=8)
-    homes = (device - n_dev, device + n_dev, device - 1, device + 1)
-
-    def side_of(n):
-        home = lax.shift_right_arithmetic(n, shift)
-        side = jnp.int32(4)
-        for d, h in enumerate(homes):
-            side = jnp.where(home == h, d, side)
-        return side
-
-    def mark(e, c):
-        for f in range(FACES):
-            n = nbr_ref[f, e]
-            seen[side_of(n) * e_dev + (n & (e_dev - 1))] = 1
-        return c
-
-    lax.fori_loop(0, e_dev, mark, 0, unroll=2)
-
-    def order(i, counts):
-        new = []
-        for d in range(4):
-            at = d * e_dev + i
-            hit = seen[at]
-            place[at] = e_dev + HALO * d + jnp.minimum(counts[d], HALO - 1)
-            new.append(counts[d] + hit)
-        place[4 * e_dev + i] = i
-        return tuple(new)
-
-    lax.fori_loop(0, e_dev, order, (jnp.int32(0),) * 4, unroll=2)
+    own_copy.wait()
     for copy in halos:
         copy.wait()
 
     def make_lefts(e, lefts):
-        left = p_ref[e]
+        left = pool[e]
         for k in range(BLOCKS):
             lefts[k] = jnp.dot(left, abuf[e, k], preferred_element_type=F32).astype(BF16)
 
     def add_products(e, lefts):
-        slot = slot_ref[e]
-        own = touch_ref[slot, device]
+        slot = route_ref[FACES, e]
         total = None
         for k in range(BLOCKS):
             if k == 0:
-                right = p_ref[e]
+                right = pool[e]
             else:
-                n = nbr_ref[k - 1, e]
-                right = pool[place[side_of(n) * e_dev + (n & (e_dev - 1))]]
+                route = route_ref[k - 1, e]
+                right = pool[route & (SAME - 1)]
             prod = lax.dot_general(lefts[k], right, (((1,), (1,)), ((), ())), preferred_element_type=F32)
             if k == 0:
                 total = prod
                 continue
-            valid = n >= 0
-            same = valid & (nagg_ref[k - 1, e] == own)
-            apart = valid & (nagg_ref[k - 1, e] != own)
-            total = total + jnp.where(same, prod, 0.0)
+            total = total + jnp.where((route & SAME) != 0, prod, 0.0)
             at = pl.multiple_of((slot * 8 + k) * width_c, width_c)
-            acc[pl.ds(at, width_c), 0:width_c] += jnp.where(apart, prod, 0.0)
+            acc[pl.ds(at, width_c), 0:width_c] += jnp.where((route & APART) != 0, prod, 0.0)
         at = pl.multiple_of(slot * 8 * width_c, width_c)
         acc[pl.ds(at, width_c), 0:width_c] += total
 
@@ -134,6 +135,12 @@
 
     def two(i, c):
         e = 2 * i + 1
+        for ahead in range(2):
+
+            @pl.when(e + ahead + WINDOW - 1 < e_dev)
+            def _():
+                fetch(e + ahead + WINDOW - 1).start()
+
         fetch(e).wait()
         fetch(e + 1).wait()
         add_products(e - 1, lefts0)
@@ -152,9 +159,8 @@
     sub = lax.broadcasted_iota(jnp.int32, (8, LANES), 0)
     per = LANES // width_c
     for t in range(TOUCH):
-        row = crow_ref[touch_ref[t, device]]
-        owner = row // rows_own
-        code = (row - owner * rows_own + 1).astype(F32)
+        owner = route_ref[FACES + 1, t]
+        code = route_ref[FACES + 1, 8 + t].astype(F32)
         for j in range(width_c // per):
             value = None
             for i in range(per):
@@ -256,42 +262,47 @@
     smem = pl.BlockSpec(memory_space=SMEM)
     vmem = pl.BlockSpec(memory_space=VMEM)
     hbm = pl.BlockSpec(memory_space=pl.ANY)
-    params = pltpu.CompilerParams(vmem_limit_bytes=56 << 20)
+
+    def params(mib):
+        return pltpu.CompilerParams(vmem_limit_bytes=mib << 20)
 
     def pack(*args):
         return pack_kernel(n_dev, *args)
 
-    halo_shape = jax.ShapeDtypeStruct((HALO, width_c, width_b), BF16)
+    halo_shape = jax.ShapeDtypeStruct((HALO + 1, width_c, width_b), BF16)
     packed = pl.pallas_call(
         pack, out_shape=(halo_shape,) * 4, in_specs=[smem, vmem], out_specs=(vmem,) * 4,
-        scratch_shapes=[pltpu.VMEM((HALO + 1, width_c, width_b), BF16)] * 4, compiler_params=params, name="pack",
+        compiler_params=params(56), name="pack",
     )(nbr.T, prolong_t)
-    up = lambda size: [(i, i + 1) for i in range(size - 1)]
-    down = lambda size: [(i + 1, i) for i in range(size - 1)]
+    up = lambda size: [(i, (i + 1) % size) for i in range(size)]
+    down = lambda size: [((i + 1) % size, i) for i in range(size)]
     from_low = lax.ppermute(packed[1], "grp", up(n_grp))
     from_high = lax.ppermute(packed[0], "grp", down(n_grp))
     from_left = lax.ppermute(packed[3], "dev", up(n_dev))
     from_right = lax.ppermute(packed[2], "dev", down(n_dev))
 
-    def main(*args):
-        return main_kernel(n_dev, rows_own, *args)
+    def route(*args):
+        return route_kernel(n_dev, rows_own, *args)
+
+    routes = pl.pallas_call(
+        route, out_shape=jax.ShapeDtypeStruct((8, LANES), jnp.int32), in_specs=[vmem] * 3 + [smem] * 2, out_specs=vmem,
+        name="routes",
+    )(elem_slot.reshape(1, e_dev), nbr.T, nbr_agg.T, touch_agg.T, coarse_row)
 
     outgoing = pl.pallas_call(
-        main, out_shape=jax.ShapeDtypeStruct((n_dev, 8, width), BF16),
-        in_specs=[smem] * 5 + [hbm, vmem] + [hbm] * 4, out_specs=vmem,
+        main_kernel, out_shape=jax.ShapeDtypeStruct((n_dev, 8, width), BF16),
+        in_specs=[smem] + [hbm] * 6, out_specs=vmem,
         scratch_shapes=[
             pltpu.VMEM((e_dev, BLOCKS, width_b, width_b), BF16),
             pltpu.VMEM((e_dev + 4 * HALO, width_c, width_b), BF16),
             pltpu.VMEM((TOUCH * 8 * width_c, LANES), F32),
             pltpu.VMEM((BLOCKS, width_c, width_b), BF16),
             pltpu.VMEM((BLOCKS, width_c, width_b), BF16),
-            pltpu.SMEM((5 * e_dev,), jnp.int32),
-            pltpu.SMEM((5 * e_dev,), jnp.int32),
             pltpu.SemaphoreType.DMA((e_dev,)),
-            pltpu.SemaphoreType.DMA((4,)),
+            pltpu.SemaphoreType.DMA((5,)),
         ],
-        compiler_params=params, name="products",
-    )(elem_slot, nbr.T, nbr_agg.T, coarse_row, touch_agg.T, a_blocks, prolong_t, from_low, from_high, from_left, from_right)
+        compiler_params=params(56), name="products",
+    )(routes, a_blocks, prolong_t, from_low, from_high, from_left, from_right)
     incoming = lax.all_to_all(outgoing, "dev", split_axis=0, concat_axis=0, tiled=True)
     piece = 8 * ((BLOCKS * group_rows) // 8 + 1)
 
@@ -301,13 +312,13 @@
     mine = pl.pallas_call(
         combine, out_shape=jax.ShapeDtypeStruct((piece, width), BF16), in_specs=[vmem], out_specs=vmem,
         scratch_shapes=[pltpu.SMEM((rows_own + 1,), jnp.int32), pltpu.SMEM((group_rows + 1,), jnp.int32)],
-        compiler_params=params, name="combine",
+        compiler_params=params(8), name="combine",
     )(incoming.reshape(n_dev * 8, width))
     swap = [(i, i ^ 1) for i in range(n_grp)]
     across = [lax.ppermute(mine, "grp", [(i, (i + 2 * k) % n_grp) for i in range(n_grp)]) for k in range(1, n_grp // 2)]
     twin = lax.ppermute(mine, "grp", swap)
-    others = lax.ppermute(jnp.stack(across), "grp", swap)
-    pieces = (mine, twin, *across, others)
+    others = [lax.ppermute(part, "grp", swap) for part in across]
+    pieces = (mine, twin, *across, *others)
 
     def scatter(*args):
         return scatter_kernel(rows_own, group_rows, *args)
@@ -322,7 +333,7 @@
             pltpu.SemaphoreType.DMA((n_grp,)),
             pltpu.SemaphoreType.DMA((4,)),
         ],
-        compiler_params=params, name="scatter",
+        compiler_params=params(16), name="scatter",
     )(*pieces)
     return jnp.swapaxes(out.reshape(BLOCKS, rows_own, width), 0, 1)
 

time: 78.7 us -> 62.4 us (0.79)
  waiting for transfers between devices: 11.7 us -> 2.11 us
  Pallas kernels: 26.4 us -> 22 us
  blocking collectives: 17.4 us -> 13.1 us
  starting transfers between devices: 20.6 us -> 23.6 us
  local copies, waits for them, and re-layouts: 2.12 us -> 1.3 us
    ppermute x3, waiting for transfers between devices: 5.29 us -> 0.01 us  [on_device(): lax.ppermute(mine, 'grp', [(i, (i + 2 * k) % n_grp) for i in range(n_grp)])]
    all_to_all x1, blocking collectives: 17.4 us -> 13.1 us  [on_device(): lax.all_to_all(outgoing, 'dev', split_axis=0, concat_axis=0, tiled=True)]
    ppermute x1, waiting for transfers between devices: 3.68 us -> 0.01 us  [on_device(): from_right = lax.ppermute(packed[2], 'dev', down(n_dev))]
    ppermute x1, starting transfers between devices: 0.09 us -> 3.65 us  [on_device(): twin = lax.ppermute(mine, 'grp', swap)]
    pallas_call x1 -> x2, Pallas kernels: 17.8 us -> 14.7 us  [the longest x1 13 us: on_device(): pl.pallas_call(main_kernel, out_shape=jax.ShapeDtypeStruct((n_dev, 8, wid...]
    ppermute x1, starting transfers between devices: 1.29 us -> 3.72 us  [on_device(): from_right = lax.ppermute(packed[2], 'dev', down(n_dev))]
    ppermute x3, starting transfers between devices: 3.18 us -> 5.12 us  [on_device(): lax.ppermute(mine, 'grp', [(i, (i + 2 * k) % n_grp) for i in range(n_grp)])]
    ppermute x1, starting transfers between devices: 1.92 us -> 0.01 us  [on_device(): from_high = lax.ppermute(packed[0], 'grp', down(n_grp))]
  transfers between devices with their start and end apart: 9 -> 11, of which waited for: 7 -> 2; matrix products, arithmetic and copies ran while one was open for 0% -> 0% of each run, Pallas kernels for 0% -> 3%
where the time goes in v3:
time: 62.4 us; the launch traced here: 62.1 us
  starting transfers between devices  23.6 us (38%)
  Pallas kernels  22 us (35%)
  blocking collectives  13.1 us (21%)
  waiting for transfers between devices  2.11 us (3%)
  local copies, waits for them, and re-layouts  1.3 us (2%)
    all_to_all x1, blocking collectives, on_device(): lax.all_to_all(outgoing, 'dev', split_axis=0, concat_axis=0, tiled=True)  13.1 us
    pallas_call x1, Pallas kernels, on_device(): pl.pallas_call(main_kernel, out_shape=jax.ShapeDtypeStruct((n_dev, 8, wid...  13 us
    ppermute x3, starting transfers between devices, on_device(): others = [lax.ppermute(part, 'grp', swap) for part in across]  6.87 us
    ppermute x3, starting transfers between devices, on_device(): lax.ppermute(mine, 'grp', [(i, (i + 2 * k) % n_grp) for i in range(n_grp)])  5.12 us
    pallas_call x1, Pallas kernels, on_device(): pl.pallas_call(scatter, out_shape=jax.ShapeDtypeStruct((BLOCKS * rows_own...  4.08 us
    ppermute x1, starting transfers between devices, on_device(): from_right = lax.ppermute(packed[2], 'dev', down(n_dev))  3.72 us
    ppermute x1, starting transfers between devices, on_device(): twin = lax.ppermute(mine, 'grp', swap)  3.65 us
    ppermute x1, starting transfers between devices, on_device(): from_low = lax.ppermute(packed[1], 'grp', up(n_grp))  3.03 us
  transfers between devices with their start and end apart: 11, of which 2 were waited for; matrix products, arithmetic and copies ran while one was open for 0% of the time, Pallas kernels for 3%

profile of v3, /device:TPU:1, one launch (start us, length us, event | category | flops | bytes accessed | tf_op | source)
XLA Modules:
  0.0 62.1 jit_solution(3030406253709632299)
XLA Ops:
  0.0 2.9 %pack.1 = (bf16[9,32,192]{2,1,0:T(8,128)(2,1)}, bf16[9,32,192]{2,1,0:T(8,128)(2,1)}, bf16[9,32,192]{2,1,0:T(8,128)(2,1)}, bf16[9,32,192]{2,1,0:T(8,128)(2,1)}) custom-call(s32[6,32]{1,0:T(8,128)} %bitcast.9, bf16[32,32,192]{2,1,0:T(8,128)(2,1)} %p_hbm.1), custom_call_target="tpu_custom_call" | custom-call | tf_op jit(solution)/shard_map/pack/pallas_call | solution.py:273
  2.9 3.0 %collective-permute-start = (bf16[9,32,192]{2,1,0:T(8,128)(2,1)}, bf16[9,32,192]{2,1,0:T(8,128)(2,1)S(1)}, u32[]{:S(2)}, u32[]{:S(2)}) collective-permute-start(bf16[9,32,192]{2,1,0:T(8,128)(2,1)} %get-tuple-element.9), channel_id=1, source_target_pairs={{0,16},{16,32},{32,48},{48,64},{64,80},{80,96},{96,112},{112,0},{1... | collective-permute-start | bytes 331784 | tf_op jit(solution)/shard_map/ppermute | solution.py:279
  5.9 0.0 collective-permute-start.1
  5.9 1.2 %collective-permute-start.2 = (bf16[9,32,192]{2,1,0:T(8,128)(2,1)}, bf16[9,32,192]{2,1,0:T(8,128)(2,1)S(1)}, u32[]{:S(2)}, u32[]{:S(2)}) collective-permute-start(bf16[9,32,192]{2,1,0:T(8,128)(2,1)} %get-tuple-element.11), channel_id=1, source_target_pairs={{0,1},{1,2},{2,3},{3,4},{4,5},{5,6},{6,7},{7,8},{8,9},{9,10},{10,1... | collective-permute-start | bytes 331784 | tf_op jit(solution)/shard_map/ppermute | solution.py:281
  7.1 3.7 %collective-permute-start.3 = (bf16[9,32,192]{2,1,0:T(8,128)(2,1)}, bf16[9,32,192]{2,1,0:T(8,128)(2,1)S(1)}, u32[]{:S(2)}, u32[]{:S(2)}) collective-permute-start(bf16[9,32,192]{2,1,0:T(8,128)(2,1)} %get-tuple-element.12), channel_id=1, source_target_pairs={{1,0},{2,1},{3,2},{4,3},{5,4},{6,5},{7,6},{8,7},{9,8},{10,9},{11,1... | collective-permute-start | bytes 331784 | tf_op jit(solution)/shard_map/ppermute | solution.py:282
  10.9 1.6 %routes.1.route_ref = s32[8,128]{1,0:T(8,128)} custom-call(s32[1,32]{1,0:T(1,128)} %bitcast.13, s32[6,32]{1,0:T(8,128)} %bitcast.10, s32[6,32]{1,0:T(8,128)} %bitcast.11, s32[6,128]{1,0:T(8,128)} %bitcast.12, s32[528]{0:T(1024)} %args_4_.4), custom_call_target="tpu_custom_call" | custom-call | tf_op jit(solution)/shard_map/routes/pallas_call | solution.py:287
  12.5 0.0 collective-permute-done.h0
  12.5 0.0 copy-start
  12.5 0.0 collective-permute-done.1.h1
  12.5 0.0 copy-start.1
  12.5 1.1 %collective-permute-done.2.h2 = bf16[9,32,192]{2,1,0:T(8,128)(2,1)S(1)} collective-permute-done((bf16[9,32,192]{2,1,0:T(8,128)(2,1)}, bf16[9,32,192]{2,1,0:T(8,128)(2,1)S(1)}, u32[]{:S(2)}, u32[]{:S(2)}) %collective-permute-start.2) | collective-permute-done | bytes 110624 | tf_op jit(solution)/shard_map/ppermute | solution.py:281
  13.6 0.0 copy-start.2
  13.6 0.0 collective-permute-done.3.h3
  13.6 0.0 copy-done
  13.6 0.0 copy-done.1
  13.6 0.6 %copy-done.2 = bf16[9,32,192]{2,1,0:T(8,128)(2,1)} copy-done((bf16[9,32,192]{2,1,0:T(8,128)(2,1)}, bf16[9,32,192]{2,1,0:T(8,128)(2,1)S(1)}, u32[]{:S(2)}) %copy-start.2) | copy-done | bytes 110616
  14.3 0.0 copy-start.3
  14.3 0.7 %copy-done.3 = bf16[9,32,192]{2,1,0:T(8,128)(2,1)} copy-done((bf16[9,32,192]{2,1,0:T(8,128)(2,1)}, bf16[9,32,192]{2,1,0:T(8,128)(2,1)S(1)}, u32[]{:S(2)}) %copy-start.3) | copy-done | bytes 110616
  14.9 13.0 %products.1 = bf16[16,8,1024]{2,1,0:T(8,128)(2,1)} custom-call(s32[8,128]{1,0:T(8,128)} %routes.1.route_ref, bf16[32,7,192,192]{3,2,1,0:T(8,128)(2,1)} %a_hbm.1, bf16[32,32,192]{2,1,0:T(8,128)(2,1)} %p_hbm.1, bf16[9,32,192]{2,1,0:T(8,128)(2,1)} %copy-done, bf16[9,32,192]{2,1,0:T(8,128)(2,1)} %copy-done.1, bf16[9,32,192]{2,1,0:T(8,128)(2,1)} %copy-done.2, ...), custom_call_target="tpu_custom_call" | custom-call | tf_op jit(solution)/shard_map/products/pallas_call | solution.py:292
  27.9 13.1 %all_to_all.5 = bf16[16,8,1024]{2,1,0:T(8,128)(2,1)S(1)} all-to-all(bf16[16,8,1024]{2,1,0:T(8,128)(2,1)} %products.1), channel_id=1, replica_groups=mesh['grp'=8,'dev'=16] {'dev'}, dimensions={0} | all-to-all | bytes 524288 | tf_op jit(solution)/shard_map/all_to_all | solution.py:306
  41.0 0.3 combine.1.args_0_
  41.3 2.3 %collective-permute-start.7 = (bf16[80,1024]{1,0:T(8,128)(2,1)S(1)}, bf16[80,1024]{1,0:T(8,128)(2,1)S(1)}, u32[]{:S(2)}, u32[]{:S(2)}) collective-permute-start(bf16[80,1024]{1,0:T(8,128)(2,1)S(1)} %combine.1.args_0_), channel_id=1, source_target_pairs={{0,96},{16,112},{32,0},{48,16},{64,32},{80,48},{96,64},{112,80},{1... | collective-permute-start | bytes 491528 | tf_op jit(solution)/shard_map/ppermute | solution.py:318
  43.6 2.3 %collective-permute-start.6 = (bf16[80,1024]{1,0:T(8,128)(2,1)S(1)}, bf16[80,1024]{1,0:T(8,128)(2,1)S(1)}, u32[]{:S(2)}, u32[]{:S(2)}) collective-permute-start(bf16[80,1024]{1,0:T(8,128)(2,1)S(1)} %combine.1.args_0_), channel_id=1, source_target_pairs={{0,64},{16,80},{32,96},{48,112},{64,0},{80,16},{96,32},{112,48},{1... | collective-permute-start | bytes 491528 | tf_op jit(solution)/shard_map/ppermute | solution.py:318
  45.9 0.5 collective-permute-start.5
  46.5 3.6 %collective-permute-start.4 = (bf16[80,1024]{1,0:T(8,128)(2,1)S(1)}, bf16[80,1024]{1,0:T(8,128)(2,1)S(1)}, u32[]{:S(2)}, u32[]{:S(2)}) collective-permute-start(bf16[80,1024]{1,0:T(8,128)(2,1)S(1)} %combine.1.args_0_), channel_id=1, source_target_pairs={{0,16},{16,0},{32,48},{48,32},{64,80},{80,64},{96,112},{112,96},{1... | collective-permute-start | bytes 491528 | tf_op jit(solution)/shard_map/ppermute | solution.py:319
  50.1 0.0 collective-permute-done.7.args_4_
  50.1 2.9 %collective-permute-start.10 = (bf16[80,1024]{1,0:T(8,128)(2,1)S(1)}, bf16[80,1024]{1,0:T(8,128)(2,1)S(1)}, u32[]{:S(2)}, u32[]{:S(2)}) collective-permute-start(bf16[80,1024]{1,0:T(8,128)(2,1)S(1)} %collective-permute-done.7.args_4_), channel_id=1, source_target_pairs={{0,16},{16,0},{32,48},{48,32},{64,80},{80,64},{96,112},{112,96},{1... | collective-permute-start | bytes 491528 | tf_op jit(solution)/shard_map/ppermute | solution.py:320
  53.0 0.0 collective-permute-done.6.args_3_
  53.0 2.3 %collective-permute-start.9 = (bf16[80,1024]{1,0:T(8,128)(2,1)S(1)}, bf16[80,1024]{1,0:T(8,128)(2,1)S(1)}, u32[]{:S(2)}, u32[]{:S(2)}) collective-permute-start(bf16[80,1024]{1,0:T(8,128)(2,1)S(1)} %collective-permute-done.6.args_3_), channel_id=1, source_target_pairs={{0,16},{16,0},{32,48},{48,32},{64,80},{80,64},{96,112},{112,96},{1... | collective-permute-start | bytes 491528 | tf_op jit(solution)/shard_map/ppermute | solution.py:320
  55.3 0.0 collective-permute-done.5.args_2_
  55.3 1.6 %collective-permute-start.8 = (bf16[80,1024]{1,0:T(8,128)(2,1)S(1)}, bf16[80,1024]{1,0:T(8,128)(2,1)S(1)}, u32[]{:S(2)}, u32[]{:S(2)}) collective-permute-start(bf16[80,1024]{1,0:T(8,128)(2,1)S(1)} %collective-permute-done.5.args_2_), channel_id=1, source_target_pairs={{0,16},{16,0},{32,48},{48,32},{64,80},{80,64},{96,112},{112,96},{1... | collective-permute-start | bytes 491528 | tf_op jit(solution)/shard_map/ppermute | solution.py:320
  57.0 0.0 collective-permute-done.4.args_1_
  57.0 0.0 collective-permute-done.10.args_7_
  57.0 0.0 collective-permute-done.9.args_6_
  57.0 1.0 %collective-permute-done.8.args_5_ = bf16[80,1024]{1,0:T(8,128)(2,1)S(1)} collective-permute-done((bf16[80,1024]{1,0:T(8,128)(2,1)S(1)}, bf16[80,1024]{1,0:T(8,128)(2,1)S(1)}, u32[]{:S(2)}, u32[]{:S(2)}) %collective-permute-start.8) | collective-permute-done | bytes 163872 | tf_op jit(solution)/shard_map/ppermute | solution.py:320
  58.0 4.1 %scatter.1 = f32[616,1024]{1,0:T(8,128)} custom-call(bf16[80,1024]{1,0:T(8,128)(2,1)S(1)} %combine.1.args_0_, bf16[80,1024]{1,0:T(8,128)(2,1)S(1)} %collective-permute-done.4.args_1_, bf16[80,1024]{1,0:T(8,128)(2,1)S(1)} %collective-permute-done.5.args_2_, bf16[80,1024]{1,0:T(8,128)(2,1)S(1)} %collective-permute-done.6.args_3_, ...), custom_call_target="tpu_custom_call" | custom-call | tf_op jit(solution)/shard_map/scatter/pallas_call | solution.py:326
Async XLA Ops:
  2.9 9.6 %collective-permute-start = (bf16[9,32,192]{2,1,0:T(8,128)(2,1)}, bf16[9,32,192]{2,1,0:T(8,128)(2,1)S(1)}, u32[]{:S(2)}, u32[]{:S(2)}) collective-permute-start(bf16[9,32,192]{2,1,0:T(8,128)(2,1)} %get-tuple-element.9), channel_id=1, source_target_pairs={{0,16},{16,32},{32,48},{48,64},{64,80},{80,96},{96,112},{112,0},{1... | collective-permute-start | bytes 331784 | tf_op jit(solution)/shard_map/ppermute | solution.py:279
  5.9 6.6 %collective-permute-start.1 = (bf16[9,32,192]{2,1,0:T(8,128)(2,1)}, bf16[9,32,192]{2,1,0:T(8,128)(2,1)S(1)}, u32[]{:S(2)}, u32[]{:S(2)}) collective-permute-start(bf16[9,32,192]{2,1,0:T(8,128)(2,1)} %get-tuple-element.10), channel_id=1, source_target_pairs={{16,0},{32,16},{48,32},{64,48},{80,64},{96,80},{112,96},{0,112},{1... | collective-permute-start | bytes 331784 | tf_op jit(solution)/shard_map/ppermute | solution.py:280
  5.9 7.7 %collective-permute-start.2 = (bf16[9,32,192]{2,1,0:T(8,128)(2,1)}, bf16[9,32,192]{2,1,0:T(8,128)(2,1)S(1)}, u32[]{:S(2)}, u32[]{:S(2)}) collective-permute-start(bf16[9,32,192]{2,1,0:T(8,128)(2,1)} %get-tuple-element.11), channel_id=1, source_target_pairs={{0,1},{1,2},{2,3},{3,4},{4,5},{5,6},{6,7},{7,8},{8,9},{9,10},{10,1... | collective-permute-start | bytes 331784 | tf_op jit(solution)/shard_map/ppermute | solution.py:281
  7.1 6.5 %collective-permute-start.3 = (bf16[9,32,192]{2,1,0:T(8,128)(2,1)}, bf16[9,32,192]{2,1,0:T(8,128)(2,1)S(1)}, u32[]{:S(2)}, u32[]{:S(2)}) collective-permute-start(bf16[9,32,192]{2,1,0:T(8,128)(2,1)} %get-tuple-element.12), channel_id=1, source_target_pairs={{1,0},{2,1},{3,2},{4,3},{5,4},{6,5},{7,6},{8,7},{9,8},{10,9},{11,1... | collective-permute-start | bytes 331784 | tf_op jit(solution)/shard_map/ppermute | solution.py:282
  12.5 1.1 %copy-start = (bf16[9,32,192]{2,1,0:T(8,128)(2,1)}, bf16[9,32,192]{2,1,0:T(8,128)(2,1)S(1)}, u32[]{:S(2)}) copy-start(bf16[9,32,192]{2,1,0:T(8,128)(2,1)S(1)} %collective-permute-done.h0) | copy-start | bytes 331780
  12.5 1.1 %copy-start.1 = (bf16[9,32,192]{2,1,0:T(8,128)(2,1)}, bf16[9,32,192]{2,1,0:T(8,128)(2,1)S(1)}, u32[]{:S(2)}) copy-start(bf16[9,32,192]{2,1,0:T(8,128)(2,1)S(1)} %collective-permute-done.1.h1) | copy-start | bytes 331780
  13.6 0.6 %copy-start.2 = (bf16[9,32,192]{2,1,0:T(8,128)(2,1)}, bf16[9,32,192]{2,1,0:T(8,128)(2,1)S(1)}, u32[]{:S(2)}) copy-start(bf16[9,32,192]{2,1,0:T(8,128)(2,1)S(1)} %collective-permute-done.2.h2) | copy-start | bytes 331780
  14.3 0.7 %copy-start.3 = (bf16[9,32,192]{2,1,0:T(8,128)(2,1)}, bf16[9,32,192]{2,1,0:T(8,128)(2,1)S(1)}, u32[]{:S(2)}) copy-start(bf16[9,32,192]{2,1,0:T(8,128)(2,1)S(1)} %collective-permute-done.3.h3) | copy-start | bytes 331780
  41.3 8.8 %collective-permute-start.7 = (bf16[80,1024]{1,0:T(8,128)(2,1)S(1)}, bf16[80,1024]{1,0:T(8,128)(2,1)S(1)}, u32[]{:S(2)}, u32[]{:S(2)}) collective-permute-start(bf16[80,1024]{1,0:T(8,128)(2,1)S(1)} %combine.1.args_0_), channel_id=1, source_target_pairs={{0,96},{16,112},{32,0},{48,16},{64,32},{80,48},{96,64},{112,80},{1... | collective-permute-start | bytes 491528 | tf_op jit(solution)/shard_map/ppermute | solution.py:318
  43.6 9.4 %collective-permute-start.6 = (bf16[80,1024]{1,0:T(8,128)(2,1)S(1)}, bf16[80,1024]{1,0:T(8,128)(2,1)S(1)}, u32[]{:S(2)}, u32[]{:S(2)}) collective-permute-start(bf16[80,1024]{1,0:T(8,128)(2,1)S(1)} %combine.1.args_0_), channel_id=1, source_target_pairs={{0,64},{16,80},{32,96},{48,112},{64,0},{80,16},{96,32},{112,48},{1... | collective-permute-start | bytes 491528 | tf_op jit(solution)/shard_map/ppermute | solution.py:318
  45.9 9.4 %collective-permute-start.5 = (bf16[80,1024]{1,0:T(8,128)(2,1)S(1)}, bf16[80,1024]{1,0:T(8,128)(2,1)S(1)}, u32[]{:S(2)}, u32[]{:S(2)}) collective-permute-start(bf16[80,1024]{1,0:T(8,128)(2,1)S(1)} %combine.1.args_0_), channel_id=1, source_target_pairs={{0,32},{16,48},{32,64},{48,80},{64,96},{80,112},{96,0},{112,16},{1... | collective-permute-start | bytes 491528 | tf_op jit(solution)/shard_map/ppermute | solution.py:318
  46.5 10.5 %collective-permute-start.4 = (bf16[80,1024]{1,0:T(8,128)(2,1)S(1)}, bf16[80,1024]{1,0:T(8,128)(2,1)S(1)}, u32[]{:S(2)}, u32[]{:S(2)}) collective-permute-start(bf16[80,1024]{1,0:T(8,128)(2,1)S(1)} %combine.1.args_0_), channel_id=1, source_target_pairs={{0,16},{16,0},{32,48},{48,32},{64,80},{80,64},{96,112},{112,96},{1... | collective-permute-start | bytes 491528 | tf_op jit(solution)/shard_map/ppermute | solution.py:319
  50.1 6.9 %collective-permute-start.10 = (bf16[80,1024]{1,0:T(8,128)(2,1)S(1)}, bf16[80,1024]{1,0:T(8,128)(2,1)S(1)}, u32[]{:S(2)}, u32[]{:S(2)}) collective-permute-start(bf16[80,1024]{1,0:T(8,128)(2,1)S(1)} %collective-permute-done.7.args_4_), channel_id=1, source_target_pairs={{0,16},{16,0},{32,48},{48,32},{64,80},{80,64},{96,112},{112,96},{1... | collective-permute-start | bytes 491528 | tf_op jit(solution)/shard_map/ppermute | solution.py:320
  53.0 4.0 %collective-permute-start.9 = (bf16[80,1024]{1,0:T(8,128)(2,1)S(1)}, bf16[80,1024]{1,0:T(8,128)(2,1)S(1)}, u32[]{:S(2)}, u32[]{:S(2)}) collective-permute-start(bf16[80,1024]{1,0:T(8,128)(2,1)S(1)} %collective-permute-done.6.args_3_), channel_id=1, source_target_pairs={{0,16},{16,0},{32,48},{48,32},{64,80},{80,64},{96,112},{112,96},{1... | collective-permute-start | bytes 491528 | tf_op jit(solution)/shard_map/ppermute | solution.py:320
  55.3 2.7 %collective-permute-start.8 = (bf16[80,1024]{1,0:T(8,128)(2,1)S(1)}, bf16[80,1024]{1,0:T(8,128)(2,1)S(1)}, u32[]{:S(2)}, u32[]{:S(2)}) collective-permute-start(bf16[80,1024]{1,0:T(8,128)(2,1)S(1)} %collective-permute-done.5.args_2_), channel_id=1, source_target_pairs={{0,16},{16,0},{32,48},{48,32},{64,80},{80,64},{96,112},{112,96},{1... | collective-permute-start | bytes 491528 | tf_op jit(solution)/shard_map/ppermute | solution.py:320

commit v4 on v3

--- a/solution.py
+++ b/solution.py
@@ -11,6 +11,7 @@
 LANES = 128
 HALO = 8
 WINDOW = 8
+EARLY = 8
 SAME = 256
 APART = 512
 F32 = jnp.float32
@@ -23,8 +24,23 @@
     return lax.axis_index("grp") * n_dev + lax.axis_index("dev")
 
 
-def pack_kernel(n_dev, nbr_ref, p_ref, *outs):
+def load(pairs):
+    copies = [pltpu.make_async_copy(src, dst, sem) for src, dst, sem in pairs]
+    for copy in copies:
+        copy.start()
+    return copies
+
+
+def pack_kernel(n_dev, nbr_hbm, p_hbm, *refs):
+    outs, nbr_ref, p_ref, sems = refs[:4], *refs[4:]
     e_dev = p_ref.shape[0]
+    quarter = e_dev // 4
+    copies = load(
+        [(nbr_hbm, nbr_ref, sems.at[4])]
+        + [(p_hbm.at[pl.ds(i * quarter, quarter)], p_ref.at[pl.ds(i * quarter, quarter)], sems.at[i]) for i in range(4)]
+    )
+    for copy in copies:
+        copy.wait()
     shift = e_dev.bit_length() - 1
     device = position(n_dev)
     homes = (device - n_dev, device + n_dev, device - 1, device + 1)
@@ -44,10 +60,31 @@
     lax.fori_loop(0, e_dev, step, (jnp.int32(0),) * 4, unroll=4)
 
 
-def route_kernel(n_dev, rows_own, slot_ref, nbr_ref, nagg_ref, touch_ref, crow_ref, out_ref):
+def early_kernel(n_dev, rows_own, slot_hbm, nbr_hbm, nagg_hbm, touch_hbm, crow_hbm, a_hbm, p_hbm, out_ref, lefts,
+                 abuf, pbuf, slot_ref, nbr_ref, nagg_ref, touch_ref, crow_ref, a_sems, p_sem, sems):
+    early = lefts.shape[0]
+    small = load(
+        [
+            (slot_hbm, slot_ref, sems.at[0]),
+            (nbr_hbm, nbr_ref, sems.at[1]),
+            (nagg_hbm, nagg_ref, sems.at[2]),
+            (touch_hbm, touch_ref, sems.at[3]),
+            (crow_hbm, crow_ref, sems.at[4]),
+        ]
+    )
+
+    def fetch(e):
+        return pltpu.make_async_copy(a_hbm.at[e], abuf.at[e], a_sems.at[e])
+
+    p_copy = pltpu.make_async_copy(p_hbm.at[pl.ds(0, early)], pbuf, p_sem)
+    for e in range(early):
+        fetch(e).start()
+    p_copy.start()
     e_dev = slot_ref.shape[1]
     shift = e_dev.bit_length() - 1
     device = position(n_dev)
+    for copy in small:
+        copy.wait()
     nbr = nbr_ref[...]
     home = lax.shift_right_arithmetic(nbr, shift)
     local = nbr & (e_dev - 1)
@@ -81,35 +118,53 @@
         owner = row // rows_own
         rows = jnp.where(lane == t, owner, jnp.where(lane == 8 + t, row - owner * rows_own + 1, rows))
     out_ref[FACES + 1 : FACES + 2] = rows
-
-
-def main_kernel(route_ref, a_hbm, p_hbm, h0, h1, h2, h3,
-                out_ref, abuf, pool, acc, lefts0, lefts1, a_sems, h_sems):
+    p_copy.wait()
+
+    def two(i, c):
+        for e in (2 * i, 2 * i + 1):
+            fetch(e).wait()
+        for e in (2 * i, 2 * i + 1):
+            for k in range(BLOCKS):
+                lefts[e, k] = jnp.dot(pbuf[e], abuf[e, k], preferred_element_type=F32).astype(BF16)
+        return c
+
+    lax.fori_loop(0, early // 2, two, 0)
+
+
+def main_kernel(route_hbm, a_hbm, p_hbm, early_hbm, h0, h1, h2, h3,
+                out_ref, abuf, pool, acc, done, lefts0, lefts1, route_ref, a_sems, h_sems):
     e_dev, width_c, _ = p_hbm.shape
+    early = done.shape[0]
 
     def fetch(e):
-        return pltpu.make_async_copy(a_hbm.at[e], abuf.at[e], a_sems.at[e])
+        return pltpu.make_async_copy(a_hbm.at[e], abuf.at[e - early], a_sems.at[e - early])
 
     own_copy = pltpu.make_async_copy(p_hbm, pool.at[pl.ds(0, e_dev)], h_sems.at[4])
     own_copy.start()
+    route_copy = pltpu.make_async_copy(route_hbm, route_ref, h_sems.at[5])
+    route_copy.start()
+    done_copy = pltpu.make_async_copy(early_hbm, done, h_sems.at[6])
+    done_copy.start()
     halos = [
         pltpu.make_async_copy(h.at[pl.ds(0, HALO)], pool.at[pl.ds(e_dev + HALO * d, HALO)], h_sems.at[d])
         for d, h in enumerate((h0, h1, h2, h3))
     ]
     for copy in halos:
         copy.start()
-    for e in range(WINDOW):
+    for e in range(early, early + WINDOW):
         fetch(e).start()
     acc[...] = jnp.zeros_like(acc)
     out_ref[...] = jnp.zeros_like(out_ref)
     own_copy.wait()
+    route_copy.wait()
+    done_copy.wait()
     for copy in halos:
         copy.wait()
 
     def make_lefts(e, lefts):
         left = pool[e]
         for k in range(BLOCKS):
-            lefts[k] = jnp.dot(left, abuf[e, k], preferred_element_type=F32).astype(BF16)
+            lefts[k] = jnp.dot(left, abuf[e - early, k], preferred_element_type=F32).astype(BF16)
 
     def add_products(e, lefts):
         slot = route_ref[FACES, e]
@@ -130,11 +185,17 @@
         at = pl.multiple_of(slot * 8 * width_c, width_c)
         acc[pl.ds(at, width_c), 0:width_c] += total
 
-    fetch(0).wait()
-    make_lefts(0, lefts0)
+    def ready(i, c):
+        for e in (2 * i, 2 * i + 1):
+            add_products(e, done.at[e])
+        return c
+
+    lax.fori_loop(0, early // 2, ready, 0)
+    fetch(early).wait()
+    make_lefts(early, lefts0)
 
     def two(i, c):
-        e = 2 * i + 1
+        e = early + 2 * i + 1
         for ahead in range(2):
 
             @pl.when(e + ahead + WINDOW - 1 < e_dev)
@@ -149,7 +210,7 @@
         make_lefts(e + 1, lefts0)
         return c
 
-    lax.fori_loop(0, e_dev // 2 - 1, two, 0)
+    lax.fori_loop(0, (e_dev - early) // 2 - 1, two, 0)
     fetch(e_dev - 1).wait()
     make_lefts(e_dev - 1, lefts1)
     add_products(e_dev - 2, lefts0)
@@ -212,24 +273,18 @@
 
 
 def scatter_kernel(rows_own, group_rows, *refs):
-    ins, out_hbm, held, chosen, out_buf, in_sems, out_sems = refs[:-6], *refs[-6:]
-    total, width = out_buf.shape
-    piece = ins[0].shape[-2]
-    sources = [ref if len(ref.shape) == 2 else ref.at[q] for ref in ins for q in range(1 if len(ref.shape) == 2 else ref.shape[0])]
-    copies = [
-        pltpu.make_async_copy(ref, held.at[pl.ds(q * piece, piece)], in_sems.at[q]) for q, ref in enumerate(sources)
-    ]
-    for copy in copies:
-        copy.start()
+    ins, out_hbm, held, chosen, out_buf, out_sems = refs[:-5], *refs[-5:]
+    width = out_buf.shape[1]
+    piece = ins[0].shape[0]
     depth = held.shape[0]
+    for q, ref in enumerate(ins):
+        held[q * piece : (q + 1) * piece] = ref[...]
     lane = lax.broadcasted_iota(jnp.int32, (1, depth), 1)
     in_piece = lane % piece
     block = in_piece // group_rows
-    for copy in copies:
-        copy.wait()
     tags = jnp.zeros((1, depth), F32)
-    for q in range(len(sources)):
-        tag = held[(q + 1) * piece - 8 : (q + 1) * piece, 0:depth].astype(F32)[7:8]
+    for q, ref in enumerate(ins):
+        tag = ref[piece - 8 : piece, 0:depth].astype(F32)[7:8]
         tags = jnp.where((lane >= q * piece) & (lane < (q + 1) * piece), tag, tags)
     tags = tags.astype(jnp.int32)
     key = jnp.where((tags > 0) & (block < BLOCKS), block * rows_own + tags - 1, -1)
@@ -271,7 +326,9 @@
 
     halo_shape = jax.ShapeDtypeStruct((HALO + 1, width_c, width_b), BF16)
     packed = pl.pallas_call(
-        pack, out_shape=(halo_shape,) * 4, in_specs=[smem, vmem], out_specs=(vmem,) * 4,
+        pack, out_shape=(halo_shape,) * 4, in_specs=[hbm] * 2, out_specs=(vmem,) * 4,
+        scratch_shapes=[pltpu.SMEM((FACES, e_dev), jnp.int32), pltpu.VMEM((e_dev, width_c, width_b), BF16),
+                        pltpu.SemaphoreType.DMA((5,))],
         compiler_params=params(56), name="pack",
     )(nbr.T, prolong_t)
     up = lambda size: [(i, (i + 1) % size) for i in range(size)]
@@ -281,28 +338,44 @@
     from_left = lax.ppermute(packed[3], "dev", up(n_dev))
     from_right = lax.ppermute(packed[2], "dev", down(n_dev))
 
-    def route(*args):
-        return route_kernel(n_dev, rows_own, *args)
-
-    routes = pl.pallas_call(
-        route, out_shape=jax.ShapeDtypeStruct((8, LANES), jnp.int32), in_specs=[vmem] * 3 + [smem] * 2, out_specs=vmem,
-        name="routes",
-    )(elem_slot.reshape(1, e_dev), nbr.T, nbr_agg.T, touch_agg.T, coarse_row)
+    def early(*args):
+        return early_kernel(n_dev, rows_own, *args)
+
+    routes, lefts = pl.pallas_call(
+        early,
+        out_shape=(jax.ShapeDtypeStruct((8, LANES), jnp.int32), jax.ShapeDtypeStruct((EARLY, BLOCKS, width_c, width_b), BF16)),
+        in_specs=[hbm] * 7, out_specs=(vmem, vmem),
+        scratch_shapes=[
+            pltpu.VMEM((EARLY, BLOCKS, width_b, width_b), BF16),
+            pltpu.VMEM((EARLY, width_c, width_b), BF16),
+            pltpu.VMEM((1, e_dev), jnp.int32),
+            pltpu.VMEM((FACES, e_dev), jnp.int32),
+            pltpu.VMEM((FACES, e_dev), jnp.int32),
+            pltpu.SMEM(touch_agg.T.shape, jnp.int32),
+            pltpu.SMEM(coarse_row.shape, jnp.int32),
+            pltpu.SemaphoreType.DMA((EARLY,)),
+            pltpu.SemaphoreType.DMA(()),
+            pltpu.SemaphoreType.DMA((5,)),
+        ],
+        compiler_params=params(56), name="early",
+    )(elem_slot.reshape(1, e_dev), nbr.T, nbr_agg.T, touch_agg.T, coarse_row, a_blocks, prolong_t)
 
     outgoing = pl.pallas_call(
         main_kernel, out_shape=jax.ShapeDtypeStruct((n_dev, 8, width), BF16),
-        in_specs=[smem] + [hbm] * 6, out_specs=vmem,
+        in_specs=[hbm] * 8, out_specs=vmem,
         scratch_shapes=[
-            pltpu.VMEM((e_dev, BLOCKS, width_b, width_b), BF16),
+            pltpu.VMEM((e_dev - EARLY, BLOCKS, width_b, width_b), BF16),
             pltpu.VMEM((e_dev + 4 * HALO, width_c, width_b), BF16),
             pltpu.VMEM((TOUCH * 8 * width_c, LANES), F32),
+            pltpu.VMEM((EARLY, BLOCKS, width_c, width_b), BF16),
             pltpu.VMEM((BLOCKS, width_c, width_b), BF16),
             pltpu.VMEM((BLOCKS, width_c, width_b), BF16),
-            pltpu.SemaphoreType.DMA((e_dev,)),
-            pltpu.SemaphoreType.DMA((5,)),
+            pltpu.SMEM((8, LANES), jnp.int32),
+            pltpu.SemaphoreType.DMA((e_dev - EARLY,)),
+            pltpu.SemaphoreType.DMA((7,)),
         ],
         compiler_params=params(56), name="products",
-    )(routes, a_blocks, prolong_t, from_low, from_high, from_left, from_right)
+    )(routes, a_blocks, prolong_t, lefts, from_low, from_high, from_left, from_right)
     incoming = lax.all_to_all(outgoing, "dev", split_axis=0, concat_axis=0, tiled=True)
     piece = 8 * ((BLOCKS * group_rows) // 8 + 1)
 
@@ -324,13 +397,12 @@
         return scatter_kernel(rows_own, group_rows, *args)
 
     out = pl.pallas_call(
-        scatter, out_shape=jax.ShapeDtypeStruct((BLOCKS * rows_own, width), F32), in_specs=[hbm] * len(pieces),
+        scatter, out_shape=jax.ShapeDtypeStruct((BLOCKS * rows_own, width), F32), in_specs=[vmem] * len(pieces),
         out_specs=hbm,
         scratch_shapes=[
             pltpu.VMEM((n_grp * piece, width), BF16),
             pltpu.VMEM((BLOCKS * rows_own, n_grp * piece), BF16),
             pltpu.VMEM((BLOCKS * rows_own, width), F32),
-            pltpu.SemaphoreType.DMA((n_grp,)),
             pltpu.SemaphoreType.DMA((4,)),
         ],
         compiler_params=params(16), name="scatter",

time: 62.4 us -> 58.8 us (0.942)
  blocking collectives: 13.1 us -> 11.2 us
  waiting for transfers between devices: 2.11 us -> 1.04 us
    pallas_call x2, Pallas kernels: 4.55 us -> 8.01 us  [the longest x1 5.12 us: on_device(): pl.pallas_call(early, out_shape=(jax.ShapeDtypeStruct((8, LANES), jnp.int...]
    all_to_all x1, blocking collectives: 13.1 us -> 11.2 us  [on_device(): lax.all_to_all(outgoing, 'dev', split_axis=0, concat_axis=0, tiled=True)]
    pallas_call x1, Pallas kernels: 4.08 us -> 2.32 us  [on_device(): pl.pallas_call(scatter, out_shape=jax.ShapeDtypeStruct((BLOCKS * rows_own...]
    pallas_call x1, Pallas kernels: 13 us -> 11.3 us  [on_device(): pl.pallas_call(main_kernel, out_shape=jax.ShapeDtypeStruct((n_dev, 8, wid...]
    ppermute x1, waiting for transfers between devices: 1.07 us -> 0.01 us  [on_device(): from_left = lax.ppermute(packed[3], 'dev', up(n_dev))]
  transfers between devices with their start and end apart: 11 -> 11, of which waited for: 2 -> 1; matrix products, arithmetic and copies ran while one was open for 0% -> 0% of each run, Pallas kernels for 3% -> 9%
where the time goes in v4:
time: 58.8 us; the launch traced here: 58.6 us
  starting transfers between devices  23.6 us (40%)
  Pallas kernels  22 us (37%)
  blocking collectives  11.2 us (19%)
  waiting for transfers between devices  1.04 us (2%)
  local copies, waits for them, and re-layouts  0.76 us (1%)
    pallas_call x1, Pallas kernels, on_device(): pl.pallas_call(main_kernel, out_shape=jax.ShapeDtypeStruct((n_dev, 8, wid...  11.3 us
    all_to_all x1, blocking collectives, on_device(): lax.all_to_all(outgoing, 'dev', split_axis=0, concat_axis=0, tiled=True)  11.2 us
    ppermute x3, starting transfers between devices, on_device(): others = [lax.ppermute(part, 'grp', swap) for part in across]  6.86 us
    pallas_call x1, Pallas kernels, on_device(): pl.pallas_call(early, out_shape=(jax.ShapeDtypeStruct((8, LANES), jnp.int...  5.12 us
    ppermute x3, starting transfers between devices, on_device(): lax.ppermute(mine, 'grp', [(i, (i + 2 * k) % n_grp) for i in range(n_grp)])  5.12 us
    ppermute x1, starting transfers between devices, on_device(): from_right = lax.ppermute(packed[2], 'dev', down(n_dev))  3.72 us
    ppermute x1, starting transfers between devices, on_device(): twin = lax.ppermute(mine, 'grp', swap)  3.66 us
    ppermute x1, starting transfers between devices, on_device(): from_low = lax.ppermute(packed[1], 'grp', up(n_grp))  3.04 us
  transfers between devices with their start and end apart: 11, of which 1 were waited for; matrix products, arithmetic and copies ran while one was open for 0% of the time, Pallas kernels for 9%

profile of v4, /device:TPU:1, one launch (start us, length us, event | category | flops | bytes accessed | tf_op | source)
XLA Modules:
  0.0 58.6 jit_solution(15471069104434321673)
XLA Ops:
  0.0 2.9 %pack.1 = (bf16[9,32,192]{2,1,0:T(8,128)(2,1)}, bf16[9,32,192]{2,1,0:T(8,128)(2,1)}, bf16[9,32,192]{2,1,0:T(8,128)(2,1)}, bf16[9,32,192]{2,1,0:T(8,128)(2,1)}) custom-call(s32[6,32]{1,0:T(8,128)} %bitcast.9, bf16[32,32,192]{2,1,0:T(8,128)(2,1)} %p_hbm.1), custom_call_target="tpu_custom_call" | custom-call | tf_op jit(solution)/shard_map/pack/pallas_call | solution.py:328
  2.9 3.0 %collective-permute-start = (bf16[9,32,192]{2,1,0:T(8,128)(2,1)}, bf16[9,32,192]{2,1,0:T(8,128)(2,1)S(1)}, u32[]{:S(2)}, u32[]{:S(2)}) collective-permute-start(bf16[9,32,192]{2,1,0:T(8,128)(2,1)} %get-tuple-element.13), channel_id=1, source_target_pairs={{0,16},{16,32},{32,48},{48,64},{64,80},{80,96},{96,112},{112,0},{1... | collective-permute-start | bytes 331784 | tf_op jit(solution)/shard_map/ppermute | solution.py:336
  5.9 0.0 collective-permute-start.1
  5.9 1.2 %collective-permute-start.2 = (bf16[9,32,192]{2,1,0:T(8,128)(2,1)}, bf16[9,32,192]{2,1,0:T(8,128)(2,1)S(1)}, u32[]{:S(2)}, u32[]{:S(2)}) collective-permute-start(bf16[9,32,192]{2,1,0:T(8,128)(2,1)} %get-tuple-element.15), channel_id=1, source_target_pairs={{0,1},{1,2},{2,3},{3,4},{4,5},{5,6},{6,7},{7,8},{8,9},{9,10},{10,1... | collective-permute-start | bytes 331784 | tf_op jit(solution)/shard_map/ppermute | solution.py:338
  7.1 3.7 %collective-permute-start.3 = (bf16[9,32,192]{2,1,0:T(8,128)(2,1)}, bf16[9,32,192]{2,1,0:T(8,128)(2,1)S(1)}, u32[]{:S(2)}, u32[]{:S(2)}) collective-permute-start(bf16[9,32,192]{2,1,0:T(8,128)(2,1)} %get-tuple-element.16), channel_id=1, source_target_pairs={{1,0},{2,1},{3,2},{4,3},{5,4},{6,5},{7,6},{8,7},{9,8},{10,9},{11,1... | collective-permute-start | bytes 331784 | tf_op jit(solution)/shard_map/ppermute | solution.py:339
  10.9 5.1 %early.1 = (s32[8,128]{1,0:T(8,128)}, bf16[8,7,32,192]{3,2,1,0:T(8,128)(2,1)}) custom-call(s32[1,32]{1,0:T(1,128)} %bitcast.13, s32[6,32]{1,0:T(8,128)} %bitcast.10, s32[6,32]{1,0:T(8,128)} %bitcast.11, s32[6,128]{1,0:T(8,128)} %bitcast.12, s32[528]{0:T(1024)} %args_4_.4, bf16[32,7,192,192]{3,2,1,0:T(8,128)(2,1)} %a_hbm.1, bf16[32,32,192]{2,1,0:T(8,128)(2,1)} %p_hbm.1), custom_call_target="tpu_custom_call" | custom-call | tf_op jit(solution)/shard_map/early/pallas_call | solution.py:344
  16.0 0.0 collective-permute-done.h0
  16.0 0.0 copy-start
  16.0 0.0 collective-permute-done.1.h1
  16.0 0.0 copy-start.1
  16.0 0.0 collective-permute-done.2.h2
  16.1 0.0 copy-start.2
  16.1 0.0 collective-permute-done.3.h3
  16.1 0.0 copy-start.3
  16.1 0.6 %copy-done = bf16[9,32,192]{2,1,0:T(8,128)(2,1)} copy-done((bf16[9,32,192]{2,1,0:T(8,128)(2,1)}, bf16[9,32,192]{2,1,0:T(8,128)(2,1)S(1)}, u32[]{:S(2)}) %copy-start) | copy-done | bytes 110616
  16.7 0.0 copy-done.1
  16.7 0.1 copy-done.2
  16.8 0.1 copy-done.3
  16.8 11.3 %products.1 = bf16[16,8,1024]{2,1,0:T(8,128)(2,1)} custom-call(s32[8,128]{1,0:T(8,128)} %get-tuple-element.11.route_hbm, bf16[32,7,192,192]{3,2,1,0:T(8,128)(2,1)} %a_hbm.1, bf16[32,32,192]{2,1,0:T(8,128)(2,1)} %p_hbm.1, bf16[8,7,32,192]{3,2,1,0:T(8,128)(2,1)} %get-tuple-element.12.early_hbm, bf16[9,32,192]{2,1,0:T(8,128)(2,1)} %copy-done, ...), custom_call_target="tpu_custom_call" | custom-call | tf_op jit(solution)/shard_map/products/pallas_call | solution.py:363
  28.1 11.2 %all_to_all.5 = bf16[16,8,1024]{2,1,0:T(8,128)(2,1)S(1)} all-to-all(bf16[16,8,1024]{2,1,0:T(8,128)(2,1)} %products.1), channel_id=1, replica_groups=mesh['grp'=8,'dev'=16] {'dev'}, dimensions={0} | all-to-all | bytes 524288 | tf_op jit(solution)/shard_map/all_to_all | solution.py:379
  39.3 0.3 combine.1.args_0_
  39.6 2.3 %collective-permute-start.7 = (bf16[80,1024]{1,0:T(8,128)(2,1)S(1)}, bf16[80,1024]{1,0:T(8,128)(2,1)S(1)}, u32[]{:S(2)}, u32[]{:S(2)}) collective-permute-start(bf16[80,1024]{1,0:T(8,128)(2,1)S(1)} %combine.1.args_0_), channel_id=1, source_target_pairs={{0,96},{16,112},{32,0},{48,16},{64,32},{80,48},{96,64},{112,80},{1... | collective-permute-start | bytes 491528 | tf_op jit(solution)/shard_map/ppermute | solution.py:391
  42.0 2.3 %collective-permute-start.6 = (bf16[80,1024]{1,0:T(8,128)(2,1)S(1)}, bf16[80,1024]{1,0:T(8,128)(2,1)S(1)}, u32[]{:S(2)}, u32[]{:S(2)}) collective-permute-start(bf16[80,1024]{1,0:T(8,128)(2,1)S(1)} %combine.1.args_0_), channel_id=1, source_target_pairs={{0,64},{16,80},{32,96},{48,112},{64,0},{80,16},{96,32},{112,48},{1... | collective-permute-start | bytes 491528 | tf_op jit(solution)/shard_map/ppermute | solution.py:391
  44.2 0.5 collective-permute-start.5
  44.7 3.7 %collective-permute-start.4 = (bf16[80,1024]{1,0:T(8,128)(2,1)S(1)}, bf16[80,1024]{1,0:T(8,128)(2,1)S(1)}, u32[]{:S(2)}, u32[]{:S(2)}) collective-permute-start(bf16[80,1024]{1,0:T(8,128)(2,1)S(1)} %combine.1.args_0_), channel_id=1, source_target_pairs={{0,16},{16,0},{32,48},{48,32},{64,80},{80,64},{96,112},{112,96},{1... | collective-permute-start | bytes 491528 | tf_op jit(solution)/shard_map/ppermute | solution.py:392
  48.4 0.0 collective-permute-done.7.args_4_
  48.4 2.9 %collective-permute-start.10 = (bf16[80,1024]{1,0:T(8,128)(2,1)S(1)}, bf16[80,1024]{1,0:T(8,128)(2,1)S(1)}, u32[]{:S(2)}, u32[]{:S(2)}) collective-permute-start(bf16[80,1024]{1,0:T(8,128)(2,1)S(1)} %collective-permute-done.7.args_4_), channel_id=1, source_target_pairs={{0,16},{16,0},{32,48},{48,32},{64,80},{80,64},{96,112},{112,96},{1... | collective-permute-start | bytes 491528 | tf_op jit(solution)/shard_map/ppermute | solution.py:393
  51.3 0.0 collective-permute-done.6.args_3_
  51.3 2.3 %collective-permute-start.9 = (bf16[80,1024]{1,0:T(8,128)(2,1)S(1)}, bf16[80,1024]{1,0:T(8,128)(2,1)S(1)}, u32[]{:S(2)}, u32[]{:S(2)}) collective-permute-start(bf16[80,1024]{1,0:T(8,128)(2,1)S(1)} %collective-permute-done.6.args_3_), channel_id=1, source_target_pairs={{0,16},{16,0},{32,48},{48,32},{64,80},{80,64},{96,112},{112,96},{1... | collective-permute-start | bytes 491528 | tf_op jit(solution)/shard_map/ppermute | solution.py:393
  53.6 0.0 collective-permute-done.5.args_2_
  53.6 1.6 %collective-permute-start.8 = (bf16[80,1024]{1,0:T(8,128)(2,1)S(1)}, bf16[80,1024]{1,0:T(8,128)(2,1)S(1)}, u32[]{:S(2)}, u32[]{:S(2)}) collective-permute-start(bf16[80,1024]{1,0:T(8,128)(2,1)S(1)} %collective-permute-done.5.args_2_), channel_id=1, source_target_pairs={{0,16},{16,0},{32,48},{48,32},{64,80},{80,64},{96,112},{112,96},{1... | collective-permute-start | bytes 491528 | tf_op jit(solution)/shard_map/ppermute | solution.py:393
  55.3 0.0 collective-permute-done.4.args_1_
  55.3 0.0 collective-permute-done.10.args_7_
  55.3 0.0 collective-permute-done.9.args_6_
  55.3 1.0 %collective-permute-done.8.args_5_ = bf16[80,1024]{1,0:T(8,128)(2,1)S(1)} collective-permute-done((bf16[80,1024]{1,0:T(8,128)(2,1)S(1)}, bf16[80,1024]{1,0:T(8,128)(2,1)S(1)}, u32[]{:S(2)}, u32[]{:S(2)}) %collective-permute-start.8) | collective-permute-done | bytes 163872 | tf_op jit(solution)/shard_map/ppermute | solution.py:393
  56.3 2.3 %scatter.1 = f32[616,1024]{1,0:T(8,128)} custom-call(bf16[80,1024]{1,0:T(8,128)(2,1)S(1)} %combine.1.args_0_, bf16[80,1024]{1,0:T(8,128)(2,1)S(1)} %collective-permute-done.4.args_1_, bf16[80,1024]{1,0:T(8,128)(2,1)S(1)} %collective-permute-done.5.args_2_, bf16[80,1024]{1,0:T(8,128)(2,1)S(1)} %collective-permute-done.6.args_3_, ...), custom_call_target="tpu_custom_call" | custom-call | tf_op jit(solution)/shard_map/scatter/pallas_call | solution.py:399
Async XLA Ops:
  2.9 13.1 %collective-permute-start = (bf16[9,32,192]{2,1,0:T(8,128)(2,1)}, bf16[9,32,192]{2,1,0:T(8,128)(2,1)S(1)}, u32[]{:S(2)}, u32[]{:S(2)}) collective-permute-start(bf16[9,32,192]{2,1,0:T(8,128)(2,1)} %get-tuple-element.13), channel_id=1, source_target_pairs={{0,16},{16,32},{32,48},{48,64},{64,80},{80,96},{96,112},{112,0},{1... | collective-permute-start | bytes 331784 | tf_op jit(solution)/shard_map/ppermute | solution.py:336
  5.9 10.1 %collective-permute-start.1 = (bf16[9,32,192]{2,1,0:T(8,128)(2,1)}, bf16[9,32,192]{2,1,0:T(8,128)(2,1)S(1)}, u32[]{:S(2)}, u32[]{:S(2)}) collective-permute-start(bf16[9,32,192]{2,1,0:T(8,128)(2,1)} %get-tuple-element.14), channel_id=1, source_target_pairs={{16,0},{32,16},{48,32},{64,48},{80,64},{96,80},{112,96},{0,112},{1... | collective-permute-start | bytes 331784 | tf_op jit(solution)/shard_map/ppermute | solution.py:337
  5.9 10.1 %collective-permute-start.2 = (bf16[9,32,192]{2,1,0:T(8,128)(2,1)}, bf16[9,32,192]{2,1,0:T(8,128)(2,1)S(1)}, u32[]{:S(2)}, u32[]{:S(2)}) collective-permute-start(bf16[9,32,192]{2,1,0:T(8,128)(2,1)} %get-tuple-element.15), channel_id=1, source_target_pairs={{0,1},{1,2},{2,3},{3,4},{4,5},{5,6},{6,7},{7,8},{8,9},{9,10},{10,1... | collective-permute-start | bytes 331784 | tf_op jit(solution)/shard_map/ppermute | solution.py:338
  7.1 8.9 %collective-permute-start.3 = (bf16[9,32,192]{2,1,0:T(8,128)(2,1)}, bf16[9,32,192]{2,1,0:T(8,128)(2,1)S(1)}, u32[]{:S(2)}, u32[]{:S(2)}) collective-permute-start(bf16[9,32,192]{2,1,0:T(8,128)(2,1)} %get-tuple-element.16), channel_id=1, source_target_pairs={{1,0},{2,1},{3,2},{4,3},{5,4},{6,5},{7,6},{8,7},{9,8},{10,9},{11,1... | collective-permute-start | bytes 331784 | tf_op jit(solution)/shard_map/ppermute | solution.py:339
  16.0 0.7 %copy-start = (bf16[9,32,192]{2,1,0:T(8,128)(2,1)}, bf16[9,32,192]{2,1,0:T(8,128)(2,1)S(1)}, u32[]{:S(2)}) copy-start(bf16[9,32,192]{2,1,0:T(8,128)(2,1)S(1)} %collective-permute-done.h0) | copy-start | bytes 331780
  16.0 0.7 %copy-start.1 = (bf16[9,32,192]{2,1,0:T(8,128)(2,1)}, bf16[9,32,192]{2,1,0:T(8,128)(2,1)S(1)}, u32[]{:S(2)}) copy-start(bf16[9,32,192]{2,1,0:T(8,128)(2,1)S(1)} %collective-permute-done.1.h1) | copy-start | bytes 331780
  16.1 0.7 %copy-start.2 = (bf16[9,32,192]{2,1,0:T(8,128)(2,1)}, bf16[9,32,192]{2,1,0:T(8,128)(2,1)S(1)}, u32[]{:S(2)}) copy-start(bf16[9,32,192]{2,1,0:T(8,128)(2,1)S(1)} %collective-permute-done.2.h2) | copy-start | bytes 331780
  16.1 0.8 %copy-start.3 = (bf16[9,32,192]{2,1,0:T(8,128)(2,1)}, bf16[9,32,192]{2,1,0:T(8,128)(2,1)S(1)}, u32[]{:S(2)}) copy-start(bf16[9,32,192]{2,1,0:T(8,128)(2,1)S(1)} %collective-permute-done.3.h3) | copy-start | bytes 331780
  39.6 8.8 %collective-permute-start.7 = (bf16[80,1024]{1,0:T(8,128)(2,1)S(1)}, bf16[80,1024]{1,0:T(8,128)(2,1)S(1)}, u32[]{:S(2)}, u32[]{:S(2)}) collective-permute-start(bf16[80,1024]{1,0:T(8,128)(2,1)S(1)} %combine.1.args_0_), channel_id=1, source_target_pairs={{0,96},{16,112},{32,0},{48,16},{64,32},{80,48},{96,64},{112,80},{1... | collective-permute-start | bytes 491528 | tf_op jit(solution)/shard_map/ppermute | solution.py:391
  42.0 9.4 %collective-permute-start.6 = (bf16[80,1024]{1,0:T(8,128)(2,1)S(1)}, bf16[80,1024]{1,0:T(8,128)(2,1)S(1)}, u32[]{:S(2)}, u32[]{:S(2)}) collective-permute-start(bf16[80,1024]{1,0:T(8,128)(2,1)S(1)} %combine.1.args_0_), channel_id=1, source_target_pairs={{0,64},{16,80},{32,96},{48,112},{64,0},{80,16},{96,32},{112,48},{1... | collective-permute-start | bytes 491528 | tf_op jit(solution)/shard_map/ppermute | solution.py:391
  44.2 9.4 %collective-permute-start.5 = (bf16[80,1024]{1,0:T(8,128)(2,1)S(1)}, bf16[80,1024]{1,0:T(8,128)(2,1)S(1)}, u32[]{:S(2)}, u32[]{:S(2)}) collective-permute-start(bf16[80,1024]{1,0:T(8,128)(2,1)S(1)} %combine.1.args_0_), channel_id=1, source_target_pairs={{0,32},{16,48},{32,64},{48,80},{64,96},{80,112},{96,0},{112,16},{1... | collective-permute-start | bytes 491528 | tf_op jit(solution)/shard_map/ppermute | solution.py:391
  44.7 10.5 %collective-permute-start.4 = (bf16[80,1024]{1,0:T(8,128)(2,1)S(1)}, bf16[80,1024]{1,0:T(8,128)(2,1)S(1)}, u32[]{:S(2)}, u32[]{:S(2)}) collective-permute-start(bf16[80,1024]{1,0:T(8,128)(2,1)S(1)} %combine.1.args_0_), channel_id=1, source_target_pairs={{0,16},{16,0},{32,48},{48,32},{64,80},{80,64},{96,112},{112,96},{1... | collective-permute-start | bytes 491528 | tf_op jit(solution)/shard_map/ppermute | solution.py:392
  48.4 6.9 %collective-permute-start.10 = (bf16[80,1024]{1,0:T(8,128)(2,1)S(1)}, bf16[80,1024]{1,0:T(8,128)(2,1)S(1)}, u32[]{:S(2)}, u32[]{:S(2)}) collective-permute-start(bf16[80,1024]{1,0:T(8,128)(2,1)S(1)} %collective-permute-done.7.args_4_), channel_id=1, source_target_pairs={{0,16},{16,0},{32,48},{48,32},{64,80},{80,64},{96,112},{112,96},{1... | collective-permute-start | bytes 491528 | tf_op jit(solution)/shard_map/ppermute | solution.py:393
  51.3 4.0 %collective-permute-start.9 = (bf16[80,1024]{1,0:T(8,128)(2,1)S(1)}, bf16[80,1024]{1,0:T(8,128)(2,1)S(1)}, u32[]{:S(2)}, u32[]{:S(2)}) collective-permute-start(bf16[80,1024]{1,0:T(8,128)(2,1)S(1)} %collective-permute-done.6.args_3_), channel_id=1, source_target_pairs={{0,16},{16,0},{32,48},{48,32},{64,80},{80,64},{96,112},{112,96},{1... | collective-permute-start | bytes 491528 | tf_op jit(solution)/shard_map/ppermute | solution.py:393
  53.6 2.7 %collective-permute-start.8 = (bf16[80,1024]{1,0:T(8,128)(2,1)S(1)}, bf16[80,1024]{1,0:T(8,128)(2,1)S(1)}, u32[]{:S(2)}, u32[]{:S(2)}) collective-permute-start(bf16[80,1024]{1,0:T(8,128)(2,1)S(1)} %collective-permute-done.5.args_2_), channel_id=1, source_target_pairs={{0,16},{16,0},{32,48},{48,32},{64,80},{80,64},{96,112},{112,96},{1... | collective-permute-start | bytes 491528 | tf_op jit(solution)/shard_map/ppermute | solution.py:393

commit v5 on v4

--- a/solution.py
+++ b/solution.py
@@ -11,7 +11,7 @@
 LANES = 128
 HALO = 8
 WINDOW = 8
-EARLY = 8
+EARLY = 12
 SAME = 256
 APART = 512
 F32 = jnp.float32
@@ -120,19 +120,20 @@
     out_ref[FACES + 1 : FACES + 2] = rows
     p_copy.wait()
 
-    def two(i, c):
-        for e in (2 * i, 2 * i + 1):
-            fetch(e).wait()
-        for e in (2 * i, 2 * i + 1):
+    def four(i, c):
+        for j in range(4):
+            fetch(4 * i + j).wait()
+        for j in range(4):
+            e = 4 * i + j
             for k in range(BLOCKS):
                 lefts[e, k] = jnp.dot(pbuf[e], abuf[e, k], preferred_element_type=F32).astype(BF16)
         return c
 
-    lax.fori_loop(0, early // 2, two, 0)
-
-
-def main_kernel(route_hbm, a_hbm, p_hbm, early_hbm, h0, h1, h2, h3,
-                out_ref, abuf, pool, acc, done, lefts0, lefts1, route_ref, a_sems, h_sems):
+    lax.fori_loop(0, early // 4, four, 0)
+
+
+def main_kernel(route_hbm, a_hbm, p_hbm, done, h0, h1, h2, h3,
+                out_ref, abuf, pool, acc, lefts0, lefts1, route_ref, a_sems, h_sems):
     e_dev, width_c, _ = p_hbm.shape
     early = done.shape[0]
 
@@ -143,8 +144,6 @@
     own_copy.start()
     route_copy = pltpu.make_async_copy(route_hbm, route_ref, h_sems.at[5])
     route_copy.start()
-    done_copy = pltpu.make_async_copy(early_hbm, done, h_sems.at[6])
-    done_copy.start()
     halos = [
         pltpu.make_async_copy(h.at[pl.ds(0, HALO)], pool.at[pl.ds(e_dev + HALO * d, HALO)], h_sems.at[d])
         for d, h in enumerate((h0, h1, h2, h3))
@@ -157,7 +156,6 @@
     out_ref[...] = jnp.zeros_like(out_ref)
     own_copy.wait()
     route_copy.wait()
-    done_copy.wait()
     for copy in halos:
         copy.wait()
 
@@ -186,11 +184,11 @@
         acc[pl.ds(at, width_c), 0:width_c] += total
 
     def ready(i, c):
-        for e in (2 * i, 2 * i + 1):
-            add_products(e, done.at[e])
+        for j in range(4):
+            add_products(4 * i + j, done.at[4 * i + j])
         return c
 
-    lax.fori_loop(0, early // 2, ready, 0)
+    lax.fori_loop(0, early // 4, ready, 0)
     fetch(early).wait()
     make_lefts(early, lefts0)
 
@@ -314,6 +312,7 @@
     group_rows = ((n_dev * half + 1) + half) // (half + 1)
     rows_own = n_grp * group_rows
     width = width_c * width_c
+    pin = lambda x: pltpu.with_memory_space_constraint(x, pltpu.MemorySpace.HBM)
     smem = pl.BlockSpec(memory_space=SMEM)
     vmem = pl.BlockSpec(memory_space=VMEM)
     hbm = pl.BlockSpec(memory_space=pl.ANY)
@@ -329,8 +328,8 @@
         pack, out_shape=(halo_shape,) * 4, in_specs=[hbm] * 2, out_specs=(vmem,) * 4,
         scratch_shapes=[pltpu.SMEM((FACES, e_dev), jnp.int32), pltpu.VMEM((e_dev, width_c, width_b), BF16),
                         pltpu.SemaphoreType.DMA((5,))],
-        compiler_params=params(56), name="pack",
-    )(nbr.T, prolong_t)
+        compiler_params=params(8), name="pack",
+    )(pin(nbr.T), pin(prolong_t))
     up = lambda size: [(i, (i + 1) % size) for i in range(size)]
     down = lambda size: [((i + 1) % size, i) for i in range(size)]
     from_low = lax.ppermute(packed[1], "grp", up(n_grp))
@@ -357,25 +356,24 @@
             pltpu.SemaphoreType.DMA(()),
             pltpu.SemaphoreType.DMA((5,)),
         ],
-        compiler_params=params(56), name="early",
-    )(elem_slot.reshape(1, e_dev), nbr.T, nbr_agg.T, touch_agg.T, coarse_row, a_blocks, prolong_t)
+        compiler_params=params(14), name="early",
+    )(*map(pin, (elem_slot.reshape(1, e_dev), nbr.T, nbr_agg.T, touch_agg.T, coarse_row, a_blocks, prolong_t)))
 
     outgoing = pl.pallas_call(
         main_kernel, out_shape=jax.ShapeDtypeStruct((n_dev, 8, width), BF16),
-        in_specs=[hbm] * 8, out_specs=vmem,
+        in_specs=[hbm] * 3 + [vmem] + [hbm] * 4, out_specs=vmem,
         scratch_shapes=[
             pltpu.VMEM((e_dev - EARLY, BLOCKS, width_b, width_b), BF16),
             pltpu.VMEM((e_dev + 4 * HALO, width_c, width_b), BF16),
             pltpu.VMEM((TOUCH * 8 * width_c, LANES), F32),
-            pltpu.VMEM((EARLY, BLOCKS, width_c, width_b), BF16),
             pltpu.VMEM((BLOCKS, width_c, width_b), BF16),
             pltpu.VMEM((BLOCKS, width_c, width_b), BF16),
             pltpu.SMEM((8, LANES), jnp.int32),
             pltpu.SemaphoreType.DMA((e_dev - EARLY,)),
-            pltpu.SemaphoreType.DMA((7,)),
+            pltpu.SemaphoreType.DMA((6,)),
         ],
-        compiler_params=params(56), name="products",
-    )(routes, a_blocks, prolong_t, lefts, from_low, from_high, from_left, from_right)
+        compiler_params=params(36), name="products",
+    )(routes, pin(a_blocks), pin(prolong_t), lefts, from_low, from_high, from_left, from_right)
     incoming = lax.all_to_all(outgoing, "dev", split_axis=0, concat_axis=0, tiled=True)
     piece = 8 * ((BLOCKS * group_rows) // 8 + 1)
 

time: 58.8 us -> 53.5 us (0.910)
  Pallas kernels: 22 us -> 18.1 us
  local copies, waits for them, and re-layouts: 0.76 us -> 0 us
  blocking collectives: 11.2 us -> 10.6 us
    pallas_call x1, Pallas kernels: 11.3 us -> 7.82 us  [on_device(): pl.pallas_call(main_kernel, out_shape=jax.ShapeDtypeStruct((n_dev, 8, wid...]
    unnamed x8 -> x0, local copies, waits for them, and re-layouts: 0.76 us -> none
    pallas_call x1, Pallas kernels: 2.88 us -> 2.16 us  [on_device(): pl.pallas_call(pack, out_shape=(halo_shape,) * 4, in_specs=[hbm] * 2, out...]
  transfers between devices with their start and end apart: 11 -> 11, of which waited for: 1 -> 1; matrix products, arithmetic and copies ran while one was open for 0% -> 0% of each run, Pallas kernels for 9% -> 10%
where the time goes in v5:
time: 53.5 us; the launch traced here: 53.3 us
  starting transfers between devices  23.4 us (44%)
  Pallas kernels  18.1 us (34%)
  blocking collectives  10.6 us (20%)
  waiting for transfers between devices  1.04 us (2%)
    all_to_all x1, blocking collectives, on_device(): lax.all_to_all(outgoing, 'dev', split_axis=0, concat_axis=0, tiled=True)  10.6 us
    pallas_call x1, Pallas kernels, on_device(): pl.pallas_call(main_kernel, out_shape=jax.ShapeDtypeStruct((n_dev, 8, wid...  7.82 us
    ppermute x3, starting transfers between devices, on_device(): others = [lax.ppermute(part, 'grp', swap) for part in across]  6.87 us
    pallas_call x1, Pallas kernels, on_device(): pl.pallas_call(early, out_shape=(jax.ShapeDtypeStruct((8, LANES), jnp.int...  5.5 us
    ppermute x3, starting transfers between devices, on_device(): lax.ppermute(mine, 'grp', [(i, (i + 2 * k) % n_grp) for i in range(n_grp)])  4.94 us
    ppermute x1, starting transfers between devices, on_device(): from_right = lax.ppermute(packed[2], 'dev', down(n_dev))  3.72 us
    ppermute x1, starting transfers between devices, on_device(): twin = lax.ppermute(mine, 'grp', swap)  3.66 us
    ppermute x1, starting transfers between devices, on_device(): from_low = lax.ppermute(packed[1], 'grp', up(n_grp))  3.04 us
  transfers between devices with their start and end apart: 11, of which 1 were waited for; matrix products, arithmetic and copies ran while one was open for 0% of the time, Pallas kernels for 10%

profile of v5, /device:TPU:1, one launch (start us, length us, event | category | flops | bytes accessed | tf_op | source)
XLA Modules:
  0.0 53.3 jit_solution(18403694735931325734)
XLA Ops:
  0.0 2.2 %pack.1 = (bf16[9,32,192]{2,1,0:T(8,128)(2,1)S(1)}, bf16[9,32,192]{2,1,0:T(8,128)(2,1)S(1)}, bf16[9,32,192]{2,1,0:T(8,128)(2,1)S(1)}, bf16[9,32,192]{2,1,0:T(8,128)(2,1)S(1)}) custom-call(s32[6,32]{1,0:T(8,128)} %bitcast.9, bf16[32,32,192]{2,1,0:T(8,128)(2,1)} %p_hbm.1), custom_call_target="tpu_custom_call" | custom-call | tf_op jit(solution)/shard_map/pack/pallas_call | solution.py:327
  2.2 3.0 %collective-permute-start = (bf16[9,32,192]{2,1,0:T(8,128)(2,1)S(1)}, bf16[9,32,192]{2,1,0:T(8,128)(2,1)S(1)}, u32[]{:S(2)}, u32[]{:S(2)}) collective-permute-start(bf16[9,32,192]{2,1,0:T(8,128)(2,1)S(1)} %get-tuple-element.13), channel_id=1, source_target_pairs={{0,16},{16,32},{32,48},{48,64},{64,80},{80,96},{96,112},{112,0},{1... | collective-permute-start | bytes 331784 | tf_op jit(solution)/shard_map/ppermute | solution.py:335
  5.2 0.0 collective-permute-start.1
  5.2 1.2 %collective-permute-start.2 = (bf16[9,32,192]{2,1,0:T(8,128)(2,1)S(1)}, bf16[9,32,192]{2,1,0:T(8,128)(2,1)S(1)}, u32[]{:S(2)}, u32[]{:S(2)}) collective-permute-start(bf16[9,32,192]{2,1,0:T(8,128)(2,1)S(1)} %get-tuple-element.15), channel_id=1, source_target_pairs={{0,1},{1,2},{2,3},{3,4},{4,5},{5,6},{6,7},{7,8},{8,9},{9,10},{10,1... | collective-permute-start | bytes 331784 | tf_op jit(solution)/shard_map/ppermute | solution.py:337
  6.4 3.7 %collective-permute-start.3 = (bf16[9,32,192]{2,1,0:T(8,128)(2,1)S(1)}, bf16[9,32,192]{2,1,0:T(8,128)(2,1)S(1)}, u32[]{:S(2)}, u32[]{:S(2)}) collective-permute-start(bf16[9,32,192]{2,1,0:T(8,128)(2,1)S(1)} %get-tuple-element.16), channel_id=1, source_target_pairs={{1,0},{2,1},{3,2},{4,3},{5,4},{6,5},{7,6},{8,7},{9,8},{10,9},{11,1... | collective-permute-start | bytes 331784 | tf_op jit(solution)/shard_map/ppermute | solution.py:338
  10.1 5.5 %early.1 = (s32[8,128]{1,0:T(8,128)S(1)}, bf16[12,7,32,192]{3,2,1,0:T(8,128)(2,1)S(1)}) custom-call(s32[1,32]{1,0:T(1,128)} %bitcast.13, s32[6,32]{1,0:T(8,128)} %bitcast.10, s32[6,32]{1,0:T(8,128)} %bitcast.11, s32[6,128]{1,0:T(8,128)} %bitcast.12, s32[528]{0:T(1024)} %args_4_.4, bf16[32,7,192,192]{3,2,1,0:T(8,128)(2,1)} %a_hbm.1, bf16[32,32,192]{2,1,0:T(8,128)(2,1)} %p_hbm.1), custom_call_target="tpu_custom_call" | custom-call | tf_op jit(solution)/shard_map/early/pallas_call | solution.py:343
  15.6 0.0 collective-permute-done.h0
  15.7 0.0 collective-permute-done.1.h1
  15.7 0.0 collective-permute-done.2.h2
  15.7 0.0 collective-permute-done.3.h3
  15.7 7.8 %products.1 = bf16[16,8,1024]{2,1,0:T(8,128)(2,1)S(1)} custom-call(s32[8,128]{1,0:T(8,128)S(1)} %get-tuple-element.11.route_hbm, bf16[32,7,192,192]{3,2,1,0:T(8,128)(2,1)} %a_hbm.1, bf16[32,32,192]{2,1,0:T(8,128)(2,1)} %p_hbm.1, bf16[12,7,32,192]{3,2,1,0:T(8,128)(2,1)S(1)} %get-tuple-element.12.done, bf16[9,32,192]{2,1,0:T(8,128)(2,1)S(1)} %collective-permute-done.h0, ...), custom_call_target="tpu_custom_call" | custom-call | tf_op jit(solution)/shard_map/products/pallas_call | solution.py:362
  23.5 10.6 %all_to_all.5 = bf16[16,8,1024]{2,1,0:T(8,128)(2,1)S(1)} all-to-all(bf16[16,8,1024]{2,1,0:T(8,128)(2,1)S(1)} %products.1), channel_id=1, replica_groups=mesh['grp'=8,'dev'=16] {'dev'}, dimensions={0} | all-to-all | bytes 524288 | tf_op jit(solution)/shard_map/all_to_all | solution.py:377
  34.1 0.3 combine.1.args_0_
  34.5 2.4 %collective-permute-start.7 = (bf16[80,1024]{1,0:T(8,128)(2,1)S(1)}, bf16[80,1024]{1,0:T(8,128)(2,1)S(1)}, u32[]{:S(2)}, u32[]{:S(2)}) collective-permute-start(bf16[80,1024]{1,0:T(8,128)(2,1)S(1)} %combine.1.args_0_), channel_id=1, source_target_pairs={{0,96},{16,112},{32,0},{48,16},{64,32},{80,48},{96,64},{112,80},{1... | collective-permute-start | bytes 491528 | tf_op jit(solution)/shard_map/ppermute | solution.py:389
  36.9 2.0 %collective-permute-start.6 = (bf16[80,1024]{1,0:T(8,128)(2,1)S(1)}, bf16[80,1024]{1,0:T(8,128)(2,1)S(1)}, u32[]{:S(2)}, u32[]{:S(2)}) collective-permute-start(bf16[80,1024]{1,0:T(8,128)(2,1)S(1)} %combine.1.args_0_), channel_id=1, source_target_pairs={{0,64},{16,80},{32,96},{48,112},{64,0},{80,16},{96,32},{112,48},{1... | collective-permute-start | bytes 491528 | tf_op jit(solution)/shard_map/ppermute | solution.py:389
  38.9 0.5 %collective-permute-start.5 = (bf16[80,1024]{1,0:T(8,128)(2,1)S(1)}, bf16[80,1024]{1,0:T(8,128)(2,1)S(1)}, u32[]{:S(2)}, u32[]{:S(2)}) collective-permute-start(bf16[80,1024]{1,0:T(8,128)(2,1)S(1)} %combine.1.args_0_), channel_id=1, source_target_pairs={{0,32},{16,48},{32,64},{48,80},{64,96},{80,112},{96,0},{112,16},{1... | collective-permute-start | bytes 491528 | tf_op jit(solution)/shard_map/ppermute | solution.py:389
  39.4 3.7 %collective-permute-start.4 = (bf16[80,1024]{1,0:T(8,128)(2,1)S(1)}, bf16[80,1024]{1,0:T(8,128)(2,1)S(1)}, u32[]{:S(2)}, u32[]{:S(2)}) collective-permute-start(bf16[80,1024]{1,0:T(8,128)(2,1)S(1)} %combine.1.args_0_), channel_id=1, source_target_pairs={{0,16},{16,0},{32,48},{48,32},{64,80},{80,64},{96,112},{112,96},{1... | collective-permute-start | bytes 491528 | tf_op jit(solution)/shard_map/ppermute | solution.py:390
  43.1 0.0 collective-permute-done.7.args_4_
  43.1 2.9 %collective-permute-start.10 = (bf16[80,1024]{1,0:T(8,128)(2,1)S(1)}, bf16[80,1024]{1,0:T(8,128)(2,1)S(1)}, u32[]{:S(2)}, u32[]{:S(2)}) collective-permute-start(bf16[80,1024]{1,0:T(8,128)(2,1)S(1)} %collective-permute-done.7.args_4_), channel_id=1, source_target_pairs={{0,16},{16,0},{32,48},{48,32},{64,80},{80,64},{96,112},{112,96},{1... | collective-permute-start | bytes 491528 | tf_op jit(solution)/shard_map/ppermute | solution.py:391
  46.0 0.0 collective-permute-done.6.args_3_
  46.0 2.3 %collective-permute-start.9 = (bf16[80,1024]{1,0:T(8,128)(2,1)S(1)}, bf16[80,1024]{1,0:T(8,128)(2,1)S(1)}, u32[]{:S(2)}, u32[]{:S(2)}) collective-permute-start(bf16[80,1024]{1,0:T(8,128)(2,1)S(1)} %collective-permute-done.6.args_3_), channel_id=1, source_target_pairs={{0,16},{16,0},{32,48},{48,32},{64,80},{80,64},{96,112},{112,96},{1... | collective-permute-start | bytes 491528 | tf_op jit(solution)/shard_map/ppermute | solution.py:391
  48.3 0.0 collective-permute-done.5.args_2_
  48.3 1.6 %collective-permute-start.8 = (bf16[80,1024]{1,0:T(8,128)(2,1)S(1)}, bf16[80,1024]{1,0:T(8,128)(2,1)S(1)}, u32[]{:S(2)}, u32[]{:S(2)}) collective-permute-start(bf16[80,1024]{1,0:T(8,128)(2,1)S(1)} %collective-permute-done.5.args_2_), channel_id=1, source_target_pairs={{0,16},{16,0},{32,48},{48,32},{64,80},{80,64},{96,112},{112,96},{1... | collective-permute-start | bytes 491528 | tf_op jit(solution)/shard_map/ppermute | solution.py:391
  49.9 0.0 collective-permute-done.4.args_1_
  49.9 0.0 collective-permute-done.10.args_7_
  50.0 0.0 collective-permute-done.9.args_6_
  50.0 1.0 %collective-permute-done.8.args_5_ = bf16[80,1024]{1,0:T(8,128)(2,1)S(1)} collective-permute-done((bf16[80,1024]{1,0:T(8,128)(2,1)S(1)}, bf16[80,1024]{1,0:T(8,128)(2,1)S(1)}, u32[]{:S(2)}, u32[]{:S(2)}) %collective-permute-start.8) | collective-permute-done | bytes 163872 | tf_op jit(solution)/shard_map/ppermute | solution.py:391
  51.0 2.3 %scatter.1 = f32[616,1024]{1,0:T(8,128)} custom-call(bf16[80,1024]{1,0:T(8,128)(2,1)S(1)} %combine.1.args_0_, bf16[80,1024]{1,0:T(8,128)(2,1)S(1)} %collective-permute-done.4.args_1_, bf16[80,1024]{1,0:T(8,128)(2,1)S(1)} %collective-permute-done.5.args_2_, bf16[80,1024]{1,0:T(8,128)(2,1)S(1)} %collective-permute-done.6.args_3_, ...), custom_call_target="tpu_custom_call" | custom-call | tf_op jit(solution)/shard_map/scatter/pallas_call | solution.py:397
Async XLA Ops:
  2.2 13.5 %collective-permute-start = (bf16[9,32,192]{2,1,0:T(8,128)(2,1)S(1)}, bf16[9,32,192]{2,1,0:T(8,128)(2,1)S(1)}, u32[]{:S(2)}, u32[]{:S(2)}) collective-permute-start(bf16[9,32,192]{2,1,0:T(8,128)(2,1)S(1)} %get-tuple-element.13), channel_id=1, source_target_pairs={{0,16},{16,32},{32,48},{48,64},{64,80},{80,96},{96,112},{112,0},{1... | collective-permute-start | bytes 331784 | tf_op jit(solution)/shard_map/ppermute | solution.py:335
  5.2 10.5 %collective-permute-start.1 = (bf16[9,32,192]{2,1,0:T(8,128)(2,1)S(1)}, bf16[9,32,192]{2,1,0:T(8,128)(2,1)S(1)}, u32[]{:S(2)}, u32[]{:S(2)}) collective-permute-start(bf16[9,32,192]{2,1,0:T(8,128)(2,1)S(1)} %get-tuple-element.14), channel_id=1, source_target_pairs={{16,0},{32,16},{48,32},{64,48},{80,64},{96,80},{112,96},{0,112},{1... | collective-permute-start | bytes 331784 | tf_op jit(solution)/shard_map/ppermute | solution.py:336
  5.2 10.5 %collective-permute-start.2 = (bf16[9,32,192]{2,1,0:T(8,128)(2,1)S(1)}, bf16[9,32,192]{2,1,0:T(8,128)(2,1)S(1)}, u32[]{:S(2)}, u32[]{:S(2)}) collective-permute-start(bf16[9,32,192]{2,1,0:T(8,128)(2,1)S(1)} %get-tuple-element.15), channel_id=1, source_target_pairs={{0,1},{1,2},{2,3},{3,4},{4,5},{5,6},{6,7},{7,8},{8,9},{9,10},{10,1... | collective-permute-start | bytes 331784 | tf_op jit(solution)/shard_map/ppermute | solution.py:337
  6.4 9.3 %collective-permute-start.3 = (bf16[9,32,192]{2,1,0:T(8,128)(2,1)S(1)}, bf16[9,32,192]{2,1,0:T(8,128)(2,1)S(1)}, u32[]{:S(2)}, u32[]{:S(2)}) collective-permute-start(bf16[9,32,192]{2,1,0:T(8,128)(2,1)S(1)} %get-tuple-element.16), channel_id=1, source_target_pairs={{1,0},{2,1},{3,2},{4,3},{5,4},{6,5},{7,6},{8,7},{9,8},{10,9},{11,1... | collective-permute-start | bytes 331784 | tf_op jit(solution)/shard_map/ppermute | solution.py:338
  34.5 8.6 %collective-permute-start.7 = (bf16[80,1024]{1,0:T(8,128)(2,1)S(1)}, bf16[80,1024]{1,0:T(8,128)(2,1)S(1)}, u32[]{:S(2)}, u32[]{:S(2)}) collective-permute-start(bf16[80,1024]{1,0:T(8,128)(2,1)S(1)} %combine.1.args_0_), channel_id=1, source_target_pairs={{0,96},{16,112},{32,0},{48,16},{64,32},{80,48},{96,64},{112,80},{1... | collective-permute-start | bytes 491528 | tf_op jit(solution)/shard_map/ppermute | solution.py:389
  36.9 9.1 %collective-permute-start.6 = (bf16[80,1024]{1,0:T(8,128)(2,1)S(1)}, bf16[80,1024]{1,0:T(8,128)(2,1)S(1)}, u32[]{:S(2)}, u32[]{:S(2)}) collective-permute-start(bf16[80,1024]{1,0:T(8,128)(2,1)S(1)} %combine.1.args_0_), channel_id=1, source_target_pairs={{0,64},{16,80},{32,96},{48,112},{64,0},{80,16},{96,32},{112,48},{1... | collective-permute-start | bytes 491528 | tf_op jit(solution)/shard_map/ppermute | solution.py:389
  38.9 9.4 %collective-permute-start.5 = (bf16[80,1024]{1,0:T(8,128)(2,1)S(1)}, bf16[80,1024]{1,0:T(8,128)(2,1)S(1)}, u32[]{:S(2)}, u32[]{:S(2)}) collective-permute-start(bf16[80,1024]{1,0:T(8,128)(2,1)S(1)} %combine.1.args_0_), channel_id=1, source_target_pairs={{0,32},{16,48},{32,64},{48,80},{64,96},{80,112},{96,0},{112,16},{1... | collective-permute-start | bytes 491528 | tf_op jit(solution)/shard_map/ppermute | solution.py:389
  39.4 10.5 %collective-permute-start.4 = (bf16[80,1024]{1,0:T(8,128)(2,1)S(1)}, bf16[80,1024]{1,0:T(8,128)(2,1)S(1)}, u32[]{:S(2)}, u32[]{:S(2)}) collective-permute-start(bf16[80,1024]{1,0:T(8,128)(2,1)S(1)} %combine.1.args_0_), channel_id=1, source_target_pairs={{0,16},{16,0},{32,48},{48,32},{64,80},{80,64},{96,112},{112,96},{1... | collective-permute-start | bytes 491528 | tf_op jit(solution)/shard_map/ppermute | solution.py:390
  43.1 6.9 %collective-permute-start.10 = (bf16[80,1024]{1,0:T(8,128)(2,1)S(1)}, bf16[80,1024]{1,0:T(8,128)(2,1)S(1)}, u32[]{:S(2)}, u32[]{:S(2)}) collective-permute-start(bf16[80,1024]{1,0:T(8,128)(2,1)S(1)} %collective-permute-done.7.args_4_), channel_id=1, source_target_pairs={{0,16},{16,0},{32,48},{48,32},{64,80},{80,64},{96,112},{112,96},{1... | collective-permute-start | bytes 491528 | tf_op jit(solution)/shard_map/ppermute | solution.py:391
  46.0 4.0 %collective-permute-start.9 = (bf16[80,1024]{1,0:T(8,128)(2,1)S(1)}, bf16[80,1024]{1,0:T(8,128)(2,1)S(1)}, u32[]{:S(2)}, u32[]{:S(2)}) collective-permute-start(bf16[80,1024]{1,0:T(8,128)(2,1)S(1)} %collective-permute-done.6.args_3_), channel_id=1, source_target_pairs={{0,16},{16,0},{32,48},{48,32},{64,80},{80,64},{96,112},{112,96},{1... | collective-permute-start | bytes 491528 | tf_op jit(solution)/shard_map/ppermute | solution.py:391
  48.3 2.7 %collective-permute-start.8 = (bf16[80,1024]{1,0:T(8,128)(2,1)S(1)}, bf16[80,1024]{1,0:T(8,128)(2,1)S(1)}, u32[]{:S(2)}, u32[]{:S(2)}) collective-permute-start(bf16[80,1024]{1,0:T(8,128)(2,1)S(1)} %collective-permute-done.5.args_2_), channel_id=1, source_target_pairs={{0,16},{16,0},{32,48},{48,32},{64,80},{80,64},{96,112},{112,96},{1... | collective-permute-start | bytes 491528 | tf_op jit(solution)/shard_map/ppermute | solution.py:391

commit v6 on v5

--- a/solution.py
+++ b/solution.py
@@ -11,7 +11,7 @@
 LANES = 128
 HALO = 8
 WINDOW = 8
-EARLY = 12
+EARLY = 16
 SAME = 256
 APART = 512
 F32 = jnp.float32
@@ -57,7 +57,7 @@
             new.append(counts[d] + hits[d].astype(jnp.int32))
         return tuple(new)
 
-    lax.fori_loop(0, e_dev, step, (jnp.int32(0),) * 4, unroll=4)
+    lax.fori_loop(0, e_dev, step, (jnp.int32(0),) * 4, unroll=16)
 
 
 def early_kernel(n_dev, rows_own, slot_hbm, nbr_hbm, nagg_hbm, touch_hbm, crow_hbm, a_hbm, p_hbm, out_ref, lefts,
@@ -356,7 +356,7 @@
             pltpu.SemaphoreType.DMA(()),
             pltpu.SemaphoreType.DMA((5,)),
         ],
-        compiler_params=params(14), name="early",
+        compiler_params=params(18), name="early",
     )(*map(pin, (elem_slot.reshape(1, e_dev), nbr.T, nbr_agg.T, touch_agg.T, coarse_row, a_blocks, prolong_t)))
 
     outgoing = pl.pallas_call(
@@ -373,7 +373,7 @@
             pltpu.SemaphoreType.DMA((6,)),
         ],
         compiler_params=params(36), name="products",
-    )(routes, pin(a_blocks), pin(prolong_t), lefts, from_low, from_high, from_left, from_right)
+    )(routes, pin(a_blocks), prolong_t, lefts, from_low, from_high, from_left, from_right)
     incoming = lax.all_to_all(outgoing, "dev", split_axis=0, concat_axis=0, tiled=True)
     piece = 8 * ((BLOCKS * group_rows) // 8 + 1)
 

time: 53.5 us -> 52.8 us (0.987)
  starting transfers between devices: 23.4 us -> 22.5 us
    pallas_call x1, Pallas kernels: 5.5 us -> 6.94 us  [on_device(): pl.pallas_call(early, out_shape=(jax.ShapeDtypeStruct((8, LANES), jnp.int...]
    pallas_call x1, Pallas kernels: 7.82 us -> 6.76 us  [on_device(): pl.pallas_call(main_kernel, out_shape=jax.ShapeDtypeStruct((n_dev, 8, wid...]
    ppermute x3, starting transfers between devices: 4.94 us -> 4.27 us  [on_device(): lax.ppermute(mine, 'grp', [(i, (i + 2 * k) % n_grp) for i in range(n_grp)])]
  transfers between devices with their start and end apart: 11 -> 11, of which waited for: 1 -> 1; matrix products, arithmetic and copies ran while one was open for 0% -> 0% of each run, Pallas kernels for 10% -> 13%
where the time goes in v6:
time: 52.8 us; the launch traced here: 52.6 us
  starting transfers between devices  22.5 us (43%)
  Pallas kernels  18.3 us (35%)
  blocking collectives  10.7 us (20%)
  waiting for transfers between devices  1.04 us (2%)
    all_to_all x1, blocking collectives, on_device(): lax.all_to_all(outgoing, 'dev', split_axis=0, concat_axis=0, tiled=True)  10.7 us
    ppermute x3, starting transfers between devices, on_device(): others = [lax.ppermute(part, 'grp', swap) for part in across]  7.02 us
    pallas_call x1, Pallas kernels, on_device(): pl.pallas_call(early, out_shape=(jax.ShapeDtypeStruct((8, LANES), jnp.int...  6.94 us
    pallas_call x1, Pallas kernels, on_device(): pl.pallas_call(main_kernel, out_shape=jax.ShapeDtypeStruct((n_dev, 8, wid...  6.76 us
    ppermute x3, starting transfers between devices, on_device(): lax.ppermute(mine, 'grp', [(i, (i + 2 * k) % n_grp) for i in range(n_grp)])  4.27 us
    ppermute x1, starting transfers between devices, on_device(): from_right = lax.ppermute(packed[2], 'dev', down(n_dev))  3.72 us
    ppermute x1, starting transfers between devices, on_device(): twin = lax.ppermute(mine, 'grp', swap)  3.23 us
    ppermute x1, starting transfers between devices, on_device(): from_low = lax.ppermute(packed[1], 'grp', up(n_grp))  3.04 us
  transfers between devices with their start and end apart: 11, of which 1 were waited for; matrix products, arithmetic and copies ran while one was open for 0% of the time, Pallas kernels for 13%

profile of v6, /device:TPU:1, one launch (start us, length us, event | category | flops | bytes accessed | tf_op | source)
XLA Modules:
  0.0 52.6 jit_solution(8044568310843127039)
XLA Ops:
  0.0 2.0 %pack.1 = (bf16[9,32,192]{2,1,0:T(8,128)(2,1)S(1)}, bf16[9,32,192]{2,1,0:T(8,128)(2,1)S(1)}, bf16[9,32,192]{2,1,0:T(8,128)(2,1)S(1)}, bf16[9,32,192]{2,1,0:T(8,128)(2,1)S(1)}) custom-call(s32[6,32]{1,0:T(8,128)} %bitcast.9, bf16[32,32,192]{2,1,0:T(8,128)(2,1)} %p_hbm.1), custom_call_target="tpu_custom_call" | custom-call | tf_op jit(solution)/shard_map/pack/pallas_call | solution.py:327
  2.0 3.0 %collective-permute-start = (bf16[9,32,192]{2,1,0:T(8,128)(2,1)S(1)}, bf16[9,32,192]{2,1,0:T(8,128)(2,1)S(1)}, u32[]{:S(2)}, u32[]{:S(2)}) collective-permute-start(bf16[9,32,192]{2,1,0:T(8,128)(2,1)S(1)} %get-tuple-element.13), channel_id=1, source_target_pairs={{0,16},{16,32},{32,48},{48,64},{64,80},{80,96},{96,112},{112,0},{1... | collective-permute-start | bytes 331784 | tf_op jit(solution)/shard_map/ppermute | solution.py:335
  5.0 0.0 collective-permute-start.1
  5.0 1.2 %collective-permute-start.2 = (bf16[9,32,192]{2,1,0:T(8,128)(2,1)S(1)}, bf16[9,32,192]{2,1,0:T(8,128)(2,1)S(1)}, u32[]{:S(2)}, u32[]{:S(2)}) collective-permute-start(bf16[9,32,192]{2,1,0:T(8,128)(2,1)S(1)} %get-tuple-element.15), channel_id=1, source_target_pairs={{0,1},{1,2},{2,3},{3,4},{4,5},{5,6},{6,7},{7,8},{8,9},{9,10},{10,1... | collective-permute-start | bytes 331784 | tf_op jit(solution)/shard_map/ppermute | solution.py:337
  6.2 3.7 %collective-permute-start.3 = (bf16[9,32,192]{2,1,0:T(8,128)(2,1)S(1)}, bf16[9,32,192]{2,1,0:T(8,128)(2,1)S(1)}, u32[]{:S(2)}, u32[]{:S(2)}) collective-permute-start(bf16[9,32,192]{2,1,0:T(8,128)(2,1)S(1)} %get-tuple-element.16), channel_id=1, source_target_pairs={{1,0},{2,1},{3,2},{4,3},{5,4},{6,5},{7,6},{8,7},{9,8},{10,9},{11,1... | collective-permute-start | bytes 331784 | tf_op jit(solution)/shard_map/ppermute | solution.py:338
  10.0 0.0 copy-start
  10.0 6.9 %early.1 = (s32[8,128]{1,0:T(8,128)S(1)}, bf16[16,7,32,192]{3,2,1,0:T(8,128)(2,1)S(1)}) custom-call(s32[1,32]{1,0:T(1,128)} %bitcast.13, s32[6,32]{1,0:T(8,128)} %bitcast.10, s32[6,32]{1,0:T(8,128)} %bitcast.11, s32[6,128]{1,0:T(8,128)} %bitcast.12, s32[528]{0:T(1024)} %args_4_.4, bf16[32,7,192,192]{3,2,1,0:T(8,128)(2,1)} %a_hbm.1, bf16[32,32,192]{2,1,0:T(8,128)(2,1)} %p_hbm.1), custom_call_target="tpu_custom_call" | custom-call | tf_op jit(solution)/shard_map/early/pallas_call | solution.py:343
  16.9 0.0 collective-permute-done.h0
  16.9 0.0 collective-permute-done.1.h1
  16.9 0.0 collective-permute-done.2.h2
  16.9 0.0 collective-permute-done.3.h3
  17.0 0.0 copy-done
  17.0 6.8 %products.1 = bf16[16,8,1024]{2,1,0:T(8,128)(2,1)S(1)} custom-call(s32[8,128]{1,0:T(8,128)S(1)} %get-tuple-element.11.route_hbm, bf16[32,7,192,192]{3,2,1,0:T(8,128)(2,1)} %a_hbm.1, bf16[32,32,192]{2,1,0:T(8,128)(2,1)S(1)} %copy-done, bf16[16,7,32,192]{3,2,1,0:T(8,128)(2,1)S(1)} %get-tuple-element.12.done, bf16[9,32,192]{2,1,0:T(8,128)(2,1)S(1)} %collective-permute-done.h0, ...), custom_call_target="tpu_custom_call" | custom-call | tf_op jit(solution)/shard_map/products/pallas_call | solution.py:362
  23.7 10.7 %all_to_all.5 = bf16[16,8,1024]{2,1,0:T(8,128)(2,1)S(1)} all-to-all(bf16[16,8,1024]{2,1,0:T(8,128)(2,1)S(1)} %products.1), channel_id=1, replica_groups=mesh['grp'=8,'dev'=16] {'dev'}, dimensions={0} | all-to-all | bytes 524288 | tf_op jit(solution)/shard_map/all_to_all | solution.py:377
  34.4 0.3 combine.1.args_0_
  34.8 2.3 %collective-permute-start.7 = (bf16[80,1024]{1,0:T(8,128)(2,1)S(1)}, bf16[80,1024]{1,0:T(8,128)(2,1)S(1)}, u32[]{:S(2)}, u32[]{:S(2)}) collective-permute-start(bf16[80,1024]{1,0:T(8,128)(2,1)S(1)} %combine.1.args_0_), channel_id=1, source_target_pairs={{0,96},{16,112},{32,0},{48,16},{64,32},{80,48},{96,64},{112,80},{1... | collective-permute-start | bytes 491528 | tf_op jit(solution)/shard_map/ppermute | solution.py:389
  37.1 1.2 %collective-permute-start.6 = (bf16[80,1024]{1,0:T(8,128)(2,1)S(1)}, bf16[80,1024]{1,0:T(8,128)(2,1)S(1)}, u32[]{:S(2)}, u32[]{:S(2)}) collective-permute-start(bf16[80,1024]{1,0:T(8,128)(2,1)S(1)} %combine.1.args_0_), channel_id=1, source_target_pairs={{0,64},{16,80},{32,96},{48,112},{64,0},{80,16},{96,32},{112,48},{1... | collective-permute-start | bytes 491528 | tf_op jit(solution)/shard_map/ppermute | solution.py:389
  38.3 0.8 %collective-permute-start.5 = (bf16[80,1024]{1,0:T(8,128)(2,1)S(1)}, bf16[80,1024]{1,0:T(8,128)(2,1)S(1)}, u32[]{:S(2)}, u32[]{:S(2)}) collective-permute-start(bf16[80,1024]{1,0:T(8,128)(2,1)S(1)} %combine.1.args_0_), channel_id=1, source_target_pairs={{0,32},{16,48},{32,64},{48,80},{64,96},{80,112},{96,0},{112,16},{1... | collective-permute-start | bytes 491528 | tf_op jit(solution)/shard_map/ppermute | solution.py:389
  39.0 3.2 %collective-permute-start.4 = (bf16[80,1024]{1,0:T(8,128)(2,1)S(1)}, bf16[80,1024]{1,0:T(8,128)(2,1)S(1)}, u32[]{:S(2)}, u32[]{:S(2)}) collective-permute-start(bf16[80,1024]{1,0:T(8,128)(2,1)S(1)} %combine.1.args_0_), channel_id=1, source_target_pairs={{0,16},{16,0},{32,48},{48,32},{64,80},{80,64},{96,112},{112,96},{1... | collective-permute-start | bytes 491528 | tf_op jit(solution)/shard_map/ppermute | solution.py:390
  42.3 0.0 collective-permute-done.7.args_4_
  42.3 3.4 %collective-permute-start.10 = (bf16[80,1024]{1,0:T(8,128)(2,1)S(1)}, bf16[80,1024]{1,0:T(8,128)(2,1)S(1)}, u32[]{:S(2)}, u32[]{:S(2)}) collective-permute-start(bf16[80,1024]{1,0:T(8,128)(2,1)S(1)} %collective-permute-done.7.args_4_), channel_id=1, source_target_pairs={{0,16},{16,0},{32,48},{48,32},{64,80},{80,64},{96,112},{112,96},{1... | collective-permute-start | bytes 491528 | tf_op jit(solution)/shard_map/ppermute | solution.py:391
  45.6 0.0 collective-permute-done.6.args_3_
  45.6 2.3 %collective-permute-start.9 = (bf16[80,1024]{1,0:T(8,128)(2,1)S(1)}, bf16[80,1024]{1,0:T(8,128)(2,1)S(1)}, u32[]{:S(2)}, u32[]{:S(2)}) collective-permute-start(bf16[80,1024]{1,0:T(8,128)(2,1)S(1)} %collective-permute-done.6.args_3_), channel_id=1, source_target_pairs={{0,16},{16,0},{32,48},{48,32},{64,80},{80,64},{96,112},{112,96},{1... | collective-permute-start | bytes 491528 | tf_op jit(solution)/shard_map/ppermute | solution.py:391
  47.9 0.0 collective-permute-done.5.args_2_
  47.9 1.4 %collective-permute-start.8 = (bf16[80,1024]{1,0:T(8,128)(2,1)S(1)}, bf16[80,1024]{1,0:T(8,128)(2,1)S(1)}, u32[]{:S(2)}, u32[]{:S(2)}) collective-permute-start(bf16[80,1024]{1,0:T(8,128)(2,1)S(1)} %collective-permute-done.5.args_2_), channel_id=1, source_target_pairs={{0,16},{16,0},{32,48},{48,32},{64,80},{80,64},{96,112},{112,96},{1... | collective-permute-start | bytes 491528 | tf_op jit(solution)/shard_map/ppermute | solution.py:391
  49.3 0.0 collective-permute-done.4.args_1_
  49.3 0.0 collective-permute-done.10.args_7_
  49.3 0.0 collective-permute-done.9.args_6_
  49.3 1.0 %collective-permute-done.8.args_5_ = bf16[80,1024]{1,0:T(8,128)(2,1)S(1)} collective-permute-done((bf16[80,1024]{1,0:T(8,128)(2,1)S(1)}, bf16[80,1024]{1,0:T(8,128)(2,1)S(1)}, u32[]{:S(2)}, u32[]{:S(2)}) %collective-permute-start.8) | collective-permute-done | bytes 163872 | tf_op jit(solution)/shard_map/ppermute | solution.py:391
  50.3 2.3 %scatter.1 = f32[616,1024]{1,0:T(8,128)} custom-call(bf16[80,1024]{1,0:T(8,128)(2,1)S(1)} %combine.1.args_0_, bf16[80,1024]{1,0:T(8,128)(2,1)S(1)} %collective-permute-done.4.args_1_, bf16[80,1024]{1,0:T(8,128)(2,1)S(1)} %collective-permute-done.5.args_2_, bf16[80,1024]{1,0:T(8,128)(2,1)S(1)} %collective-permute-done.6.args_3_, ...), custom_call_target="tpu_custom_call" | custom-call | tf_op jit(solution)/shard_map/scatter/pallas_call | solution.py:397
Async XLA Ops:
  2.0 14.9 %collective-permute-start = (bf16[9,32,192]{2,1,0:T(8,128)(2,1)S(1)}, bf16[9,32,192]{2,1,0:T(8,128)(2,1)S(1)}, u32[]{:S(2)}, u32[]{:S(2)}) collective-permute-start(bf16[9,32,192]{2,1,0:T(8,128)(2,1)S(1)} %get-tuple-element.13), channel_id=1, source_target_pairs={{0,16},{16,32},{32,48},{48,64},{64,80},{80,96},{96,112},{112,0},{1... | collective-permute-start | bytes 331784 | tf_op jit(solution)/shard_map/ppermute | solution.py:335
  5.0 11.9 %collective-permute-start.1 = (bf16[9,32,192]{2,1,0:T(8,128)(2,1)S(1)}, bf16[9,32,192]{2,1,0:T(8,128)(2,1)S(1)}, u32[]{:S(2)}, u32[]{:S(2)}) collective-permute-start(bf16[9,32,192]{2,1,0:T(8,128)(2,1)S(1)} %get-tuple-element.14), channel_id=1, source_target_pairs={{16,0},{32,16},{48,32},{64,48},{80,64},{96,80},{112,96},{0,112},{1... | collective-permute-start | bytes 331784 | tf_op jit(solution)/shard_map/ppermute | solution.py:336
  5.0 11.9 %collective-permute-start.2 = (bf16[9,32,192]{2,1,0:T(8,128)(2,1)S(1)}, bf16[9,32,192]{2,1,0:T(8,128)(2,1)S(1)}, u32[]{:S(2)}, u32[]{:S(2)}) collective-permute-start(bf16[9,32,192]{2,1,0:T(8,128)(2,1)S(1)} %get-tuple-element.15), channel_id=1, source_target_pairs={{0,1},{1,2},{2,3},{3,4},{4,5},{5,6},{6,7},{7,8},{8,9},{9,10},{10,1... | collective-permute-start | bytes 331784 | tf_op jit(solution)/shard_map/ppermute | solution.py:337
  6.2 10.7 %collective-permute-start.3 = (bf16[9,32,192]{2,1,0:T(8,128)(2,1)S(1)}, bf16[9,32,192]{2,1,0:T(8,128)(2,1)S(1)}, u32[]{:S(2)}, u32[]{:S(2)}) collective-permute-start(bf16[9,32,192]{2,1,0:T(8,128)(2,1)S(1)} %get-tuple-element.16), channel_id=1, source_target_pairs={{1,0},{2,1},{3,2},{4,3},{5,4},{6,5},{7,6},{8,7},{9,8},{10,9},{11,1... | collective-permute-start | bytes 331784 | tf_op jit(solution)/shard_map/ppermute | solution.py:338
  10.0 7.0 %copy-start = (bf16[32,32,192]{2,1,0:T(8,128)(2,1)S(1)}, bf16[32,32,192]{2,1,0:T(8,128)(2,1)}, u32[]{:S(2)}) copy-start(bf16[32,32,192]{2,1,0:T(8,128)(2,1)} %p_hbm.1) | copy-start | bytes 1179652
  34.8 7.5 %collective-permute-start.7 = (bf16[80,1024]{1,0:T(8,128)(2,1)S(1)}, bf16[80,1024]{1,0:T(8,128)(2,1)S(1)}, u32[]{:S(2)}, u32[]{:S(2)}) collective-permute-start(bf16[80,1024]{1,0:T(8,128)(2,1)S(1)} %combine.1.args_0_), channel_id=1, source_target_pairs={{0,96},{16,112},{32,0},{48,16},{64,32},{80,48},{96,64},{112,80},{1... | collective-permute-start | bytes 491528 | tf_op jit(solution)/shard_map/ppermute | solution.py:389
  37.1 8.6 %collective-permute-start.6 = (bf16[80,1024]{1,0:T(8,128)(2,1)S(1)}, bf16[80,1024]{1,0:T(8,128)(2,1)S(1)}, u32[]{:S(2)}, u32[]{:S(2)}) collective-permute-start(bf16[80,1024]{1,0:T(8,128)(2,1)S(1)} %combine.1.args_0_), channel_id=1, source_target_pairs={{0,64},{16,80},{32,96},{48,112},{64,0},{80,16},{96,32},{112,48},{1... | collective-permute-start | bytes 491528 | tf_op jit(solution)/shard_map/ppermute | solution.py:389
  38.3 9.7 %collective-permute-start.5 = (bf16[80,1024]{1,0:T(8,128)(2,1)S(1)}, bf16[80,1024]{1,0:T(8,128)(2,1)S(1)}, u32[]{:S(2)}, u32[]{:S(2)}) collective-permute-start(bf16[80,1024]{1,0:T(8,128)(2,1)S(1)} %combine.1.args_0_), channel_id=1, source_target_pairs={{0,32},{16,48},{32,64},{48,80},{64,96},{80,112},{96,0},{112,16},{1... | collective-permute-start | bytes 491528 | tf_op jit(solution)/shard_map/ppermute | solution.py:389
  39.0 10.3 %collective-permute-start.4 = (bf16[80,1024]{1,0:T(8,128)(2,1)S(1)}, bf16[80,1024]{1,0:T(8,128)(2,1)S(1)}, u32[]{:S(2)}, u32[]{:S(2)}) collective-permute-start(bf16[80,1024]{1,0:T(8,128)(2,1)S(1)} %combine.1.args_0_), channel_id=1, source_target_pairs={{0,16},{16,0},{32,48},{48,32},{64,80},{80,64},{96,112},{112,96},{1... | collective-permute-start | bytes 491528 | tf_op jit(solution)/shard_map/ppermute | solution.py:390
  42.3 7.0 %collective-permute-start.10 = (bf16[80,1024]{1,0:T(8,128)(2,1)S(1)}, bf16[80,1024]{1,0:T(8,128)(2,1)S(1)}, u32[]{:S(2)}, u32[]{:S(2)}) collective-permute-start(bf16[80,1024]{1,0:T(8,128)(2,1)S(1)} %collective-permute-done.7.args_4_), channel_id=1, source_target_pairs={{0,16},{16,0},{32,48},{48,32},{64,80},{80,64},{96,112},{112,96},{1... | collective-permute-start | bytes 491528 | tf_op jit(solution)/shard_map/ppermute | solution.py:391
  45.6 3.7 %collective-permute-start.9 = (bf16[80,1024]{1,0:T(8,128)(2,1)S(1)}, bf16[80,1024]{1,0:T(8,128)(2,1)S(1)}, u32[]{:S(2)}, u32[]{:S(2)}) collective-permute-start(bf16[80,1024]{1,0:T(8,128)(2,1)S(1)} %collective-permute-done.6.args_3_), channel_id=1, source_target_pairs={{0,16},{16,0},{32,48},{48,32},{64,80},{80,64},{96,112},{112,96},{1... | collective-permute-start | bytes 491528 | tf_op jit(solution)/shard_map/ppermute | solution.py:391
  47.9 2.4 %collective-permute-start.8 = (bf16[80,1024]{1,0:T(8,128)(2,1)S(1)}, bf16[80,1024]{1,0:T(8,128)(2,1)S(1)}, u32[]{:S(2)}, u32[]{:S(2)}) collective-permute-start(bf16[80,1024]{1,0:T(8,128)(2,1)S(1)} %collective-permute-done.5.args_2_), channel_id=1, source_target_pairs={{0,16},{16,0},{32,48},{48,32},{64,80},{80,64},{96,112},{112,96},{1... | collective-permute-start | bytes 491528 | tf_op jit(solution)/shard_map/ppermute | solution.py:391

commit v7 on v6

--- a/solution.py
+++ b/solution.py
@@ -11,7 +11,7 @@
 LANES = 128
 HALO = 8
 WINDOW = 8
-EARLY = 16
+EARLY = 20
 SAME = 256
 APART = 512
 F32 = jnp.float32
@@ -356,7 +356,7 @@
             pltpu.SemaphoreType.DMA(()),
             pltpu.SemaphoreType.DMA((5,)),
         ],
-        compiler_params=params(18), name="early",
+        compiler_params=params(24), name="early",
     )(*map(pin, (elem_slot.reshape(1, e_dev), nbr.T, nbr_agg.T, touch_agg.T, coarse_row, a_blocks, prolong_t)))
 
     outgoing = pl.pallas_call(
@@ -401,7 +401,7 @@
             pltpu.VMEM((n_grp * piece, width), BF16),
             pltpu.VMEM((BLOCKS * rows_own, n_grp * piece), BF16),
             pltpu.VMEM((BLOCKS * rows_own, width), F32),
-            pltpu.SemaphoreType.DMA((4,)),
+            pltpu.SemaphoreType.DMA((2,)),
         ],
         compiler_params=params(16), name="scatter",
     )(*pieces)

time: 52.8 us -> 53.4 us (1.011)
  Pallas kernels: 18.3 us -> 18.9 us
    pallas_call x1, Pallas kernels: 6.94 us -> 8.41 us  [on_device(): pl.pallas_call(early, out_shape=(jax.ShapeDtypeStruct((8, LANES), jnp.int...]
    pallas_call x1, Pallas kernels: 6.76 us -> 5.94 us  [on_device(): pl.pallas_call(main_kernel, out_shape=jax.ShapeDtypeStruct((n_dev, 8, wid...]
  transfers between devices with their start and end apart: 11 -> 11, of which waited for: 1 -> 1; matrix products, arithmetic and copies ran while one was open for 0% -> 0% of each run, Pallas kernels for 13% -> 16%
where the time goes in v7:
time: 53.4 us; the launch traced here: 53.2 us
  starting transfers between devices  22.5 us (42%)
  Pallas kernels  18.9 us (35%)
  blocking collectives  10.7 us (20%)
  waiting for transfers between devices  1.04 us (2%)
    all_to_all x1, blocking collectives, on_device(): lax.all_to_all(outgoing, 'dev', split_axis=0, concat_axis=0, tiled=True)  10.7 us
    pallas_call x1, Pallas kernels, on_device(): pl.pallas_call(early, out_shape=(jax.ShapeDtypeStruct((8, LANES), jnp.int...  8.41 us
    ppermute x3, starting transfers between devices, on_device(): others = [lax.ppermute(part, 'grp', swap) for part in across]  7.01 us
    pallas_call x1, Pallas kernels, on_device(): pl.pallas_call(main_kernel, out_shape=jax.ShapeDtypeStruct((n_dev, 8, wid...  5.94 us
    ppermute x3, starting transfers between devices, on_device(): lax.ppermute(mine, 'grp', [(i, (i + 2 * k) % n_grp) for i in range(n_grp)])  4.25 us
    ppermute x1, starting transfers between devices, on_device(): from_right = lax.ppermute(packed[2], 'dev', down(n_dev))  3.72 us
    ppermute x1, starting transfers between devices, on_device(): twin = lax.ppermute(mine, 'grp', swap)  3.25 us
    ppermute x1, starting transfers between devices, on_device(): from_low = lax.ppermute(packed[1], 'grp', up(n_grp))  3.04 us
  transfers between devices with their start and end apart: 11, of which 1 were waited for; matrix products, arithmetic and copies ran while one was open for 0% of the time, Pallas kernels for 16%

profile of v7, /device:TPU:1, one launch (start us, length us, event | category | flops | bytes accessed | tf_op | source)
XLA Modules:
  0.0 53.2 jit_solution(15941804118354362365)
XLA Ops:
  0.0 2.0 %pack.1 = (bf16[9,32,192]{2,1,0:T(8,128)(2,1)S(1)}, bf16[9,32,192]{2,1,0:T(8,128)(2,1)S(1)}, bf16[9,32,192]{2,1,0:T(8,128)(2,1)S(1)}, bf16[9,32,192]{2,1,0:T(8,128)(2,1)S(1)}) custom-call(s32[6,32]{1,0:T(8,128)} %bitcast.9, bf16[32,32,192]{2,1,0:T(8,128)(2,1)} %p_hbm.1), custom_call_target="tpu_custom_call" | custom-call | tf_op jit(solution)/shard_map/pack/pallas_call | solution.py:327
  2.0 3.0 %collective-permute-start = (bf16[9,32,192]{2,1,0:T(8,128)(2,1)S(1)}, bf16[9,32,192]{2,1,0:T(8,128)(2,1)S(1)}, u32[]{:S(2)}, u32[]{:S(2)}) collective-permute-start(bf16[9,32,192]{2,1,0:T(8,128)(2,1)S(1)} %get-tuple-element.13), channel_id=1, source_target_pairs={{0,16},{16,32},{32,48},{48,64},{64,80},{80,96},{96,112},{112,0},{1... | collective-permute-start | bytes 331784 | tf_op jit(solution)/shard_map/ppermute | solution.py:335
  5.0 0.0 collective-permute-start.1
  5.0 1.2 %collective-permute-start.2 = (bf16[9,32,192]{2,1,0:T(8,128)(2,1)S(1)}, bf16[9,32,192]{2,1,0:T(8,128)(2,1)S(1)}, u32[]{:S(2)}, u32[]{:S(2)}) collective-permute-start(bf16[9,32,192]{2,1,0:T(8,128)(2,1)S(1)} %get-tuple-element.15), channel_id=1, source_target_pairs={{0,1},{1,2},{2,3},{3,4},{4,5},{5,6},{6,7},{7,8},{8,9},{9,10},{10,1... | collective-permute-start | bytes 331784 | tf_op jit(solution)/shard_map/ppermute | solution.py:337
  6.2 3.7 %collective-permute-start.3 = (bf16[9,32,192]{2,1,0:T(8,128)(2,1)S(1)}, bf16[9,32,192]{2,1,0:T(8,128)(2,1)S(1)}, u32[]{:S(2)}, u32[]{:S(2)}) collective-permute-start(bf16[9,32,192]{2,1,0:T(8,128)(2,1)S(1)} %get-tuple-element.16), channel_id=1, source_target_pairs={{1,0},{2,1},{3,2},{4,3},{5,4},{6,5},{7,6},{8,7},{9,8},{10,9},{11,1... | collective-permute-start | bytes 331784 | tf_op jit(solution)/shard_map/ppermute | solution.py:338
  10.0 0.0 copy-start
  10.0 8.4 %early.1 = (s32[8,128]{1,0:T(8,128)S(1)}, bf16[20,7,32,192]{3,2,1,0:T(8,128)(2,1)S(1)}) custom-call(s32[1,32]{1,0:T(1,128)} %bitcast.13, s32[6,32]{1,0:T(8,128)} %bitcast.10, s32[6,32]{1,0:T(8,128)} %bitcast.11, s32[6,128]{1,0:T(8,128)} %bitcast.12, s32[528]{0:T(1024)} %args_4_.4, bf16[32,7,192,192]{3,2,1,0:T(8,128)(2,1)} %a_hbm.1, bf16[32,32,192]{2,1,0:T(8,128)(2,1)} %p_hbm.1), custom_call_target="tpu_custom_call" | custom-call | tf_op jit(solution)/shard_map/early/pallas_call | solution.py:343
  18.4 0.0 collective-permute-done.h0
  18.4 0.0 collective-permute-done.1.h1
  18.4 0.0 collective-permute-done.2.h2
  18.4 0.0 collective-permute-done.3.h3
  18.4 0.0 copy-done
  18.4 5.9 %products.1 = bf16[16,8,1024]{2,1,0:T(8,128)(2,1)S(1)} custom-call(s32[8,128]{1,0:T(8,128)S(1)} %get-tuple-element.11.route_hbm, bf16[32,7,192,192]{3,2,1,0:T(8,128)(2,1)} %a_hbm.1, bf16[32,32,192]{2,1,0:T(8,128)(2,1)S(1)} %copy-done, bf16[20,7,32,192]{3,2,1,0:T(8,128)(2,1)S(1)} %get-tuple-element.12.done, bf16[9,32,192]{2,1,0:T(8,128)(2,1)S(1)} %collective-permute-done.h0, ...), custom_call_target="tpu_custom_call" | custom-call | tf_op jit(solution)/shard_map/products/pallas_call | solution.py:362
  24.4 10.7 %all_to_all.5 = bf16[16,8,1024]{2,1,0:T(8,128)(2,1)S(1)} all-to-all(bf16[16,8,1024]{2,1,0:T(8,128)(2,1)S(1)} %products.1), channel_id=1, replica_groups=mesh['grp'=8,'dev'=16] {'dev'}, dimensions={0} | all-to-all | bytes 524288 | tf_op jit(solution)/shard_map/all_to_all | solution.py:377
  35.1 0.3 combine.1.args_0_
  35.4 2.3 %collective-permute-start.7 = (bf16[80,1024]{1,0:T(8,128)(2,1)S(1)}, bf16[80,1024]{1,0:T(8,128)(2,1)S(1)}, u32[]{:S(2)}, u32[]{:S(2)}) collective-permute-start(bf16[80,1024]{1,0:T(8,128)(2,1)S(1)} %combine.1.args_0_), channel_id=1, source_target_pairs={{0,96},{16,112},{32,0},{48,16},{64,32},{80,48},{96,64},{112,80},{1... | collective-permute-start | bytes 491528 | tf_op jit(solution)/shard_map/ppermute | solution.py:389
  37.7 1.2 %collective-permute-start.6 = (bf16[80,1024]{1,0:T(8,128)(2,1)S(1)}, bf16[80,1024]{1,0:T(8,128)(2,1)S(1)}, u32[]{:S(2)}, u32[]{:S(2)}) collective-permute-start(bf16[80,1024]{1,0:T(8,128)(2,1)S(1)} %combine.1.args_0_), channel_id=1, source_target_pairs={{0,64},{16,80},{32,96},{48,112},{64,0},{80,16},{96,32},{112,48},{1... | collective-permute-start | bytes 491528 | tf_op jit(solution)/shard_map/ppermute | solution.py:389
  38.9 0.8 %collective-permute-start.5 = (bf16[80,1024]{1,0:T(8,128)(2,1)S(1)}, bf16[80,1024]{1,0:T(8,128)(2,1)S(1)}, u32[]{:S(2)}, u32[]{:S(2)}) collective-permute-start(bf16[80,1024]{1,0:T(8,128)(2,1)S(1)} %combine.1.args_0_), channel_id=1, source_target_pairs={{0,32},{16,48},{32,64},{48,80},{64,96},{80,112},{96,0},{112,16},{1... | collective-permute-start | bytes 491528 | tf_op jit(solution)/shard_map/ppermute | solution.py:389
  39.7 3.3 %collective-permute-start.4 = (bf16[80,1024]{1,0:T(8,128)(2,1)S(1)}, bf16[80,1024]{1,0:T(8,128)(2,1)S(1)}, u32[]{:S(2)}, u32[]{:S(2)}) collective-permute-start(bf16[80,1024]{1,0:T(8,128)(2,1)S(1)} %combine.1.args_0_), channel_id=1, source_target_pairs={{0,16},{16,0},{32,48},{48,32},{64,80},{80,64},{96,112},{112,96},{1... | collective-permute-start | bytes 491528 | tf_op jit(solution)/shard_map/ppermute | solution.py:390
  42.9 0.0 collective-permute-done.7.args_4_
  42.9 3.4 %collective-permute-start.10 = (bf16[80,1024]{1,0:T(8,128)(2,1)S(1)}, bf16[80,1024]{1,0:T(8,128)(2,1)S(1)}, u32[]{:S(2)}, u32[]{:S(2)}) collective-permute-start(bf16[80,1024]{1,0:T(8,128)(2,1)S(1)} %collective-permute-done.7.args_4_), channel_id=1, source_target_pairs={{0,16},{16,0},{32,48},{48,32},{64,80},{80,64},{96,112},{112,96},{1... | collective-permute-start | bytes 491528 | tf_op jit(solution)/shard_map/ppermute | solution.py:391
  46.3 0.0 collective-permute-done.6.args_3_
  46.3 2.3 %collective-permute-start.9 = (bf16[80,1024]{1,0:T(8,128)(2,1)S(1)}, bf16[80,1024]{1,0:T(8,128)(2,1)S(1)}, u32[]{:S(2)}, u32[]{:S(2)}) collective-permute-start(bf16[80,1024]{1,0:T(8,128)(2,1)S(1)} %collective-permute-done.6.args_3_), channel_id=1, source_target_pairs={{0,16},{16,0},{32,48},{48,32},{64,80},{80,64},{96,112},{112,96},{1... | collective-permute-start | bytes 491528 | tf_op jit(solution)/shard_map/ppermute | solution.py:391
  48.6 0.0 collective-permute-done.5.args_2_
  48.6 1.4 %collective-permute-start.8 = (bf16[80,1024]{1,0:T(8,128)(2,1)S(1)}, bf16[80,1024]{1,0:T(8,128)(2,1)S(1)}, u32[]{:S(2)}, u32[]{:S(2)}) collective-permute-start(bf16[80,1024]{1,0:T(8,128)(2,1)S(1)} %collective-permute-done.5.args_2_), channel_id=1, source_target_pairs={{0,16},{16,0},{32,48},{48,32},{64,80},{80,64},{96,112},{112,96},{1... | collective-permute-start | bytes 491528 | tf_op jit(solution)/shard_map/ppermute | solution.py:391
  49.9 0.0 collective-permute-done.4.args_1_
  49.9 0.0 collective-permute-done.10.args_7_
  50.0 0.0 collective-permute-done.9.args_6_
  50.0 1.0 %collective-permute-done.8.args_5_ = bf16[80,1024]{1,0:T(8,128)(2,1)S(1)} collective-permute-done((bf16[80,1024]{1,0:T(8,128)(2,1)S(1)}, bf16[80,1024]{1,0:T(8,128)(2,1)S(1)}, u32[]{:S(2)}, u32[]{:S(2)}) %collective-permute-start.8) | collective-permute-done | bytes 163872 | tf_op jit(solution)/shard_map/ppermute | solution.py:391
  51.0 2.2 %scatter.1 = f32[616,1024]{1,0:T(8,128)} custom-call(bf16[80,1024]{1,0:T(8,128)(2,1)S(1)} %combine.1.args_0_, bf16[80,1024]{1,0:T(8,128)(2,1)S(1)} %collective-permute-done.4.args_1_, bf16[80,1024]{1,0:T(8,128)(2,1)S(1)} %collective-permute-done.5.args_2_, bf16[80,1024]{1,0:T(8,128)(2,1)S(1)} %collective-permute-done.6.args_3_, ...), custom_call_target="tpu_custom_call" | custom-call | tf_op jit(solution)/shard_map/scatter/pallas_call | solution.py:397
Async XLA Ops:
  2.0 16.4 %collective-permute-start = (bf16[9,32,192]{2,1,0:T(8,128)(2,1)S(1)}, bf16[9,32,192]{2,1,0:T(8,128)(2,1)S(1)}, u32[]{:S(2)}, u32[]{:S(2)}) collective-permute-start(bf16[9,32,192]{2,1,0:T(8,128)(2,1)S(1)} %get-tuple-element.13), channel_id=1, source_target_pairs={{0,16},{16,32},{32,48},{48,64},{64,80},{80,96},{96,112},{112,0},{1... | collective-permute-start | bytes 331784 | tf_op jit(solution)/shard_map/ppermute | solution.py:335
  5.0 13.4 %collective-permute-start.1 = (bf16[9,32,192]{2,1,0:T(8,128)(2,1)S(1)}, bf16[9,32,192]{2,1,0:T(8,128)(2,1)S(1)}, u32[]{:S(2)}, u32[]{:S(2)}) collective-permute-start(bf16[9,32,192]{2,1,0:T(8,128)(2,1)S(1)} %get-tuple-element.14), channel_id=1, source_target_pairs={{16,0},{32,16},{48,32},{64,48},{80,64},{96,80},{112,96},{0,112},{1... | collective-permute-start | bytes 331784 | tf_op jit(solution)/shard_map/ppermute | solution.py:336
  5.0 13.4 %collective-permute-start.2 = (bf16[9,32,192]{2,1,0:T(8,128)(2,1)S(1)}, bf16[9,32,192]{2,1,0:T(8,128)(2,1)S(1)}, u32[]{:S(2)}, u32[]{:S(2)}) collective-permute-start(bf16[9,32,192]{2,1,0:T(8,128)(2,1)S(1)} %get-tuple-element.15), channel_id=1, source_target_pairs={{0,1},{1,2},{2,3},{3,4},{4,5},{5,6},{6,7},{7,8},{8,9},{9,10},{10,1... | collective-permute-start | bytes 331784 | tf_op jit(solution)/shard_map/ppermute | solution.py:337
  6.2 12.2 %collective-permute-start.3 = (bf16[9,32,192]{2,1,0:T(8,128)(2,1)S(1)}, bf16[9,32,192]{2,1,0:T(8,128)(2,1)S(1)}, u32[]{:S(2)}, u32[]{:S(2)}) collective-permute-start(bf16[9,32,192]{2,1,0:T(8,128)(2,1)S(1)} %get-tuple-element.16), channel_id=1, source_target_pairs={{1,0},{2,1},{3,2},{4,3},{5,4},{6,5},{7,6},{8,7},{9,8},{10,9},{11,1... | collective-permute-start | bytes 331784 | tf_op jit(solution)/shard_map/ppermute | solution.py:338
  10.0 8.5 %copy-start = (bf16[32,32,192]{2,1,0:T(8,128)(2,1)S(1)}, bf16[32,32,192]{2,1,0:T(8,128)(2,1)}, u32[]{:S(2)}) copy-start(bf16[32,32,192]{2,1,0:T(8,128)(2,1)} %p_hbm.1) | copy-start | bytes 1179652
  35.4 7.5 %collective-permute-start.7 = (bf16[80,1024]{1,0:T(8,128)(2,1)S(1)}, bf16[80,1024]{1,0:T(8,128)(2,1)S(1)}, u32[]{:S(2)}, u32[]{:S(2)}) collective-permute-start(bf16[80,1024]{1,0:T(8,128)(2,1)S(1)} %combine.1.args_0_), channel_id=1, source_target_pairs={{0,96},{16,112},{32,0},{48,16},{64,32},{80,48},{96,64},{112,80},{1... | collective-permute-start | bytes 491528 | tf_op jit(solution)/shard_map/ppermute | solution.py:389
  37.7 8.6 %collective-permute-start.6 = (bf16[80,1024]{1,0:T(8,128)(2,1)S(1)}, bf16[80,1024]{1,0:T(8,128)(2,1)S(1)}, u32[]{:S(2)}, u32[]{:S(2)}) collective-permute-start(bf16[80,1024]{1,0:T(8,128)(2,1)S(1)} %combine.1.args_0_), channel_id=1, source_target_pairs={{0,64},{16,80},{32,96},{48,112},{64,0},{80,16},{96,32},{112,48},{1... | collective-permute-start | bytes 491528 | tf_op jit(solution)/shard_map/ppermute | solution.py:389
  38.9 9.7 %collective-permute-start.5 = (bf16[80,1024]{1,0:T(8,128)(2,1)S(1)}, bf16[80,1024]{1,0:T(8,128)(2,1)S(1)}, u32[]{:S(2)}, u32[]{:S(2)}) collective-permute-start(bf16[80,1024]{1,0:T(8,128)(2,1)S(1)} %combine.1.args_0_), channel_id=1, source_target_pairs={{0,32},{16,48},{32,64},{48,80},{64,96},{80,112},{96,0},{112,16},{1... | collective-permute-start | bytes 491528 | tf_op jit(solution)/shard_map/ppermute | solution.py:389
  39.7 10.3 %collective-permute-start.4 = (bf16[80,1024]{1,0:T(8,128)(2,1)S(1)}, bf16[80,1024]{1,0:T(8,128)(2,1)S(1)}, u32[]{:S(2)}, u32[]{:S(2)}) collective-permute-start(bf16[80,1024]{1,0:T(8,128)(2,1)S(1)} %combine.1.args_0_), channel_id=1, source_target_pairs={{0,16},{16,0},{32,48},{48,32},{64,80},{80,64},{96,112},{112,96},{1... | collective-permute-start | bytes 491528 | tf_op jit(solution)/shard_map/ppermute | solution.py:390
  42.9 7.0 %collective-permute-start.10 = (bf16[80,1024]{1,0:T(8,128)(2,1)S(1)}, bf16[80,1024]{1,0:T(8,128)(2,1)S(1)}, u32[]{:S(2)}, u32[]{:S(2)}) collective-permute-start(bf16[80,1024]{1,0:T(8,128)(2,1)S(1)} %collective-permute-done.7.args_4_), channel_id=1, source_target_pairs={{0,16},{16,0},{32,48},{48,32},{64,80},{80,64},{96,112},{112,96},{1... | collective-permute-start | bytes 491528 | tf_op jit(solution)/shard_map/ppermute | solution.py:391
  46.3 3.7 %collective-permute-start.9 = (bf16[80,1024]{1,0:T(8,128)(2,1)S(1)}, bf16[80,1024]{1,0:T(8,128)(2,1)S(1)}, u32[]{:S(2)}, u32[]{:S(2)}) collective-permute-start(bf16[80,1024]{1,0:T(8,128)(2,1)S(1)} %collective-permute-done.6.args_3_), channel_id=1, source_target_pairs={{0,16},{16,0},{32,48},{48,32},{64,80},{80,64},{96,112},{112,96},{1... | collective-permute-start | bytes 491528 | tf_op jit(solution)/shard_map/ppermute | solution.py:391
  48.6 2.4 %collective-permute-start.8 = (bf16[80,1024]{1,0:T(8,128)(2,1)S(1)}, bf16[80,1024]{1,0:T(8,128)(2,1)S(1)}, u32[]{:S(2)}, u32[]{:S(2)}) collective-permute-start(bf16[80,1024]{1,0:T(8,128)(2,1)S(1)} %collective-permute-done.5.args_2_), channel_id=1, source_target_pairs={{0,16},{16,0},{32,48},{48,32},{64,80},{80,64},{96,112},{112,96},{1... | collective-permute-start | bytes 491528 | tf_op jit(solution)/shard_map/ppermute | solution.py:391
